TPU v7x, 32 devices: a whole 2x2x4 slice. The times are simulated.
32 devices in a mesh: rep: 4 (over y, core), fsdp: 8 (over z, x).
Axes of the slice: x: 2, y: 2, z: 4, core: 2. Of those that a mesh axis runs over, the one named last changes fastest.
Arguments:
- activations: bfloat16 [4, 3072, 4096], P('rep', 'fsdp'), may hold values from -6 to 6
- key_cotangent: bfloat16 [4, 3072, 512], P('rep', 'fsdp'), may hold values from -12 to 12
- doc_ids: int32 [4, 3072], P('rep', 'fsdp'), may hold values from 0 to 7, as said below
- replica_params: float32 [4, 4096, 512], P('rep', 'fsdp'), may hold values from -14 to 14
- first_moment: float32 [4, 4096, 512], P('rep', 'fsdp'), may hold values from -6 to 6
- second_moment: float32 [4, 4096, 512], P('rep', 'fsdp'), may hold values from 1 to 16
- anchor: float32 [4096, 512], P(('fsdp', 'rep')), may hold values from -8 to 8
- momentum: float32 [4096, 512], P(('fsdp', 'rep')), may hold values from -3 to 3
Outputs:
- new_first: float32 [4, 4096, 512], P('rep', 'fsdp')
- new_second: float32 [4, 4096, 512], P('rep', 'fsdp')
- new_momentum: float32 [4096, 512], P(('fsdp', 'rep'))
- new_params: float32 [4096, 512], P('fsdp')
Inputs may be any that keep to these rules, and one draw needn't show every extreme that they name: `doc_ids`: within each group the numbers never fall along the tokens; every block of 384 consecutive tokens (from token 0) holds the first token of exactly one document; every document holds 1 to 767 tokens and one holds exactly 767.
All inputs are finite; a program needn't handle non-finite values.
Results may differ from a plain program's by a relative error of at most 0.0035.
Values may be sent and summed in bfloat16 or wider, within the bound.
No kernel may reach another device: no remote copies, remote signals or barrier semaphores. Data moves between devices by JAX's collectives and lax.ppermute only.
A program may use at most 64 MiB of HBM per device.

v0:
```python
import math

import jax
import jax.numpy as jnp
from jax import lax
from jax.sharding import PartitionSpec as P

KV_HEADS = 4
HEAD = 128


rope_base = 500000.0


def entering(array, axis, combine, identity):
    peers, index = (lax.axis_size(axis), lax.axis_index(axis))
    everything = jax.tree.map(lambda part: lax.all_gather(part, axis), array)
    start = jax.tree.map(
        lambda part, zero: jnp.broadcast_to(jnp.asarray(zero, part.dtype), part.shape),
        array,
        identity,
    )

    def hop(k, before):
        reached = k < index
        new = combine(before, jax.tree.map(lambda part: part[k], everything))
        return jax.tree.map(lambda a, b: jnp.where(reached, a, b), new, before)

    return lax.fori_loop(0, peers, hop, start)


def rotate_back(cotangent, offsets):
    row_count = cotangent.shape[0]
    half_head = HEAD // 2
    blocks = cotangent.astype(jnp.float32).reshape(row_count, KV_HEADS, 2, half_head)
    frequency = jnp.exp(
        jnp.arange(half_head, dtype=jnp.float32) * (-math.log(rope_base) / half_head)
    )
    angles = offsets[:, None] * frequency[None, :]
    cosine = jnp.cos(angles)[:, None, :]
    sine_part = jnp.sin(angles)[:, None, :]
    lower_half = blocks[:, :, 0, :]
    upper_half = blocks[:, :, 1, :]
    fresh_lower = lower_half * cosine + upper_half * sine_part
    fresh_upper = upper_half * cosine - lower_half * sine_part
    return (
        jnp.stack([fresh_lower, fresh_upper], axis=2)
        .reshape(row_count, KV_HEADS * HEAD)
        .astype(jnp.bfloat16)
    )


def inner_step(grad, params, first, second):
    fresh_first = 0.9 * first + 0.1 * grad
    fresh_second = 0.95 * second + 0.05 * grad * grad
    stepped = params - 0.2 * (fresh_first / (jnp.sqrt(fresh_second) + 1e-08) + 0.1 * params)
    return (fresh_first, fresh_second, stepped)


def join_runs(before, behind):
    joined_doc = jnp.where(behind[0] < 0, before[0], behind[0])
    joined_start = jnp.where(
        behind[0] < 0, before[1], jnp.where(behind[0] == before[0], before[1], behind[1])
    )
    return (joined_doc, joined_start)


def local(
    activations,
    key_cotangent,
    doc_ids,
    replica_params,
    first_moment,
    second_moment,
    anchor,
    momentum,
):
    features = activations[0]
    cotangent = key_cotangent[0]
    doc_block = doc_ids[0]
    tok_rows = features.shape[0]
    groups = lax.axis_size("fsdp")
    replicas = lax.axis_size("rep")
    device = lax.axis_index("fsdp")
    root = device * tok_rows
    places = jnp.arange(tok_rows, dtype=jnp.int32)
    last_doc = doc_block[tok_rows - 1]
    last_start = jnp.min(jnp.where(doc_block == last_doc, places, jnp.int32(tok_rows))) + root
    prior_doc, prior_start = entering(
        (last_doc, last_start), "fsdp", join_runs, (jnp.int32(-1), jnp.int32(0))
    )
    begins = jnp.concatenate([jnp.ones((1,), jnp.bool_), doc_block[1:] != doc_block[:-1]])
    local_start = lax.cummax(jnp.where(begins, places, jnp.int32(0)), axis=0) + root
    run_start = jnp.where(doc_block == prior_doc, prior_start, local_start)
    offsets = (root + places - run_start).astype(jnp.float32)
    rotated = rotate_back(cotangent, offsets)
    grad_scale = 1.0 / math.sqrt(tok_rows * groups)
    product = lax.dot_general(
        features, rotated, (((0,), (0,)), ((), ())), preferred_element_type=jnp.float32
    )
    grad = lax.psum_scatter(
        (product * grad_scale).astype(jnp.bfloat16), "fsdp", scatter_dimension=0, tiled=True
    ).astype(jnp.float32)
    fresh_first, fresh_second, stepped = inner_step(
        grad, replica_params[0], first_moment[0], second_moment[0]
    )
    share_rows = anchor.shape[0]
    summed = lax.psum(stepped, "rep")
    anchor_rows, momentum_rows = (
        lax.all_gather(anchor, "rep", axis=0, tiled=True),
        lax.all_gather(momentum, "rep", axis=0, tiled=True),
    )
    pseudo_grad = anchor_rows - summed / replicas
    momentum_full = 0.9 * momentum_rows + pseudo_grad
    new_params = anchor_rows - 0.7 * (pseudo_grad + 0.9 * momentum_full)
    new_momentum = lax.dynamic_slice_in_dim(
        momentum_full, lax.axis_index("rep") * share_rows, share_rows, 0
    )
    return (fresh_first[None], fresh_second[None], new_momentum, new_params)


def solution(mesh):
    placed = (
        P("rep", "fsdp", None),
        P("rep", "fsdp", None),
        P("rep", "fsdp"),
        P("rep", "fsdp", None),
        P("rep", "fsdp", None),
        P("rep", "fsdp", None),
        P(("fsdp", "rep"), None),
        P(("fsdp", "rep"), None),
    )
    return jax.shard_map(
        local,
        mesh=mesh,
        in_specs=placed,
        out_specs=(
            P("rep", "fsdp", None),
            P("rep", "fsdp", None),
            P(("fsdp", "rep"), None),
            P("fsdp", None),
        ),
        check_vma=False,
    )
```

profile of v0, /device:TPU:0, one launch (start us, length us, event | category | flops | bytes accessed | tf_op | source)
XLA Modules:
  0.0 208.1 jit_solution(2617310549342385104)
XLA Ops:
  8.1 1.4 slice.28
  9.5 0.8 compare_reduce_fusion
  10.3 1.2 copy.22
  11.5 0.9 convert.9
  12.5 1.3 compare_reduce_fusion.2
  13.7 0.7 select_reduce_fusion
  14.4 1.2 dynamic-slice
  15.6 1.2 bitcast_dynamic-update-slice_fusion
  17.5 0.8 dynamic-update-slice.1
  18.3 13.1 %all-reduce.2 = (s32[8]{0:T(128)S(1)}, s32[8]{0:T(128)S(1)}) all-reduce(s32[8]{0:T(128)S(1)} %bitcast_dynamic-update-slice_fusion, s32[8]{0:T(128)S(1)} %dynamic-update-slice.1), channel_id=2, replica_groups=mesh['rep'=4,'fsdp'=8] {'fsdp'}, use_global_device_ids=true, to_apply=%add | all-reduce | flops 16 | bytes 128 | tf_op jit(solution)/shard_map/all_gather | solution.py:17
  31.3 27.6 %while.15 = (s32[]{:T(128)}, s32[]{:T(128)}, s32[]{:T(128)}, s32[]{:T(128)}, s32[8]{0:T(128)S(1)}, /*index=5*/s32[8]{0:T(128)S(1)}, s32[]{:T(128)}, s32[]{:T(128)}) while((s32[]{:T(128)}, s32[]{:T(128)}, s32[]{:T(128)}, s32[]{:T(128)}, s32[8]{0:T(128)S(1)}, /*index=5*/s32[8]{0:T(128)S(1)}, s32[]{:T(128)}, s32[]{:T(128)}) %tuple.39), condition=%wide.region_2.3_spmd, body=%wide.region_1.2_spmd.sunk | while | flops 10 | bytes 217 | solution.py:29
  31.3 0.6 dynamic_slice.21
  33.6 0.6 dynamic_slice.22
  34.8 0.6 dynamic_slice.21
  37.0 0.6 dynamic_slice.22
  38.2 0.6 dynamic_slice.21
  40.5 0.6 dynamic_slice.22
  41.7 0.6 dynamic_slice.21
  43.9 0.6 dynamic_slice.22
  45.1 0.6 dynamic_slice.21
  47.4 0.6 dynamic_slice.22
  48.6 0.6 dynamic_slice.21
  50.8 0.6 dynamic_slice.22
  52.0 0.6 dynamic_slice.21
  54.3 0.6 dynamic_slice.22
  55.5 0.6 dynamic_slice.21
  57.7 0.6 dynamic_slice.22
  58.9 0.7 compare_reduce_fusion.1
  59.7 0.3 reduce-window.9
  60.1 0.1 slice_reduce_fusion
  60.2 0.1 fusion.9
  60.3 0.4 multiply_cosine_fusion
  60.7 1.2 add_convert_fusion
  62.0 4.3 %fusion = bf16[4096,512]{0,1:T(8,128)(2,1)} fusion(bf16[384,512]{0,1:T(8,128)(2,1)S(1)} %bitcast.56, bf16[1,384,4096]{2,1,0:T(8,128)(2,1)S(1)} %copy-done), kind=kOutput, calls=%fused_computation.1 | convolution fusion | flops 1614807040 | bytes 7733248 | tf_op jit(solution)/shard_map/dot_general | solution.py:98
  66.4 0.9 copy-done.1
  67.3 0.8 copy.25
  68.2 1.8 copy.24
  70.1 2.5 %copy.26 = f32[1,512,512]{1,2,0:T(8,128)} copy(f32[1,512,512]{2,1,0:T(8,128)} %param.13) | data formatting | bytes 2097152 | tf_op args[3]
  72.6 2.6 %copy.21 = f32[1,512,512]{1,2,0:T(8,128)} copy(f32[1,512,512]{2,1,0:T(8,128)} %param.14) | data formatting | bytes 2097152 | tf_op args[4]
  75.2 2.5 %copy.23 = f32[1,512,512]{1,2,0:T(8,128)} copy(f32[1,512,512]{2,1,0:T(8,128)} %param.15) | data formatting | bytes 2097152 | tf_op args[5]
  77.7 75.5 %reduce-scatter.2.cloned.1.call-done = bf16[512,512]{0,1:T(8,128)(2,1)} async-done(((bf16[4096,512]{0,1:T(8,128)(2,1)}), bf16[512,512]{0,1:T(8,128)(2,1)}) %reduce-scatter.2.cloned.1.call-update) | async-done | bytes 524304 | tf_op jit(solution)/shard_map/reduce_scatter | solution.py:101
  153.2 4.1 %bitcast_subtract_fusion = (f32[512,512]{0,1:T(8,128)}, f32[1,512,512]{1,2,0:T(8,128)}, f32[1,512,512]{1,2,0:T(8,128)}) fusion(f32[1,512,512]{1,2,0:T(8,128)} %copy.26, bf16[512,512]{0,1:T(8,128)(2,1)} %reduce-scatter.2.cloned.1.call-done, f32[1,512,512]{1,2,0:T(8,128)} %copy.21, f32[1,512,512]{1,2,0:T(8,128)} %copy.23), kind=kLoop, calls=%fused_computation.7 | loop fusion | flops 3670016 | bytes 6815744 | tf_op jit(solution)/shard_map/sub | solution.py:56
  157.4 2.5 %copy.27 = f32[1,512,512]{2,1,0:T(8,128)} copy(f32[1,512,512]{1,2,0:T(8,128)} %get-tuple-element.142) | data formatting | bytes 2097152
  159.9 2.5 %copy.28 = f32[1,512,512]{2,1,0:T(8,128)} copy(f32[1,512,512]{1,2,0:T(8,128)} %get-tuple-element.141) | data formatting | bytes 2097152
  162.4 31.4 %all-reduce.5.cloned.1.call-done = f32[512,512]{0,1:T(8,128)} async-done(((f32[512,512]{0,1:T(8,128)}), f32[512,512]{0,1:T(8,128)}) %all-reduce.5.cloned.1.call-update) | async-done | bytes 1048592 | tf_op jit(solution)/shard_map/psum | solution.py:108
  193.8 3.3 %multiply_subtract_fusion = (f32[512,512]{0,1:T(8,128)}, f32[512,512]{0,1:T(8,128)S(1)}) fusion(f32[512,512]{0,1:T(8,128)} %all-gather.6.cloned.1.call-done, f32[512,512]{0,1:T(8,128)} %all-reduce.5.cloned.1.call-done, f32[512,512]{0,1:T(8,128)} %all-gather.4.cloned.1.call-done), kind=kLoop, calls=%fused_computation.11 | loop fusion | flops 2097152 | bytes 5242880 | tf_op jit(solution)/shard_map/sub | solution.py:115
  197.2 0.8 copy.29
  198.0 2.5 %copy.30 = f32[512,512]{1,0:T(8,128)} copy(f32[512,512]{0,1:T(8,128)} %get-tuple-element.138) | data formatting | bytes 2097152
  (21 shorter events, 0.5 us)
Async XLA Ops:
  8.0 54.0 %copy-start = (bf16[1,384,4096]{2,1,0:T(8,128)(2,1)S(1)}, bf16[1,384,4096]{2,1,0:T(8,128)(2,1)}, u32[]{:S(2)}) copy-start(bf16[1,384,4096]{2,1,0:T(8,128)(2,1)} %param.10) | copy-start | bytes 9437188
  8.0 145.2 %reduce-scatter.2.cloned.1.call-start = ((), (), s32[]{:S(2)}) async-start(), calls=%async_computation.1 | async-start | bytes 4718592 | tf_op jit(solution)/shard_map/reduce_scatter | solution.py:101
  66.3 0.9 copy-start.1
  66.3 96.1 %all-gather.6.cloned.1.call-start = ((), (), s32[]{:S(2)}) async-start(), calls=%async_computation.3 | async-start | bytes 1310720 | tf_op jit(solution)/shard_map/all_gather | solution.py:110
  68.1 94.3 %all-gather.4.cloned.1.call-start = ((), (), s32[]{:S(2)}) async-start(), calls=%async_computation.2 | async-start | bytes 1310720 | tf_op jit(solution)/shard_map/all_gather | solution.py:111
  70.0 123.8 %all-reduce.5.cloned.1.call-start = ((), (), s32[]{:S(2)}) async-start(), calls=%async_computation.4 | async-start | bytes 2097152 | tf_op jit(solution)/shard_map/psum | solution.py:108
Sparse Core Ops, SparseCore 0:
  66.5 86.6 reduce-scatter.1
Sparse Core Ops, SparseCore 1:
  69.0 14.9 all-gather.5
  85.5 16.7 all-gather.3
  157.4 36.4 all-reduce.4
where the time goes:
time: 209 us; the launch traced here: 208 us
  waiting for transfers between devices  107 us (51%)
  local copies, waits for them, and re-layouts  34.9 us (17%)
  loops' own time  18.3 us (9%)
  between operations  16.4 us (8%)
  other arithmetic  14 us (7%)
  blocking collectives  13.1 us (6%)
  matrix products  4.28 us (2%)
    reduce_scatter x1, waiting for transfers between devices, local(): lax.psum_scatter((product * grad_scale).astype(jnp.bfloat16), 'fsdp', sca...  75.5 us
    psum x1, waiting for transfers between devices, local(): summed = lax.psum(stepped, 'rep')  31.4 us
    unnamed x19, local copies, waits for them, and re-layouts  24 us
    another operation x1, loops' own time, entering(): return lax.fori_loop(0, peers, hop, start)  18.3 us
    all_gather x1, blocking collectives, entering(): everything = jax.tree.map(lambda part: lax.all_gather(part, axis), array)  13.1 us
    dynamic_slice x16, local copies, waits for them, and re-layouts, hop(): new = combine(before, jax.tree.map(lambda part: part[k], everything))  9.29 us
    dot_general x1, matrix products, local(): lax.dot_general(features, rotated, (((0,), (0,)), ((), ())), preferred_el...  4.28 us
  transfers between devices with their start and end apart: 4, of which 2 were waited for; matrix products, arithmetic and copies ran while one was open for 9% of the time, Pallas kernels for 0%

commit v1 on v0

v1 whole, which is shorter than its diff:
```python
import functools
import math

import jax
import jax.numpy as jnp
import numpy as np
from jax import lax
from jax.experimental import pallas as pl
from jax.experimental.pallas import tpu as pltpu
from jax.sharding import PartitionSpec as P

HEAD = 128
ROPE_BASE = 500000.0
HALVES = 2
F32, BF16 = jnp.float32, jnp.bfloat16
VMEM_LIMIT = 48 * 1024 * 1024


def schedule(line):
    order = np.zeros((line, line), np.int32)
    for z in range(line):
        when = {}
        for d in range(line):
            when[d] = line - d + z if d > z else (d + line - z if d < z else 10 * line)
        order[z] = sorted(range(line), key=lambda d: (when[d], abs(d - z) * -1))
    place = np.argsort(order, axis=1)
    sends = []
    for t in range(1, line):
        even, odd = [], []
        for z in range(line):
            right = line - t + z
            right = right if right < line else -1
            left = t - line + z
            left = left if left >= 0 else -1
            even.append(right if z % 2 == 0 else left)
            odd.append(left if z % 2 == 0 else right)
        sends.append((even, odd))
    return order, place, sends


def dot(a, b):
    return lax.dot_general(a, b, (((1,), (0,)), ((), ())), preferred_element_type=F32)


def rotate_kernel(row, doc_ref, prev_ref, cot_ref, *outs):
    tokens = doc_ref.shape[1]

    def start(doc):
        last = jnp.max(doc, axis=1, keepdims=True)
        return tokens - jnp.sum((doc == last).astype(jnp.int32), axis=1, keepdims=True)

    places = lax.broadcasted_iota(jnp.int32, (1, tokens), 1)
    own = start(doc_ref[...])
    before = start(prev_ref[...])
    offsets = jnp.where(places >= own, places - own, places + tokens - before).astype(F32)
    half = HEAD // 2
    steps = lax.broadcasted_iota(jnp.int32, (half, 1), 0).astype(F32)
    frequency = jnp.exp(steps * (-math.log(ROPE_BASE) / half))
    angles = frequency * offsets
    cosine, sine = jnp.cos(angles), jnp.sin(angles)
    width = outs[0].shape[0]
    for part, out in enumerate(outs):
        turned = cot_ref[:, part * width : (part + 1) * width].astype(F32).T
        for head in range(width // HEAD):
            low = turned[head * HEAD : head * HEAD + half]
            high = turned[head * HEAD + half : (head + 1) * HEAD]
            out[head * HEAD : head * HEAD + half, :] = (low * cosine + high * sine).astype(BF16)
            out[head * HEAD + half : (head + 1) * HEAD, :] = (high * cosine - low * sine).astype(BF16)


def send_kernel(cols, chunks, row, *refs):
    own, peer = refs[0], refs[1]
    at = 2
    streams = []
    for stream in cols:
        streams.append((stream, refs[at]))
        at += 1
    pieces = {}
    for k in chunks:
        pieces[k] = refs[at]
        at += 1
    befores = []
    for (slot, options, has_before), _ in streams:
        befores.append(refs[at] if has_before else None)
        at += int(has_before)
    outs = refs[at:]
    for ((slot, options, _), mine), before, out in zip(streams, befores, outs):
        valid, place = row[slot + 1], row[slot + 2]

        @pl.when(valid == 0)
        def _():
            out[...] = jnp.zeros_like(out)

        for k in options:

            @pl.when((valid == 1) & (place == k))
            def _():
                total = dot(own[...], mine[...]) + dot(peer[...], pieces[k][...])
                if before is not None:
                    total = total + before[...].astype(F32)
                out[...] = total.astype(BF16)


def final_kernel(scale, core_slot, row, *refs):
    own, peer, mine, theirs, even, odd, first, second = refs[:8]
    new_first, new_second, keep, give = refs[-4:]
    total = dot(own[...], mine[...]) + dot(peer[...], theirs[...])
    total = total + even[...].astype(F32) + odd[...].astype(F32)
    grad = total.T * scale
    fresh_first = 0.9 * first[...] + 0.1 * grad
    fresh_second = 0.95 * second[...] + 0.05 * grad * grad
    new_first[...] = fresh_first
    new_second[...] = fresh_second
    update = fresh_first / (jnp.sqrt(fresh_second) + 1e-08)
    count, share, width = keep.shape
    pairs = update.reshape(count, 2, share, width)
    zero = row[core_slot] == 0
    keep[...] = jnp.where(zero, pairs[:, 0], pairs[:, 1]).astype(keep.dtype)
    give[...] = jnp.where(zero, pairs[:, 1], pairs[:, 0]).astype(give.dtype)


def assemble_kernel(core_slot, row, mine, theirs, *refs):
    out = refs[-1]
    zero = row[core_slot] == 0
    a, b = mine[...], theirs[...]
    both = jnp.stack([jnp.where(zero, a, b), jnp.where(zero, b, a)], axis=1)
    out[...] = both.reshape(out.shape)


def call(kernel, row, grid, ins, outs, aliases=None):
    specs = []
    for array, block, index in ins:
        if index == "any":
            specs.append(pl.BlockSpec(memory_space=pl.ANY))
        elif block is None:
            rank = array.ndim
            specs.append(pl.BlockSpec(array.shape, functools.partial(lambda rank, i, s: (0,) * rank, rank)))
        else:
            specs.append(pl.BlockSpec(block, index))
    out_specs, shapes = [], []
    for shape, dtype, block, index in outs:
        rank = len(shape)
        shapes.append(jax.ShapeDtypeStruct(shape, dtype))
        if block is None:
            out_specs.append(pl.BlockSpec(shape, functools.partial(lambda rank, i, s: (0,) * rank, rank)))
        else:
            out_specs.append(pl.BlockSpec(block, index))
    return pl.pallas_call(
        kernel,
        grid_spec=pltpu.PrefetchScalarGridSpec(
            num_scalar_prefetch=1, grid=(grid,), in_specs=specs, out_specs=out_specs
        ),
        out_shape=shapes,
        input_output_aliases={k + 1: v for k, v in (aliases or {}).items()},
        compiler_params=pltpu.CompilerParams(vmem_limit_bytes=VMEM_LIMIT),
    )(row, *[array for array, _, _ in ins])


def local(fsdp, reps, activations, key_cotangent, doc_ids, replica_params, first_moment, second_moment, anchor, momentum):
    features, cotangent = activations[0], key_cotangent[0]
    params, first, second = replica_params[0], first_moment[0], second_moment[0]
    tokens, model = features.shape
    keys = cotangent.shape[1]
    rows = model // fsdp
    line = fsdp // 2
    share = anchor.shape[0]
    outer = reps // 2
    width = keys // HALVES
    order, place, sends = schedule(line)

    table, slots = [], {}
    for device in range(reps * fsdp):
        group, spot = divmod(device, fsdp)
        z, x = divmod(spot, 2)
        numbers = {"core": group % 2, "outer": group // 2}
        for k in range(line):
            numbers["pack", k] = 2 * order[z][k] + 1 - x
        numbers["own"] = 2 * z + x
        for t, streams in enumerate(sends, 1):
            for name, chunk in zip("eo", streams):
                d = chunk[z]
                numbers[name, t] = 2 * max(d, 0) + x
                numbers[name, t, "valid"] = int(d >= 0)
                numbers[name, t, "place"] = place[z][max(d, 0)]
        slots = {key: i for i, key in enumerate(numbers)}
        table.append([int(v) for v in numbers.values()])
    here = lax.axis_index("rep") * fsdp + lax.axis_index("fsdp")
    row = lax.dynamic_slice_in_dim(jnp.asarray(np.array(table, np.int32)), here, 1, 0)[0]
    core, out_spot = row[slots["core"]], row[slots["outer"]]

    pair = [(f, f ^ 1) for f in range(fsdp)]
    cores = [(r, r ^ 1) for r in range(reps)]
    across = [(r, r ^ 2) for r in range(reps)]
    evens, odds = [], []
    for z in range(line - 1):
        for x in range(2):
            a, b = 2 * z + x, 2 * z + 2 + x
            (evens if z % 2 == 0 else odds).extend([(a, b), (b, a)])

    prev = lax.ppermute(doc_ids, "fsdp", [(f, (f + 1) % fsdp) for f in range(fsdp)])

    def packed(k):
        return lax.dynamic_slice_in_dim(features, row[slots["pack", k]] * rows, rows, 1)

    pieces = [lax.ppermute(packed(0), "fsdp", pair)]
    own = call(
        rotate_kernel, row, 1, [(doc_ids, None, None), (prev, None, None), (cotangent, None, None)],
        [((width, tokens), BF16, None, None)] * HALVES,
    )
    peer = [lax.ppermute(part, "fsdp", pair) for part in own]
    for k in range(1, line):
        pieces.append(lax.ppermute(packed(k), "fsdp", pair))

    decay = 1.0 - 0.2 * 0.1
    groups = [[2 * q + c for q in range(outer)] for c in range(2)]
    split = params.reshape(outer, 2, share, keys)
    give = lax.dynamic_index_in_dim(split, 1 - core, 1, keepdims=False)
    stay = lax.dynamic_index_in_dim(split, core, 1, keepdims=False)
    held = stay + lax.ppermute(give, "rep", cores)
    if outer == 2:
        mine = lax.dynamic_index_in_dim(held, out_spot, 0, keepdims=False)
        other = lax.dynamic_index_in_dim(held, 1 - out_spot, 0, keepdims=False)
        summed = mine + lax.ppermute(other, "rep", across)
    else:
        summed = lax.psum_scatter(held, "rep", scatter_dimension=0, axis_index_groups=groups, tiled=False)
    base = anchor - (decay / reps) * summed
    momentum_base = 0.9 * momentum + base
    params_base = anchor - 0.7 * (base + 0.9 * momentum_base)
    if outer == 2:
        far = lax.ppermute(params_base, "rep", across)
        near = out_spot == 0
        bases = jnp.stack([jnp.where(near, params_base, far), jnp.where(near, far, params_base)])
    else:
        bases = lax.all_gather(params_base, "rep", axis_index_groups=groups)

    came = [(None, None)] * HALVES
    for t, streams in enumerate(sends, 1):
        for h in range(HALVES):
            cols, chunks, ins, outs = [], set(), [], []
            before = []
            for name, chunk, arrived in zip("eo", streams, came[h][::-1]):
                options = sorted({int(place[z][d]) for z, d in enumerate(chunk) if d >= 0 and 0 <= (z + (1 if (name == "e") == (z % 2 == 0) else -1)) < line})
                if not options:
                    continue
                chunks.update(options)
                cols.append((slots[name, t], options, arrived is not None))
                if arrived is not None:
                    before.append((arrived, None, None))
            ins = [(own[h], None, None), (peer[h], None, None)]
            for slot, _, _ in cols:
                ins.append((features, (tokens, rows), functools.partial(lambda slot, i, s: (0, s[slot]), slot)))
            ins += [(pieces[k], None, None) for k in sorted(chunks)] + before
            outs = [((width, rows), BF16, None, None)] * len(cols)
            sent = call(functools.partial(send_kernel, cols, sorted(chunks)), row, 1, ins, outs)
            even = lax.ppermute(sent[0], "fsdp", evens)
            odd = lax.ppermute(sent[1], "fsdp", odds) if len(sent) > 1 else None
            came[h] = (even, odd)

    scale = 1.0 / math.sqrt(tokens * fsdp)
    tall = max(2 * share, 128)
    steps = rows // tall
    new_first = new_second = new_params = None
    momenta = []
    for h in range(HALVES):
        even, odd = came[h]
        side = functools.partial(lambda h, i, s: (i, h), h)
        ins = [
            (own[h], None, None),
            (peer[h], None, None),
            (features, (tokens, tall), lambda i, s: (0, s[slots["own"]] * steps + i)),
            (pieces[line - 1], (tokens, tall), lambda i, s: (0, i)),
            (even, (width, tall), lambda i, s: (0, i)),
            (odd, (width, tall), lambda i, s: (0, i)),
            (first, (tall, width), side),
            (second, (tall, width), side),
        ]
        aliases = None
        if new_first is not None:
            ins += [(new_first, None, "any"), (new_second, None, "any")]
            aliases = {8: 0, 9: 1}
        each = tall // (2 * share)
        new_first, new_second, keep, give = call(
            functools.partial(final_kernel, scale, slots["core"]), row, steps, ins,
            [
                ((rows, keys), F32, (tall, width), side),
                ((rows, keys), F32, (tall, width), side),
                ((outer, share, width), F32, (each, share, width), lambda i, s: (i, 0, 0)),
                ((outer, share, width), BF16, (each, share, width), lambda i, s: (i, 0, 0)),
            ],
            aliases,
        )
        both = keep + lax.ppermute(give, "rep", cores).astype(F32)
        if outer == 2:
            both = both.astype(BF16)
            total = both.astype(F32) + lax.ppermute(both, "rep", across).astype(F32)
        else:
            total = lax.psum(both, "rep", axis_index_groups=groups)
        part = slice(h * width, (h + 1) * width)
        mean = (0.2 / reps) * total
        momenta.append(momentum_base[:, part] + lax.dynamic_index_in_dim(mean, out_spot, 0, keepdims=False))
        fresh = bases[:, :, part] - (0.7 * 1.9) * mean
        theirs = lax.ppermute(fresh, "rep", cores)
        ins = [(fresh, None, None), (theirs, None, None)]
        aliases = None
        if new_params is not None:
            ins.append((new_params, None, "any"))
            aliases = {2: 0}
        (new_params,) = call(
            functools.partial(assemble_kernel, slots["core"]), row, 1, ins,
            [((rows, keys), F32, (rows, width), functools.partial(lambda h, i, s: (0, h), h))],
            aliases,
        )
    new_momentum = jnp.concatenate(momenta, axis=1)
    return (new_first[None], new_second[None], new_momentum, new_params)


def solution(mesh):
    fsdp, reps = mesh.shape["fsdp"], mesh.shape["rep"]
    placed = (
        P("rep", "fsdp", None),
        P("rep", "fsdp", None),
        P("rep", "fsdp"),
        P("rep", "fsdp", None),
        P("rep", "fsdp", None),
        P("rep", "fsdp", None),
        P(("fsdp", "rep"), None),
        P(("fsdp", "rep"), None),
    )
    return jax.shard_map(
        functools.partial(local, fsdp, reps),
        mesh=mesh,
        in_specs=placed,
        out_specs=(
            P("rep", "fsdp", None),
            P("rep", "fsdp", None),
            P(("fsdp", "rep"), None),
            P("fsdp", None),
        ),
        check_vma=False,
    )
```

time: 209 us -> 115 us (0.55)
  waiting for transfers between devices: 107 us -> 24.9 us
  starting transfers between devices: 0.17 us -> 35.9 us
  Pallas kernels: 0 us -> 26.4 us
  local copies, waits for them, and re-layouts: 34.9 us -> 14.4 us
  loops' own time: 18.3 us -> 0 us
  blocking collectives: 13.1 us -> 0 us
  other arithmetic: 14 us -> 2.37 us
  between operations: 16.4 us -> 10.5 us
  matrix products: 4.28 us -> 0 us
    reduce_scatter x1 -> x0, waiting for transfers between devices: 75.5 us -> none  [local(): lax.psum_scatter((product * grad_scale).astype(jnp.bfloat16), 'fsdp', sca...]
    ppermute x0 -> x26, starting transfers between devices: none -> 35.9 us  [the longest x6 13.4 us: local(): even = lax.ppermute(sent[0], 'fsdp', evens)]
    psum x1 -> x0, waiting for transfers between devices: 31.4 us -> none  [local(): summed = lax.psum(stepped, 'rep')]
    pallas_call x0 -> x11, Pallas kernels: none -> 26.4 us  [call(): pl.pallas_call(kernel, grid_spec=pltpu.PrefetchScalarGridSpec(num_scalar_...]
    ppermute x0 -> x26, waiting for transfers between devices: none -> 24.9 us  [the longest x1 7.54 us: local(): lax.ppermute(doc_ids, 'fsdp', [(f, (f + 1) % fsdp) for f in range(fsdp)])]
    another operation x1 -> x0, loops' own time: 18.3 us -> none  [entering(): return lax.fori_loop(0, peers, hop, start)]
    unnamed x19 -> x50, local copies, waits for them, and re-layouts: 24 us -> 9.2 us
    all_gather x1 -> x0, blocking collectives: 13.1 us -> none  [entering(): everything = jax.tree.map(lambda part: lax.all_gather(part, axis), array)]
  transfers between devices with their start and end apart: 4 -> 26, of which waited for: 2 -> 8; matrix products, arithmetic and copies ran while one was open for 9% -> 3% of each run, Pallas kernels for 0% -> 22%
where the time goes in v1:
time: 115 us
  starting transfers between devices  35.9 us (31%)
  Pallas kernels  26.4 us (23%)
  waiting for transfers between devices  24.9 us (22%)
  local copies, waits for them, and re-layouts  14.4 us (13%)
  between operations  10.5 us (9%)
  other arithmetic  2.37 us (2%)
    pallas_call x11, Pallas kernels, call(): pl.pallas_call(kernel, grid_spec=pltpu.PrefetchScalarGridSpec(num_scalar_...  26.4 us
    ppermute x6, starting transfers between devices, local(): even = lax.ppermute(sent[0], 'fsdp', evens)  13.4 us
    unnamed x50, local copies, waits for them, and re-layouts  9.2 us
    ppermute x1, waiting for transfers between devices, local(): lax.ppermute(doc_ids, 'fsdp', [(f, (f + 1) % fsdp) for f in range(fsdp)])  7.54 us
    ppermute x3, starting transfers between devices, local(): pieces.append(lax.ppermute(packed(k), 'fsdp', pair))  6.77 us
    ppermute x1, waiting for transfers between devices, local(): far = lax.ppermute(params_base, 'rep', across)  5.63 us
    ppermute x2, waiting for transfers between devices, local(): total = both.astype(F32) + lax.ppermute(both, 'rep', across).astype(F32)  5.17 us
    ppermute x4, starting transfers between devices, local(): odd = lax.ppermute(sent[1], 'fsdp', odds) if len(sent) > 1 else None  4.79 us
  transfers between devices with their start and end apart: 26, of which 8 were waited for; matrix products, arithmetic and copies ran while one was open for 3% of the time, Pallas kernels for 22%

profile of v1, /device:TPU:0, one launch (start us, length us, event | category | flops | bytes accessed | tf_op | source)
XLA Modules:
  0.0 114.6 jit_solution(1407026636707954826)
XLA Ops:
  0.7 0.8 constant_dynamic-slice_fusion
  1.5 0.7 fusion.10
  4.8 2.6 %dynamic-slice_bitcast_fusion.1 = (bf16[384,512]{1,0:T(8,128)(2,1)}, bf16[384,512]{1,0:T(8,128)(2,1)}, bf16[384,512]{1,0:T(8,128)(2,1)}, bf16[384,512]{1,0:T(8,128)(2,1)}) fusion(bf16[1,384,4096]{2,1,0:T(8,128)(2,1)} %param.9, s32[]{:T(128)S(6)} %select_n.48, s32[]{:T(128)S(6)} %select_n.46, s32[]{:T(128)S(6)} %select_n.45, s32[]{:T(128)S(6)} %select_n.47), kind=kLoop, calls=%fused_computation.4 | loop fusion | bytes 3145744 | tf_op jit(solution)/shard_map/dynamic_slice | solution.py:203
  7.4 2.9 %collective-permute-start.5 = (bf16[384,512]{1,0:T(8,128)(2,1)}, bf16[384,512]{1,0:T(8,128)(2,1)}, u32[]{:S(2)}, u32[]{:S(2)}) collective-permute-start(bf16[384,512]{1,0:T(8,128)(2,1)} %get-tuple-element.42), channel_id=1, source_target_pairs={{0,1},{1,0},{2,3},{3,2},{4,5},{5,4},{6,7},{7,6},{8,9},{9,8},{10,11... | collective-permute-start | bytes 1179656 | tf_op jit(solution)/shard_map/ppermute | solution.py:205
  11.5 7.5 %collective-permute-done.prev_ref = s32[1,384]{1,0:T(1,128)S(1)} collective-permute-done((s32[1,384]{1,0:T(1,128)S(1)}, s32[1,384]{1,0:T(1,128)S(1)}, u32[]{:S(2)}, u32[]{:S(2)}) %collective-permute-start) | collective-permute-done | bytes 1568 | tf_op jit(solution)/shard_map/ppermute | solution.py:200
  19.0 1.0 copy-done.19
  20.0 1.3 %shard_map.120 = (bf16[256,384]{1,0:T(8,128)(2,1)S(1)}, bf16[256,384]{1,0:T(8,128)(2,1)S(1)}) custom-call(s32[25]{0:T(128)S(1)} %get-tuple-element.55.row, s32[1,384]{1,0:T(1,128)S(1)} %copy-done.20, s32[1,384]{1,0:T(1,128)S(1)} %collective-permute-done.prev_ref, bf16[384,512]{1,0:T(8,128)(2,1)S(1)} %bitcast.68), custom_call_target="tpu_custom_call" | custom-call | tf_op jit(solution)/shard_map/pallas_call | solution.py:148
  21.3 2.5 %collective-permute-start.11 = (bf16[256,384]{1,0:T(8,128)(2,1)S(1)}, bf16[256,384]{1,0:T(8,128)(2,1)S(1)}, u32[]{:S(2)}, u32[]{:S(2)}) collective-permute-start(bf16[256,384]{1,0:T(8,128)(2,1)S(1)} %get-tuple-element.27.refs_0_), channel_id=1, source_target_pairs={{0,1},{1,0},{2,3},{3,2},{4,5},{5,4},{6,7},{7,6},{8,9},{9,8},{10,11... | collective-permute-start | bytes 589832 | tf_op jit(solution)/shard_map/ppermute | solution.py:210
  23.9 1.1 dynamic-slice_bitcast_fusion
  25.2 2.0 %collective-permute-start.3 = (bf16[384,512]{1,0:T(8,128)(2,1)}, bf16[384,512]{1,0:T(8,128)(2,1)S(1)}, u32[]{:S(2)}, u32[]{:S(2)}) collective-permute-start(bf16[384,512]{1,0:T(8,128)(2,1)} %get-tuple-element.43), channel_id=1, source_target_pairs={{0,1},{1,0},{2,3},{3,2},{4,5},{5,4},{6,7},{7,6},{8,9},{9,8},{10,11... | collective-permute-start | bytes 1179656 | tf_op jit(solution)/shard_map/ppermute | solution.py:212
  27.1 1.3 %collective-permute-done.11.refs_1_ = bf16[256,384]{1,0:T(8,128)(2,1)S(1)} collective-permute-done((bf16[256,384]{1,0:T(8,128)(2,1)S(1)}, bf16[256,384]{1,0:T(8,128)(2,1)S(1)}, u32[]{:S(2)}, u32[]{:S(2)}) %collective-permute-start.11) | collective-permute-done | bytes 196640 | tf_op jit(solution)/shard_map/ppermute | solution.py:210
  28.4 2.5 %collective-permute-start.4 = (bf16[384,512]{1,0:T(8,128)(2,1)}, bf16[384,512]{1,0:T(8,128)(2,1)S(1)}, u32[]{:S(2)}, u32[]{:S(2)}) collective-permute-start(bf16[384,512]{1,0:T(8,128)(2,1)} %get-tuple-element.45), channel_id=1, source_target_pairs={{0,1},{1,0},{2,3},{3,2},{4,5},{5,4},{6,7},{7,6},{8,9},{9,8},{10,11... | collective-permute-start | bytes 1179656 | tf_op jit(solution)/shard_map/ppermute | solution.py:212
  30.9 2.0 %shard_map.124 = bf16[256,512]{1,0:T(8,128)(2,1)S(1)} custom-call(s32[25]{0:T(128)S(1)} %get-tuple-element.55.row, bf16[256,384]{1,0:T(8,128)(2,1)S(1)} %get-tuple-element.27.refs_0_, bf16[256,384]{1,0:T(8,128)(2,1)S(1)} %collective-permute-done.11.refs_1_, bf16[384,4096]{1,0:T(8,128)(2,1)S(1)} %bitcast.54, ...), custom_call_target="tpu_custom_call" | custom-call | tf_op jit(solution)/shard_map/pallas_call | solution.py:148
  32.9 1.2 %collective-permute-start.12 = (bf16[256,512]{1,0:T(8,128)(2,1)S(1)}, bf16[256,512]{1,0:T(8,128)(2,1)S(1)}, u32[]{:S(2)}, u32[]{:S(2)}) collective-permute-start(bf16[256,512]{1,0:T(8,128)(2,1)S(1)} %shard_map.124), channel_id=1, source_target_pairs={{0,2},{2,0},{1,3},{3,1},{4,6},{6,4},{5,7},{7,5},{8,10},{10,8},{9,1... | collective-permute-start | bytes 786440 | tf_op jit(solution)/shard_map/ppermute | solution.py:255
  34.1 2.0 %shard_map.121 = bf16[256,512]{1,0:T(8,128)(2,1)S(1)} custom-call(s32[25]{0:T(128)S(1)} %get-tuple-element.55.row, bf16[256,384]{1,0:T(8,128)(2,1)S(1)} %get-tuple-element.22.refs_0_, bf16[256,384]{1,0:T(8,128)(2,1)S(1)} %collective-permute-done.1.refs_1_, bf16[384,4096]{1,0:T(8,128)(2,1)S(1)} %bitcast.55, ...), custom_call_target="tpu_custom_call" | custom-call | tf_op jit(solution)/shard_map/pallas_call | solution.py:148
  36.6 4.6 %collective-permute-done.3.refs_5_.refs_4_ = bf16[384,512]{1,0:T(8,128)(2,1)S(1)} collective-permute-done((bf16[384,512]{1,0:T(8,128)(2,1)}, bf16[384,512]{1,0:T(8,128)(2,1)S(1)}, u32[]{:S(2)}, u32[]{:S(2)}) %collective-permute-start.3) | collective-permute-done | bytes 393248 | tf_op jit(solution)/shard_map/ppermute | solution.py:212
  41.2 2.3 %collective-permute-start.2 = (bf16[384,512]{1,0:T(8,128)(2,1)}, bf16[384,512]{1,0:T(8,128)(2,1)}, u32[]{:S(2)}, u32[]{:S(2)}) collective-permute-start(bf16[384,512]{1,0:T(8,128)(2,1)} %get-tuple-element.44), channel_id=1, source_target_pairs={{0,1},{1,0},{2,3},{3,2},{4,5},{5,4},{6,7},{7,6},{8,9},{9,8},{10,11... | collective-permute-start | bytes 1179656 | tf_op jit(solution)/shard_map/ppermute | solution.py:212
  43.6 2.8 %shard_map.125 = (bf16[256,512]{1,0:T(8,128)(2,1)}, bf16[256,512]{1,0:T(8,128)(2,1)}) custom-call(s32[25]{0:T(128)S(1)} %get-tuple-element.55.row, bf16[256,384]{1,0:T(8,128)(2,1)S(1)} %get-tuple-element.27.refs_0_, bf16[256,384]{1,0:T(8,128)(2,1)S(1)} %collective-permute-done.11.refs_1_, bf16[384,4096]{1,0:T(8,128)(2,1)S(1)} %bitcast.56, ...), custom_call_target="tpu_custom_call" | custom-call | tf_op jit(solution)/shard_map/pallas_call | solution.py:148
  46.4 1.4 %collective-permute-start.13 = (bf16[256,512]{1,0:T(8,128)(2,1)}, bf16[256,512]{1,0:T(8,128)(2,1)}, u32[]{:S(2)}, u32[]{:S(2)}) collective-permute-start(bf16[256,512]{1,0:T(8,128)(2,1)} %get-tuple-element.28), channel_id=1, source_target_pairs={{2,4},{4,2},{3,5},{5,3},{10,12},{12,10},{11,13},{13,11},{18,20},{2... | collective-permute-start | bytes 786440 | tf_op jit(solution)/shard_map/ppermute | solution.py:256
  47.7 3.8 %collective-permute-start.14 = (bf16[256,512]{1,0:T(8,128)(2,1)}, bf16[256,512]{1,0:T(8,128)(2,1)}, u32[]{:S(2)}, u32[]{:S(2)}) collective-permute-start(bf16[256,512]{1,0:T(8,128)(2,1)} %get-tuple-element.29), channel_id=1, source_target_pairs={{0,2},{2,0},{1,3},{3,1},{4,6},{6,4},{5,7},{7,5},{8,10},{10,8},{9,1... | collective-permute-start | bytes 786440 | tf_op jit(solution)/shard_map/ppermute | solution.py:255
  51.5 2.8 %shard_map.122 = (bf16[256,512]{1,0:T(8,128)(2,1)}, bf16[256,512]{1,0:T(8,128)(2,1)}) custom-call(s32[25]{0:T(128)S(1)} %get-tuple-element.55.row, bf16[256,384]{1,0:T(8,128)(2,1)S(1)} %get-tuple-element.22.refs_0_, bf16[256,384]{1,0:T(8,128)(2,1)S(1)} %collective-permute-done.1.refs_1_, bf16[384,4096]{1,0:T(8,128)(2,1)S(1)} %bitcast.58, ...), custom_call_target="tpu_custom_call" | custom-call | tf_op jit(solution)/shard_map/pallas_call | solution.py:148
  54.3 0.7 copy-done.17
  55.0 1.4 %collective-permute-start.7 = (bf16[256,512]{1,0:T(8,128)(2,1)}, bf16[256,512]{1,0:T(8,128)(2,1)}, u32[]{:S(2)}, u32[]{:S(2)}) collective-permute-start(bf16[256,512]{1,0:T(8,128)(2,1)} %get-tuple-element.23), channel_id=1, source_target_pairs={{2,4},{4,2},{3,5},{5,3},{10,12},{12,10},{11,13},{13,11},{18,20},{2... | collective-permute-start | bytes 786440 | tf_op jit(solution)/shard_map/ppermute | solution.py:256
  56.4 1.6 %collective-permute-start.8 = (bf16[256,512]{1,0:T(8,128)(2,1)}, bf16[256,512]{1,0:T(8,128)(2,1)}, u32[]{:S(2)}, u32[]{:S(2)}) collective-permute-start(bf16[256,512]{1,0:T(8,128)(2,1)} %get-tuple-element.24), channel_id=1, source_target_pairs={{0,2},{2,0},{1,3},{3,1},{4,6},{6,4},{5,7},{7,5},{8,10},{10,8},{9,1... | collective-permute-start | bytes 786440 | tf_op jit(solution)/shard_map/ppermute | solution.py:255
  61.0 1.3 %bitcast_add_fusion = f32[2,128,512]{2,1,0:T(8,128)S(1)} fusion(f32[2,128,512]{2,1,0:T(8,128)} %collective-permute-done.17, f32[2,2,128,512]{3,2,1,0:T(8,128)} %bitcast.72, s32[]{:T(128)S(6)} %select_n.49), kind=kLoop, calls=%fused_computation.2 | loop fusion | flops 131072 | bytes 1572868 | tf_op jit(solution)/shard_map/add | solution.py:219
  62.4 1.2 %copy-done.12 = bf16[256,384]{1,0:T(8,128)(2,1)S(1)} copy-done((bf16[256,384]{1,0:T(8,128)(2,1)S(1)}, bf16[256,384]{1,0:T(8,128)(2,1)}, u32[]{:S(2)}) %copy-start.12) | copy-done | bytes 196632
  63.5 0.9 copy-done.15
  64.5 1.0 copy-done.18
  65.5 2.8 %shard_map.126 = (bf16[256,512]{1,0:T(8,128)(2,1)}, bf16[256,512]{1,0:T(8,128)(2,1)}) custom-call(s32[25]{0:T(128)S(1)} %get-tuple-element.55.row, bf16[256,384]{1,0:T(8,128)(2,1)S(1)} %copy-done.12, bf16[256,384]{1,0:T(8,128)(2,1)S(1)} %copy-done.15, bf16[384,4096]{1,0:T(8,128)(2,1)S(1)} %bitcast.60, bf16[384,4096]{1,0:T(8,128)(2,1)S(1)} %bitcast.61, ...), custom_call_target="tpu_custom_call" | custom-call | tf_op jit(solution)/shard_map/pallas_call | solution.py:148
  68.3 0.9 collective-permute-start.15
  69.2 1.4 %collective-permute-start.16 = (bf16[256,512]{1,0:T(8,128)(2,1)}, bf16[256,512]{1,0:T(8,128)(2,1)}, u32[]{:S(2)}, u32[]{:S(2)}) collective-permute-start(bf16[256,512]{1,0:T(8,128)(2,1)} %get-tuple-element.31), channel_id=1, source_target_pairs={{2,4},{4,2},{3,5},{5,3},{10,12},{12,10},{11,13},{13,11},{18,20},{2... | collective-permute-start | bytes 786440 | tf_op jit(solution)/shard_map/ppermute | solution.py:256
  70.6 2.8 %shard_map.123 = (bf16[256,512]{1,0:T(8,128)(2,1)}, bf16[256,512]{1,0:T(8,128)(2,1)}) custom-call(s32[25]{0:T(128)S(1)} %get-tuple-element.55.row, bf16[256,384]{1,0:T(8,128)(2,1)S(1)} %copy-done.6, bf16[256,384]{1,0:T(8,128)(2,1)S(1)} %copy-done.9, bf16[384,4096]{1,0:T(8,128)(2,1)S(1)} %bitcast.62, bf16[384,4096]{1,0:T(8,128)(2,1)S(1)} %bitcast.63, ...), custom_call_target="tpu_custom_call" | custom-call | tf_op jit(solution)/shard_map/pallas_call | solution.py:148
  74.1 5.4 %collective-permute-start.9 = (bf16[256,512]{1,0:T(8,128)(2,1)}, bf16[256,512]{1,0:T(8,128)(2,1)S(1)}, u32[]{:S(2)}, u32[]{:S(2)}) collective-permute-start(bf16[256,512]{1,0:T(8,128)(2,1)} %get-tuple-element.25), channel_id=1, source_target_pairs={{0,2},{2,0},{1,3},{3,1},{4,6},{6,4},{5,7},{7,5},{8,10},{10,8},{9,1... | collective-permute-start | bytes 786440 | tf_op jit(solution)/shard_map/ppermute | solution.py:255
  79.5 1.6 %collective-permute-start.18 = (f32[128,512]{1,0:T(8,128)S(1)}, f32[128,512]{1,0:T(8,128)S(1)}, u32[]{:S(2)}, u32[]{:S(2)}) collective-permute-start(f32[128,512]{1,0:T(8,128)S(1)} %dynamic-slice_bitcast_fusion.5), channel_id=1, source_target_pairs={{0,16},{8,24},{16,0},{24,8},{1,17},{9,25},{17,1},{25,9},{2,18},{10... | collective-permute-start | bytes 786440 | tf_op jit(solution)/shard_map/ppermute | solution.py:223
  83.9 1.2 %copy-done.1 = f32[1,512,512]{2,1,0:T(8,128)S(1)} copy-done((f32[1,512,512]{2,1,0:T(8,128)S(1)}, f32[1,512,512]{2,1,0:T(8,128)}, u32[]{:S(2)}) %copy-start.1) | copy-done | bytes 1048600
  85.1 1.2 %copy-done.3 = f32[1,512,512]{2,1,0:T(8,128)S(1)} copy-done((f32[1,512,512]{2,1,0:T(8,128)S(1)}, f32[1,512,512]{2,1,0:T(8,128)}, u32[]{:S(2)}) %copy-start.3) | copy-done | bytes 1048600
  86.4 0.9 copy-done.13
  87.3 0.9 copy-done.16
  88.2 3.8 %shard_map.127 = (f32[512,512]{1,0:T(8,128)}, f32[512,512]{1,0:T(8,128)}, f32[2,128,256]{2,1,0:T(8,128)S(1)}, bf16[2,128,256]{2,1,0:T(8,128)(2,1)S(1)}) custom-call(s32[25]{0:T(128)S(1)} %get-tuple-element.55.row, bf16[256,384]{1,0:T(8,128)(2,1)S(1)} %copy-done.13, bf16[256,384]{1,0:T(8,128)(2,1)S(1)} %copy-done.16, bf16[384,4096]{1,0:T(8,128)(2,1)} %bitcast.52, ...), custom_call_target="tpu_custom_call" | custom-call | tf_op jit(solution)/shard_map/pallas_call | solution.py:148
  92.1 3.5 %shard_map.128 = (f32[512,512]{1,0:T(8,128)}, f32[512,512]{1,0:T(8,128)}, f32[2,128,256]{2,1,0:T(8,128)S(1)}, bf16[2,128,256]{2,1,0:T(8,128)(2,1)S(1)}) custom-call(s32[25]{0:T(128)S(1)} %get-tuple-element.55.row, bf16[256,384]{1,0:T(8,128)(2,1)S(1)} %copy-done.7, bf16[256,384]{1,0:T(8,128)(2,1)S(1)} %copy-done.10, ...), custom_call_target="tpu_custom_call", output_to_operand_aliasing={{0}: (9, {}), {1}: (10, {})} | custom-call | tf_op jit(solution)/shard_map/pallas_call | solution.py:148
  96.9 1.2 %collective-permute-start.22 = (bf16[2,128,256]{2,1,0:T(8,128)(2,1)S(1)}, bf16[2,128,256]{2,1,0:T(8,128)(2,1)S(1)}, u32[]{:S(2)}, u32[]{:S(2)}) collective-permute-start(bf16[2,128,256]{2,1,0:T(8,128)(2,1)S(1)} %add_convert_fusion), channel_id=1, source_target_pairs={{0,16},{8,24},{16,0},{24,8},{1,17},{9,25},{17,1},{25,9},{2,18},{10... | collective-permute-start | bytes 393224 | tf_op jit(solution)/shard_map/ppermute | solution.py:295
  98.2 1.1 collective-permute-start.20
  99.3 5.6 %collective-permute-done.23 = f32[128,512]{1,0:T(8,128)S(1)} collective-permute-done((f32[128,512]{1,0:T(8,128)S(1)}, f32[128,512]{1,0:T(8,128)S(1)}, u32[]{:S(2)}, u32[]{:S(2)}) %collective-permute-start.23) | collective-permute-done | bytes 262176 | tf_op jit(solution)/shard_map/ppermute | solution.py:230
  104.9 2.8 %collective-permute-done.22 = bf16[2,128,256]{2,1,0:T(8,128)(2,1)S(1)} collective-permute-done((bf16[2,128,256]{2,1,0:T(8,128)(2,1)S(1)}, bf16[2,128,256]{2,1,0:T(8,128)(2,1)S(1)}, u32[]{:S(2)}, u32[]{:S(2)}) %collective-permute-start.22) | collective-permute-done | bytes 131104 | tf_op jit(solution)/shard_map/ppermute | solution.py:295
  107.7 2.4 %collective-permute-done.20 = bf16[2,128,256]{2,1,0:T(8,128)(2,1)S(1)} collective-permute-done((bf16[2,128,256]{2,1,0:T(8,128)(2,1)S(1)}, bf16[2,128,256]{2,1,0:T(8,128)(2,1)S(1)}, u32[]{:S(2)}, u32[]{:S(2)}) %collective-permute-start.20) | collective-permute-done | bytes 131104 | tf_op jit(solution)/shard_map/ppermute | solution.py:295
  110.8 0.7 pad_maximum_fusion.1
  111.8 1.4 %shard_map.129.refs_0_ = f32[512,512]{1,0:T(8,128)} custom-call(s32[25]{0:T(128)S(1)} %get-tuple-element.55.row, f32[2,128,256]{2,1,0:T(8,128)S(1)} %get-tuple-element.46.mine, f32[2,128,256]{2,1,0:T(8,128)S(1)} %collective-permute-done.25.theirs), custom_call_target="tpu_custom_call" | custom-call | tf_op jit(solution)/shard_map/pallas_call | solution.py:148
  113.2 1.4 %shard_map.130 = f32[512,512]{1,0:T(8,128)} custom-call(s32[25]{0:T(128)S(1)} %get-tuple-element.55.row, f32[2,128,256]{2,1,0:T(8,128)S(1)} %get-tuple-element.47.mine, f32[2,128,256]{2,1,0:T(8,128)S(1)} %collective-permute-done.24.theirs, f32[512,512]{1,0:T(8,128)} %shard_map.129.refs_0_), custom_call_target="tpu_custom_call", output_to_operand_aliasing={{}: (3, {})} | custom-call | tf_op jit(solution)/shard_map/pallas_call | solution.py:148
  (78 shorter events, 4.0 us)
Async XLA Ops:
  0.6 30.3 %copy-start = (bf16[1,384,4096]{2,1,0:T(8,128)(2,1)S(1)}, bf16[1,384,4096]{2,1,0:T(8,128)(2,1)}, u32[]{:S(2)}) copy-start(bf16[1,384,4096]{2,1,0:T(8,128)(2,1)} %param.9) | copy-start | bytes 9437188
  0.6 9.7 %copy-start.20 = (s32[1,384]{1,0:T(1,128)S(1)}, s32[1,384]{1,0:T(1,128)}, u32[]{:S(2)}) copy-start(s32[1,384]{1,0:T(1,128)} %doc_ref.1) | copy-start | bytes 4612
  7.4 23.6 %collective-permute-start.5 = (bf16[384,512]{1,0:T(8,128)(2,1)}, bf16[384,512]{1,0:T(8,128)(2,1)}, u32[]{:S(2)}, u32[]{:S(2)}) collective-permute-start(bf16[384,512]{1,0:T(8,128)(2,1)} %get-tuple-element.42), channel_id=1, source_target_pairs={{0,1},{1,0},{2,3},{3,2},{4,5},{5,4},{6,7},{7,6},{8,9},{9,8},{10,11... | collective-permute-start | bytes 1179656 | tf_op jit(solution)/shard_map/ppermute | solution.py:205
  10.3 8.7 %collective-permute-start = (s32[1,384]{1,0:T(1,128)S(1)}, s32[1,384]{1,0:T(1,128)S(1)}, u32[]{:S(2)}, u32[]{:S(2)}) collective-permute-start(s32[1,384]{1,0:T(1,128)S(1)} %copy-done.20), channel_id=1, source_target_pairs={{0,1},{1,2},{2,3},{3,4},{4,5},{5,6},{6,7},{7,0},{8,9},{9,10},{10,1... | collective-permute-start | bytes 4616 | tf_op jit(solution)/shard_map/ppermute | solution.py:200
  19.0 1.0 copy-start.19
  21.3 22.3 %copy-start.11 = (bf16[256,384]{1,0:T(8,128)(2,1)}, bf16[256,384]{1,0:T(8,128)(2,1)S(1)}, u32[]{:S(2)}) copy-start(bf16[256,384]{1,0:T(8,128)(2,1)S(1)} %get-tuple-element.27.refs_0_) | copy-start | bytes 589828
  21.3 30.2 %copy-start.5 = (bf16[256,384]{1,0:T(8,128)(2,1)}, bf16[256,384]{1,0:T(8,128)(2,1)S(1)}, u32[]{:S(2)}) copy-start(bf16[256,384]{1,0:T(8,128)(2,1)S(1)} %get-tuple-element.22.refs_0_) | copy-start | bytes 589828
  21.3 7.1 %collective-permute-start.11 = (bf16[256,384]{1,0:T(8,128)(2,1)S(1)}, bf16[256,384]{1,0:T(8,128)(2,1)S(1)}, u32[]{:S(2)}, u32[]{:S(2)}) collective-permute-start(bf16[256,384]{1,0:T(8,128)(2,1)S(1)} %get-tuple-element.27.refs_0_), channel_id=1, source_target_pairs={{0,1},{1,0},{2,3},{3,2},{4,5},{5,4},{6,7},{7,6},{8,9},{9,8},{10,11... | collective-permute-start | bytes 589832 | tf_op jit(solution)/shard_map/ppermute | solution.py:210
  25.0 31.5 %collective-permute-start.17 = (f32[2,128,512]{2,1,0:T(8,128)S(1)}, f32[2,128,512]{2,1,0:T(8,128)}, u32[]{:S(2)}, u32[]{:S(2)}) collective-permute-start(f32[2,128,512]{2,1,0:T(8,128)S(1)} %dynamic-slice_bitcast_fusion), channel_id=1, source_target_pairs={{0,8},{8,0},{16,24},{24,16},{1,9},{9,1},{17,25},{25,17},{2,10},{10... | collective-permute-start | bytes 1572872 | tf_op jit(solution)/shard_map/ppermute | solution.py:219
  25.0 9.1 %collective-permute-start.1 = (bf16[256,384]{1,0:T(8,128)(2,1)S(1)}, bf16[256,384]{1,0:T(8,128)(2,1)S(1)}, u32[]{:S(2)}, u32[]{:S(2)}) collective-permute-start(bf16[256,384]{1,0:T(8,128)(2,1)S(1)} %get-tuple-element.22.refs_0_), channel_id=1, source_target_pairs={{0,1},{1,0},{2,3},{3,2},{4,5},{5,4},{6,7},{7,6},{8,9},{9,8},{10,11... | collective-permute-start | bytes 589832 | tf_op jit(solution)/shard_map/ppermute | solution.py:210
  25.2 16.1 %collective-permute-start.3 = (bf16[384,512]{1,0:T(8,128)(2,1)}, bf16[384,512]{1,0:T(8,128)(2,1)S(1)}, u32[]{:S(2)}, u32[]{:S(2)}) collective-permute-start(bf16[384,512]{1,0:T(8,128)(2,1)} %get-tuple-element.43), channel_id=1, source_target_pairs={{0,1},{1,0},{2,3},{3,2},{4,5},{5,4},{6,7},{7,6},{8,9},{9,8},{10,11... | collective-permute-start | bytes 1179656 | tf_op jit(solution)/shard_map/ppermute | solution.py:212
  28.4 15.1 %copy-start.14 = (bf16[256,384]{1,0:T(8,128)(2,1)}, bf16[256,384]{1,0:T(8,128)(2,1)S(1)}, u32[]{:S(2)}) copy-start(bf16[256,384]{1,0:T(8,128)(2,1)S(1)} %collective-permute-done.11.refs_1_) | copy-start | bytes 589828
  28.4 25.9 %collective-permute-start.4 = (bf16[384,512]{1,0:T(8,128)(2,1)}, bf16[384,512]{1,0:T(8,128)(2,1)S(1)}, u32[]{:S(2)}, u32[]{:S(2)}) collective-permute-start(bf16[384,512]{1,0:T(8,128)(2,1)} %get-tuple-element.45), channel_id=1, source_target_pairs={{0,1},{1,0},{2,3},{3,2},{4,5},{5,4},{6,7},{7,6},{8,9},{9,8},{10,11... | collective-permute-start | bytes 1179656 | tf_op jit(solution)/shard_map/ppermute | solution.py:212
  32.9 10.7 %collective-permute-start.12 = (bf16[256,512]{1,0:T(8,128)(2,1)S(1)}, bf16[256,512]{1,0:T(8,128)(2,1)S(1)}, u32[]{:S(2)}, u32[]{:S(2)}) collective-permute-start(bf16[256,512]{1,0:T(8,128)(2,1)S(1)} %shard_map.124), channel_id=1, source_target_pairs={{0,2},{2,0},{1,3},{3,1},{4,6},{6,4},{5,7},{7,5},{8,10},{10,8},{9,1... | collective-permute-start | bytes 786440 | tf_op jit(solution)/shard_map/ppermute | solution.py:255
  34.1 17.4 %copy-start.8 = (bf16[256,384]{1,0:T(8,128)(2,1)}, bf16[256,384]{1,0:T(8,128)(2,1)S(1)}, u32[]{:S(2)}) copy-start(bf16[256,384]{1,0:T(8,128)(2,1)S(1)} %collective-permute-done.1.refs_1_) | copy-start | bytes 589828
  36.1 11.6 %collective-permute-start.6 = (bf16[256,512]{1,0:T(8,128)(2,1)S(1)}, bf16[256,512]{1,0:T(8,128)(2,1)S(1)}, u32[]{:S(2)}, u32[]{:S(2)}) collective-permute-start(bf16[256,512]{1,0:T(8,128)(2,1)S(1)} %shard_map.121), channel_id=1, source_target_pairs={{0,2},{2,0},{1,3},{3,1},{4,6},{6,4},{5,7},{7,5},{8,10},{10,8},{9,1... | collective-permute-start | bytes 786440 | tf_op jit(solution)/shard_map/ppermute | solution.py:255
  41.2 38.3 %collective-permute-start.2 = (bf16[384,512]{1,0:T(8,128)(2,1)}, bf16[384,512]{1,0:T(8,128)(2,1)}, u32[]{:S(2)}, u32[]{:S(2)}) collective-permute-start(bf16[384,512]{1,0:T(8,128)(2,1)} %get-tuple-element.44), channel_id=1, source_target_pairs={{0,1},{1,0},{2,3},{3,2},{4,5},{5,4},{6,7},{7,6},{8,9},{9,8},{10,11... | collective-permute-start | bytes 1179656 | tf_op jit(solution)/shard_map/ppermute | solution.py:212
  46.4 16.0 %collective-permute-start.13 = (bf16[256,512]{1,0:T(8,128)(2,1)}, bf16[256,512]{1,0:T(8,128)(2,1)}, u32[]{:S(2)}, u32[]{:S(2)}) collective-permute-start(bf16[256,512]{1,0:T(8,128)(2,1)} %get-tuple-element.28), channel_id=1, source_target_pairs={{2,4},{4,2},{3,5},{5,3},{10,12},{12,10},{11,13},{13,11},{18,20},{2... | collective-permute-start | bytes 786440 | tf_op jit(solution)/shard_map/ppermute | solution.py:256
  47.7 14.6 %collective-permute-start.14 = (bf16[256,512]{1,0:T(8,128)(2,1)}, bf16[256,512]{1,0:T(8,128)(2,1)}, u32[]{:S(2)}, u32[]{:S(2)}) collective-permute-start(bf16[256,512]{1,0:T(8,128)(2,1)} %get-tuple-element.29), channel_id=1, source_target_pairs={{0,2},{2,0},{1,3},{3,1},{4,6},{6,4},{5,7},{7,5},{8,10},{10,8},{9,1... | collective-permute-start | bytes 786440 | tf_op jit(solution)/shard_map/ppermute | solution.py:255
  55.0 15.5 %collective-permute-start.7 = (bf16[256,512]{1,0:T(8,128)(2,1)}, bf16[256,512]{1,0:T(8,128)(2,1)}, u32[]{:S(2)}, u32[]{:S(2)}) collective-permute-start(bf16[256,512]{1,0:T(8,128)(2,1)} %get-tuple-element.23), channel_id=1, source_target_pairs={{2,4},{4,2},{3,5},{5,3},{10,12},{12,10},{11,13},{13,11},{18,20},{2... | collective-permute-start | bytes 786440 | tf_op jit(solution)/shard_map/ppermute | solution.py:256
  56.4 14.1 %collective-permute-start.8 = (bf16[256,512]{1,0:T(8,128)(2,1)}, bf16[256,512]{1,0:T(8,128)(2,1)}, u32[]{:S(2)}, u32[]{:S(2)}) collective-permute-start(bf16[256,512]{1,0:T(8,128)(2,1)} %get-tuple-element.24), channel_id=1, source_target_pairs={{0,2},{2,0},{1,3},{3,1},{4,6},{6,4},{5,7},{7,5},{8,10},{10,8},{9,1... | collective-permute-start | bytes 786440 | tf_op jit(solution)/shard_map/ppermute | solution.py:255
  62.3 17.2 %copy-start.21 = (f32[2,128,512]{2,1,0:T(8,128)}, f32[2,128,512]{2,1,0:T(8,128)S(1)}, u32[]{:S(2)}) copy-start(f32[2,128,512]{2,1,0:T(8,128)S(1)} %bitcast_add_fusion) | copy-start | bytes 1572868
  62.3 8.2 %copy-start.6 = (bf16[256,384]{1,0:T(8,128)(2,1)S(1)}, bf16[256,384]{1,0:T(8,128)(2,1)}, u32[]{:S(2)}) copy-start(bf16[256,384]{1,0:T(8,128)(2,1)} %copy-done.5) | copy-start | bytes 589828
  62.3 8.2 %copy-start.9 = (bf16[256,384]{1,0:T(8,128)(2,1)S(1)}, bf16[256,384]{1,0:T(8,128)(2,1)}, u32[]{:S(2)}) copy-start(bf16[256,384]{1,0:T(8,128)(2,1)} %copy-done.8) | copy-start | bytes 589828
  62.4 1.2 %copy-start.12 = (bf16[256,384]{1,0:T(8,128)(2,1)S(1)}, bf16[256,384]{1,0:T(8,128)(2,1)}, u32[]{:S(2)}) copy-start(bf16[256,384]{1,0:T(8,128)(2,1)} %copy-done.11) | copy-start | bytes 589828
  63.5 0.9 copy-start.15
  64.5 1.0 copy-start.18
  68.3 15.6 %collective-permute-start.15 = (bf16[256,512]{1,0:T(8,128)(2,1)}, bf16[256,512]{1,0:T(8,128)(2,1)}, u32[]{:S(2)}, u32[]{:S(2)}) collective-permute-start(bf16[256,512]{1,0:T(8,128)(2,1)} %get-tuple-element.30), channel_id=1, source_target_pairs={{0,2},{2,0},{1,3},{3,1},{4,6},{6,4},{5,7},{7,5},{8,10},{10,8},{9,1... | collective-permute-start | bytes 786440 | tf_op jit(solution)/shard_map/ppermute | solution.py:255
  69.2 14.7 %collective-permute-start.16 = (bf16[256,512]{1,0:T(8,128)(2,1)}, bf16[256,512]{1,0:T(8,128)(2,1)}, u32[]{:S(2)}, u32[]{:S(2)}) collective-permute-start(bf16[256,512]{1,0:T(8,128)(2,1)} %get-tuple-element.31), channel_id=1, source_target_pairs={{2,4},{4,2},{3,5},{5,3},{10,12},{12,10},{11,13},{13,11},{18,20},{2... | collective-permute-start | bytes 786440 | tf_op jit(solution)/shard_map/ppermute | solution.py:256
  73.4 18.6 %collective-permute-start.10 = (bf16[256,512]{1,0:T(8,128)(2,1)}, bf16[256,512]{1,0:T(8,128)(2,1)S(1)}, u32[]{:S(2)}, u32[]{:S(2)}) collective-permute-start(bf16[256,512]{1,0:T(8,128)(2,1)} %get-tuple-element.26), channel_id=1, source_target_pairs={{2,4},{4,2},{3,5},{5,3},{10,12},{12,10},{11,13},{13,11},{18,20},{2... | collective-permute-start | bytes 786440 | tf_op jit(solution)/shard_map/ppermute | solution.py:256
  74.1 17.9 %collective-permute-start.9 = (bf16[256,512]{1,0:T(8,128)(2,1)}, bf16[256,512]{1,0:T(8,128)(2,1)S(1)}, u32[]{:S(2)}, u32[]{:S(2)}) collective-permute-start(bf16[256,512]{1,0:T(8,128)(2,1)} %get-tuple-element.25), channel_id=1, source_target_pairs={{0,2},{2,0},{1,3},{3,1},{4,6},{6,4},{5,7},{7,5},{8,10},{10,8},{9,1... | collective-permute-start | bytes 786440 | tf_op jit(solution)/shard_map/ppermute | solution.py:255
  79.5 16.0 %collective-permute-start.18 = (f32[128,512]{1,0:T(8,128)S(1)}, f32[128,512]{1,0:T(8,128)S(1)}, u32[]{:S(2)}, u32[]{:S(2)}) collective-permute-start(f32[128,512]{1,0:T(8,128)S(1)} %dynamic-slice_bitcast_fusion.5), channel_id=1, source_target_pairs={{0,16},{8,24},{16,0},{24,8},{1,17},{9,25},{17,1},{25,9},{2,18},{10... | collective-permute-start | bytes 786440 | tf_op jit(solution)/shard_map/ppermute | solution.py:223
  83.9 1.2 %copy-start.1 = (f32[1,512,512]{2,1,0:T(8,128)S(1)}, f32[1,512,512]{2,1,0:T(8,128)}, u32[]{:S(2)}) copy-start(f32[1,512,512]{2,1,0:T(8,128)} %param.13) | copy-start | bytes 3145732
  85.1 1.2 %copy-start.3 = (f32[1,512,512]{2,1,0:T(8,128)S(1)}, f32[1,512,512]{2,1,0:T(8,128)}, u32[]{:S(2)}) copy-start(f32[1,512,512]{2,1,0:T(8,128)} %param.14) | copy-start | bytes 3145732
  88.2 3.8 %copy-start.2 = (f32[1,512,512]{2,1,0:T(8,128)S(1)}, f32[1,512,512]{2,1,0:T(8,128)}, u32[]{:S(2)}) copy-start(f32[1,512,512]{2,1,0:T(8,128)} %param.13) | copy-start | bytes 3145732
  88.2 3.8 %copy-start.4 = (f32[1,512,512]{2,1,0:T(8,128)S(1)}, f32[1,512,512]{2,1,0:T(8,128)}, u32[]{:S(2)}) copy-start(f32[1,512,512]{2,1,0:T(8,128)} %param.14) | copy-start | bytes 3145732
  88.2 3.8 %copy-start.7 = (bf16[256,384]{1,0:T(8,128)(2,1)S(1)}, bf16[256,384]{1,0:T(8,128)(2,1)}, u32[]{:S(2)}) copy-start(bf16[256,384]{1,0:T(8,128)(2,1)} %copy-done.5) | copy-start | bytes 589828
  88.2 3.8 %copy-start.10 = (bf16[256,384]{1,0:T(8,128)(2,1)S(1)}, bf16[256,384]{1,0:T(8,128)(2,1)}, u32[]{:S(2)}) copy-start(bf16[256,384]{1,0:T(8,128)(2,1)} %copy-done.8) | copy-start | bytes 589828
  92.1 3.5 %copy-start.22 = (f32[2,128,512]{2,1,0:T(8,128)S(1)}, f32[2,128,512]{2,1,0:T(8,128)}, u32[]{:S(2)}) copy-start(f32[2,128,512]{2,1,0:T(8,128)} %copy-done.21) | copy-start | bytes 1572868
  92.1 3.5 %copy-start.23 = (f32[128,512]{1,0:T(8,128)S(1)}, f32[128,512]{1,0:T(8,128)}, u32[]{:S(2)}) copy-start(f32[128,512]{1,0:T(8,128)} %param.15) | copy-start | bytes 786436
  92.1 3.5 %copy-start.24 = (f32[128,512]{1,0:T(8,128)S(1)}, f32[128,512]{1,0:T(8,128)}, u32[]{:S(2)}) copy-start(f32[128,512]{1,0:T(8,128)} %param.16) | copy-start | bytes 786436
  95.6 1.3 %collective-permute-start.21 = (bf16[2,128,256]{2,1,0:T(8,128)(2,1)S(1)}, bf16[2,128,256]{2,1,0:T(8,128)(2,1)S(1)}, u32[]{:S(2)}, u32[]{:S(2)}) collective-permute-start(bf16[2,128,256]{2,1,0:T(8,128)(2,1)S(1)} %get-tuple-element.39), channel_id=1, source_target_pairs={{0,8},{8,0},{16,24},{24,16},{1,9},{9,1},{17,25},{25,17},{2,10},{10... | collective-permute-start | bytes 393224 | tf_op jit(solution)/shard_map/ppermute | solution.py:292
  95.7 9.2 %collective-permute-start.23 = (f32[128,512]{1,0:T(8,128)S(1)}, f32[128,512]{1,0:T(8,128)S(1)}, u32[]{:S(2)}, u32[]{:S(2)}) collective-permute-start(f32[128,512]{1,0:T(8,128)S(1)} %get-tuple-element.40), channel_id=1, source_target_pairs={{0,16},{8,24},{16,0},{24,8},{1,17},{9,25},{17,1},{25,9},{2,18},{10... | collective-permute-start | bytes 786440 | tf_op jit(solution)/shard_map/ppermute | solution.py:230
  96.3 1.8 %collective-permute-start.19 = (bf16[2,128,256]{2,1,0:T(8,128)(2,1)S(1)}, bf16[2,128,256]{2,1,0:T(8,128)(2,1)S(1)}, u32[]{:S(2)}, u32[]{:S(2)}) collective-permute-start(bf16[2,128,256]{2,1,0:T(8,128)(2,1)S(1)} %get-tuple-element.37), channel_id=1, source_target_pairs={{0,8},{8,0},{16,24},{24,16},{1,9},{9,1},{17,25},{25,17},{2,10},{10... | collective-permute-start | bytes 393224 | tf_op jit(solution)/shard_map/ppermute | solution.py:292
  96.9 10.8 %collective-permute-start.22 = (bf16[2,128,256]{2,1,0:T(8,128)(2,1)S(1)}, bf16[2,128,256]{2,1,0:T(8,128)(2,1)S(1)}, u32[]{:S(2)}, u32[]{:S(2)}) collective-permute-start(bf16[2,128,256]{2,1,0:T(8,128)(2,1)S(1)} %add_convert_fusion), channel_id=1, source_target_pairs={{0,16},{8,24},{16,0},{24,8},{1,17},{9,25},{17,1},{25,9},{2,18},{10... | collective-permute-start | bytes 393224 | tf_op jit(solution)/shard_map/ppermute | solution.py:295
  98.2 11.9 %collective-permute-start.20 = (bf16[2,128,256]{2,1,0:T(8,128)(2,1)S(1)}, bf16[2,128,256]{2,1,0:T(8,128)(2,1)S(1)}, u32[]{:S(2)}, u32[]{:S(2)}) collective-permute-start(bf16[2,128,256]{2,1,0:T(8,128)(2,1)S(1)} %add_convert_fusion.1), channel_id=1, source_target_pairs={{0,16},{8,24},{16,0},{24,8},{1,17},{9,25},{17,1},{25,9},{2,18},{10... | collective-permute-start | bytes 393224 | tf_op jit(solution)/shard_map/ppermute | solution.py:295
  110.2 1.6 %collective-permute-start.25 = (f32[2,128,256]{2,1,0:T(8,128)S(1)}, f32[2,128,256]{2,1,0:T(8,128)S(1)}, u32[]{:S(2)}, u32[]{:S(2)}) collective-permute-start(f32[2,128,256]{2,1,0:T(8,128)S(1)} %get-tuple-element.46.mine), channel_id=1, source_target_pairs={{0,8},{8,0},{16,24},{24,16},{1,9},{9,1},{17,25},{25,17},{2,10},{10... | collective-permute-start | bytes 786440 | tf_op jit(solution)/shard_map/ppermute | solution.py:302
  110.3 2.9 %collective-permute-start.24 = (f32[2,128,256]{2,1,0:T(8,128)S(1)}, f32[2,128,256]{2,1,0:T(8,128)S(1)}, u32[]{:S(2)}, u32[]{:S(2)}) collective-permute-start(f32[2,128,256]{2,1,0:T(8,128)S(1)} %get-tuple-element.47.mine), channel_id=1, source_target_pairs={{0,8},{8,0},{16,24},{24,16},{1,9},{9,1},{17,25},{25,17},{2,10},{10... | collective-permute-start | bytes 786440 | tf_op jit(solution)/shard_map/ppermute | solution.py:302
  (3 other events, 2.6 us)

commit v2 on v1

v2 whole, which is shorter than its diff:
```python
import functools
import math

import jax
import jax.numpy as jnp
import numpy as np
from jax import lax
from jax.experimental import pallas as pl
from jax.experimental.pallas import tpu as pltpu
from jax.sharding import PartitionSpec as P

HEAD = 128
ROPE_BASE = 500000.0
HALVES = 2
F32, BF16 = jnp.float32, jnp.bfloat16
VMEM_LIMIT = 16 * 1024 * 1024


def schedule(line):
    order = np.zeros((line, line), np.int32)
    for z in range(line):
        when = {}
        for d in range(line):
            when[d] = line - d + z if d > z else (d + line - z if d < z else 10 * line)
        order[z] = sorted(range(line), key=lambda d: (when[d], abs(d - z) * -1))
    place = np.argsort(order, axis=1)
    sends = []
    for t in range(1, line):
        even, odd = [], []
        for z in range(line):
            right = line - t + z
            right = right if right < line else -1
            left = t - line + z
            left = left if left >= 0 else -1
            even.append(right if z % 2 == 0 else left)
            odd.append(left if z % 2 == 0 else right)
        sends.append((even, odd))
    return order, place, sends


def dot(a, b):
    return lax.dot_general(a, b, (((1,), (0,)), ((), ())), preferred_element_type=F32)


def spot():
    here = lax.axis_index("fsdp")
    return lax.div(here, 2), lax.rem(here, 2)


def pick(index, values):
    total = jnp.int32(0)
    for i, value in enumerate(values):
        if value:
            total = total + jnp.where(index == i, jnp.int32(value), 0)
    return total


def columns(chunk, side, rows):
    return pl.ds(pl.multiple_of((2 * chunk + side) * rows, rows), rows)


def pack_kernel(order, which, features, *refs):
    z, x = spot()
    outs, sems = refs[:-1], refs[-1]
    rows = outs[0].shape[1]
    copies = []
    for i, (k, out) in enumerate(zip(which, outs)):
        chunk = pick(z, [int(order[p][k]) for p in range(len(order))])
        copies.append(pltpu.make_async_copy(features.at[:, columns(chunk, 1 - x, rows)], out, sems.at[i]))
    for copy in copies:
        copy.start()
    for copy in copies:
        copy.wait()


def rotate_kernel(doc_ref, prev_ref, cot_ref, *outs):
    tokens = doc_ref.shape[1]

    def start(doc):
        last = jnp.max(doc, axis=1, keepdims=True)
        return tokens - jnp.sum((doc == last).astype(jnp.int32), axis=1, keepdims=True)

    places = lax.broadcasted_iota(jnp.int32, (1, tokens), 1)
    own = start(doc_ref[...])
    before = start(prev_ref[...])
    offsets = jnp.where(places >= own, places - own, places + tokens - before).astype(F32)
    half = HEAD // 2
    steps = lax.broadcasted_iota(jnp.int32, (half, 1), 0).astype(F32)
    frequency = jnp.exp(steps * (-math.log(ROPE_BASE) / half))
    angles = frequency * offsets
    cosine, sine = jnp.cos(angles), jnp.sin(angles)
    width = outs[0].shape[0]
    for part, out in enumerate(outs):
        turned = cot_ref[:, part * width : (part + 1) * width].astype(F32).T
        for head in range(width // HEAD):
            low = turned[head * HEAD : head * HEAD + half]
            high = turned[head * HEAD + half : (head + 1) * HEAD]
            out[head * HEAD : head * HEAD + half, :] = (low * cosine + high * sine).astype(BF16)
            out[head * HEAD + half : (head + 1) * HEAD, :] = (high * cosine - low * sine).astype(BF16)


def send_kernel(line, streams, chunks, own, peer, features, *refs):
    z, x = spot()
    pieces = dict(zip(chunks, refs))
    befores = refs[len(chunks) : len(refs) - len(streams)]
    outs = refs[len(refs) - len(streams) :]
    at = 0
    for (chunk, place, options, has_before), out in zip(streams, outs):
        rows = out.shape[1]
        before = befores[at] if has_before else None
        at += int(has_before)
        valid = pick(z, [int(d >= 0) for d in chunk])
        where = pick(z, place)
        mine = columns(pick(z, [max(d, 0) for d in chunk]), x, rows)

        @pl.when(valid == 0)
        def _():
            out[...] = jnp.zeros_like(out)

        for k in options:

            @pl.when((valid == 1) & (where == k))
            def _():
                total = dot(own[...], features[:, mine]) + dot(peer[...], pieces[k][...])
                if before is not None:
                    total = total + before[...].astype(F32)
                out[...] = total.astype(BF16)


def final_kernel(scale, part, own, peer, features, theirs, even, odd, first, second, *refs):
    new_first, new_second, keep, give = refs[-4:]
    z, x = spot()
    rows = theirs.shape[1]
    count, share, width = keep.shape
    total = dot(own[...], features[:, columns(z, x, rows)]) + dot(peer[...], theirs[...])
    total = total + even[...].astype(F32) + odd[...].astype(F32)
    grad = total.T * scale
    cols = slice(part * width, (part + 1) * width)
    fresh_first = 0.9 * first[:, cols] + 0.1 * grad
    fresh_second = 0.95 * second[:, cols] + 0.05 * grad * grad
    new_first[...] = fresh_first
    new_second[...] = fresh_second
    update = fresh_first / (jnp.sqrt(fresh_second) + 1e-08)
    ours, theirs = halves(update, count, share)
    keep[...] = ours.astype(keep.dtype)
    give[...] = theirs.astype(give.dtype)


def halves(value, count, share):
    pairs = value.reshape(count, 2, share, value.shape[-1])
    zero = lax.rem(lax.axis_index("rep"), 2) == 0
    return jnp.where(zero, pairs[:, 0], pairs[:, 1]), jnp.where(zero, pairs[:, 1], pairs[:, 0])


def split_kernel(params, stay, give):
    count, share, _ = stay.shape
    stay[...], give[...] = halves(params[...], count, share)


def partial_kernel(stay, came, mine, other):
    near = lax.div(lax.axis_index("rep"), 2) == 0
    held = stay[...] + came[...]
    mine[...] = jnp.where(near, held[0], held[1])
    other[...] = jnp.where(near, held[1], held[0])


def outer_kernel(part, reps, both, came, params_base, far_base, momentum_base, *refs):
    momentum, fresh = refs[-2:]
    near = lax.div(lax.axis_index("rep"), 2) == 0
    mean = (both[...].astype(F32) + came[...].astype(F32)) * (0.2 / reps)
    width = mean.shape[-1]
    cols = slice(part * width, (part + 1) * width)
    mine, far = params_base[:, cols], far_base[:, cols]
    fresh[0] = jnp.where(near, mine, far) - (0.7 * 1.9) * mean[0]
    fresh[1] = jnp.where(near, far, mine) - (0.7 * 1.9) * mean[1]
    momentum[...] = momentum_base[:, cols] + jnp.where(near, mean[0], mean[1])


def assemble_kernel(mine, theirs, *refs):
    out = refs[-1]
    zero = lax.rem(lax.axis_index("rep"), 2) == 0
    a, b = mine[...], theirs[...]
    both = jnp.stack([jnp.where(zero, a, b), jnp.where(zero, b, a)], axis=1)
    out[...] = both.reshape(out.shape)


def after(value, *others):
    return lax.optimization_barrier((value, *others))[0]


def call(kernel, ins, outs, scratch=(), into=None, places=None):
    into = into or []
    spaces = list(places or [pltpu.VMEM] * len(ins)) + [pl.ANY] * len(into)
    out_specs, shapes = [], []
    for shape, dtype, *block in outs:
        shapes.append(jax.ShapeDtypeStruct(shape, dtype))
        if block:
            out_specs.append(pl.BlockSpec((shape[0], block[1]), functools.partial(lambda part, i: (0, part), block[0])))
        else:
            out_specs.append(pl.BlockSpec(memory_space=pltpu.VMEM))
    return pl.pallas_call(
        kernel,
        grid=(1,),
        in_specs=[pl.BlockSpec(memory_space=space) for space in spaces],
        out_specs=out_specs,
        out_shape=shapes,
        scratch_shapes=list(scratch),
        input_output_aliases={len(ins) + i: i for i in range(len(into))},
        compiler_params=pltpu.CompilerParams(vmem_limit_bytes=VMEM_LIMIT),
    )(*ins, *into)


def local(fsdp, reps, activations, key_cotangent, doc_ids, replica_params, first_moment, second_moment, anchor, momentum):
    features, cotangent = activations[0], key_cotangent[0]
    params, first, second = replica_params[0], first_moment[0], second_moment[0]
    tokens, model = features.shape
    keys = cotangent.shape[1]
    rows = model // fsdp
    line = fsdp // 2
    share = anchor.shape[0]
    outer = reps // 2
    width = keys // HALVES
    order, place, sends = schedule(line)

    pair = [(f, f ^ 1) for f in range(fsdp)]
    cores = [(r, r ^ 1) for r in range(reps)]
    across = [(r, r ^ 2) for r in range(reps)]
    evens, odds = [], []
    for z in range(line - 1):
        for x in range(2):
            a, b = 2 * z + x, 2 * z + 2 + x
            (evens if z % 2 == 0 else odds).extend([(a, b), (b, a)])

    prev = lax.ppermute(doc_ids, "fsdp", [(f, f + 1) for f in range(fsdp - 1)])

    def packed(source, which):
        return call(
            functools.partial(pack_kernel, order, which), [source],
            [((tokens, rows), BF16)] * len(which),
            scratch=[pltpu.SemaphoreType.DMA((len(which),))], places=[pl.ANY],
        )

    pieces = [lax.ppermute(after(packed(features, [0])[0], prev), "fsdp", pair)]
    own = list(call(rotate_kernel, [doc_ids, prev, cotangent], [((width, tokens), BF16)] * HALVES))
    peer = [lax.ppermute(part, "fsdp", pair) for part in own]
    pieces += [lax.ppermute(piece, "fsdp", pair) for piece in packed(features, list(range(1, line)))]

    decay = 1.0 - 0.2 * 0.1
    groups = [[2 * q + c for q in range(outer)] for c in range(2)]
    block = ((outer, share, keys), F32)
    stay, give = call(split_kernel, [after(params, own[0])], [block] * 2)
    crossed = lax.ppermute(give, "rep", cores)
    ready = None
    if outer == 2:
        mine, ready = call(partial_kernel, [stay, crossed], [((share, keys), F32)] * 2)
        summed = mine + lax.ppermute(ready, "rep", across)
    else:
        summed = lax.psum_scatter(stay + crossed, "rep", scatter_dimension=0, axis_index_groups=groups, tiled=False)
    base = anchor - (decay / reps) * summed
    momentum_base = 0.9 * momentum + base
    params_base = anchor - 0.7 * (base + 0.9 * momentum_base)
    if outer == 2:
        far_base = lax.ppermute(params_base, "rep", across)
    else:
        bases = lax.all_gather(params_base, "rep", axis_index_groups=groups)

    came = [(None, None)] * HALVES
    for t, streams in enumerate(sends, 1):
        for h in range(HALVES):
            kept, chunks, before = [], set(), []
            for chunk, arrived in zip(streams, came[h][::-1]):
                options = sorted({int(place[z][d]) for z, d in enumerate(chunk) if d >= 0})
                if not options:
                    continue
                chunks.update(options)
                kept.append((chunk, [int(place[z][max(d, 0)]) for z, d in enumerate(chunk)], options, arrived is not None))
                if arrived is not None:
                    before.append(arrived)
            if outer == 2 and h == 0:
                if t == 2:
                    own[h] = after(own[h], ready)
                if t == 3:
                    own[h] = after(own[h], params_base)
            sent = call(
                functools.partial(send_kernel, line, kept, sorted(chunks)),
                [own[h], peer[h], features] + [pieces[k] for k in sorted(chunks)] + before,
                [((width, rows), BF16)] * len(kept),
            )
            even = lax.ppermute(sent[0], "fsdp", evens)
            odd = lax.ppermute(sent[1], "fsdp", odds) if len(sent) > 1 else None
            came[h] = (even, odd)

    scale = 1.0 / math.sqrt(tokens * fsdp)
    new_first = new_second = new_params = new_momentum = None
    momenta = []
    for h in range(HALVES):
        ins = [own[h], peer[h], features, pieces[line - 1], *came[h], first, second]
        new_first, new_second, keep, give = call(
            functools.partial(final_kernel, scale, h), ins,
            [((rows, keys), F32, h, width)] * 2 + [((outer, share, width), BF16)] * 2,
            into=[new_first, new_second] if h else None,
        )
        both = keep.astype(F32) + lax.ppermute(give, "rep", cores).astype(F32)
        if outer == 2:
            both = both.astype(BF16)
            ins = [both, lax.ppermute(both, "rep", across), params_base, far_base, momentum_base]
            new_momentum, fresh = call(
                functools.partial(outer_kernel, h, reps), ins,
                [((share, keys), F32, h, width), ((outer, share, width), F32)],
                into=[new_momentum] if h else None,
            )
        else:
            part = slice(h * width, (h + 1) * width)
            mean = (0.2 / reps) * lax.psum(both, "rep", axis_index_groups=groups)
            mine = lax.dynamic_index_in_dim(mean, lax.div(lax.axis_index("rep"), 2), 0, keepdims=False)
            momenta.append(momentum_base[:, part] + mine)
            fresh = bases[:, :, part] - (0.7 * 1.9) * mean
        ins = [fresh, lax.ppermute(fresh, "rep", cores)]
        (new_params,) = call(
            assemble_kernel, ins, [((rows, keys), F32, h, width)],
            into=[new_params] if h else None,
        )
    if outer != 2:
        new_momentum = jnp.concatenate(momenta, axis=1)
    return (new_first[None], new_second[None], new_momentum, new_params)


def solution(mesh):
    fsdp, reps = mesh.shape["fsdp"], mesh.shape["rep"]
    placed = (
        P("rep", "fsdp", None),
        P("rep", "fsdp", None),
        P("rep", "fsdp"),
        P("rep", "fsdp", None),
        P("rep", "fsdp", None),
        P("rep", "fsdp", None),
        P(("fsdp", "rep"), None),
        P(("fsdp", "rep"), None),
    )
    return jax.shard_map(
        functools.partial(local, fsdp, reps),
        mesh=mesh,
        in_specs=placed,
        out_specs=(
            P("rep", "fsdp", None),
            P("rep", "fsdp", None),
            P(("fsdp", "rep"), None),
            P("fsdp", None),
        ),
        check_vma=False,
    )
```

time: 115 us -> 92.9 us (0.81); the launches traced: 115 us -> 91.3 us
  Pallas kernels: 26.4 us -> 10.5 us
  between operations: 10.5 us -> 0.9 us
  local copies, waits for them, and re-layouts: 14.4 us -> 4.81 us
  waiting for transfers between devices: 24.9 us -> 34.4 us
  starting transfers between devices: 35.9 us -> 40.6 us
  other arithmetic: 2.37 us -> 0.19 us
    pallas_call x11 -> x17, Pallas kernels: 26.4 us -> 10.5 us  [call(): pl.pallas_call(kernel, grid=(1,), in_specs=[pl.BlockSpec(memory_space=spa...]
    ppermute x2, waiting for transfers between devices: 1.31 us -> 12.5 us  [local(): peer = [lax.ppermute(part, 'fsdp', pair) for part in own]]
    ppermute x14, waiting for transfers between devices: 23.6 us -> 13.7 us  [the longest x2 4.52 us: local(): lax.ppermute(both, 'rep', across)]
    ppermute x6, waiting for transfers between devices: 0.02 us -> 8.22 us  [local(): even = lax.ppermute(sent[0], 'fsdp', evens)]
    ppermute x6, starting transfers between devices: 13.4 us -> 18.6 us  [local(): even = lax.ppermute(sent[0], 'fsdp', evens)]
    unnamed x50 -> x18, local copies, waits for them, and re-layouts: 9.2 us -> 4.81 us
    dynamic_slice x2 -> x0, local copies, waits for them, and re-layouts: 3.42 us -> none  [the longest x1 2.57 us: packed(): lax.dynamic_slice_in_dim(features, row[slots['pack', k]] * rows, rows, 1)]
    ppermute x14, starting transfers between devices: 15.1 us -> 17.2 us  [the longest x1 4.84 us: local(): prev = lax.ppermute(doc_ids, 'fsdp', [(f, f + 1) for f in range(fsdp - 1)])]
  transfers between devices with their start and end apart: 26 -> 26, of which waited for: 8 -> 11; matrix products, arithmetic and copies ran while one was open for 3% -> 0% of each run, Pallas kernels for 22% -> 10%
where the time goes in v2:
time: 92.9 us; the launch traced here: 91.3 us
  starting transfers between devices  40.6 us (44%)
  waiting for transfers between devices  34.4 us (37%)
  Pallas kernels  10.5 us (11%)
  local copies, waits for them, and re-layouts  4.81 us (5%)
    ppermute x6, starting transfers between devices, local(): even = lax.ppermute(sent[0], 'fsdp', evens)  18.6 us
    ppermute x2, waiting for transfers between devices, local(): peer = [lax.ppermute(part, 'fsdp', pair) for part in own]  12.5 us
    pallas_call x17, Pallas kernels, call(): pl.pallas_call(kernel, grid=(1,), in_specs=[pl.BlockSpec(memory_space=spa...  10.5 us
    ppermute x6, waiting for transfers between devices, local(): even = lax.ppermute(sent[0], 'fsdp', evens)  8.22 us
    ppermute x1, starting transfers between devices, local(): prev = lax.ppermute(doc_ids, 'fsdp', [(f, f + 1) for f in range(fsdp - 1)])  4.84 us
    unnamed x18, local copies, waits for them, and re-layouts  4.81 us
    ppermute x2, waiting for transfers between devices, local(): lax.ppermute(both, 'rep', across)  4.52 us
    ppermute x3, starting transfers between devices, local(): lax.ppermute(piece, 'fsdp', pair)  4.04 us
  transfers between devices with their start and end apart: 26, of which 11 were waited for; matrix products, arithmetic and copies ran while one was open for 0% of the time, Pallas kernels for 10%

profile of v2, /device:TPU:0, one launch (start us, length us, event | category | flops | bytes accessed | tf_op | source)
XLA Modules:
  0.0 91.3 jit_solution(17919627425961468385)
XLA Ops:
  0.6 4.8 %collective-permute-start = (s32[1,384]{1,0:T(1,128)}, s32[1,384]{1,0:T(1,128)S(1)}, u32[]{:S(2)}, u32[]{:S(2)}) collective-permute-start(s32[1,384]{1,0:T(1,128)} %doc_ref.1), channel_id=1, source_target_pairs={{0,1},{1,2},{2,3},{3,4},{4,5},{5,6},{6,7},{8,9},{9,10},{10,11},{11... | collective-permute-start | bytes 4616 | tf_op jit(solution)/shard_map/ppermute | solution.py:234
  5.5 1.5 %collective-permute-done.prev_ref = s32[1,384]{1,0:T(1,128)S(1)} collective-permute-done((s32[1,384]{1,0:T(1,128)}, s32[1,384]{1,0:T(1,128)S(1)}, u32[]{:S(2)}, u32[]{:S(2)}) %collective-permute-start) | collective-permute-done | bytes 1568 | tf_op jit(solution)/shard_map/ppermute | solution.py:234
  7.0 1.0 %copy-done.5 = bf16[1,384,512]{2,1,0:T(8,128)(2,1)S(1)} copy-done((bf16[1,384,512]{2,1,0:T(8,128)(2,1)S(1)}, bf16[1,384,512]{2,1,0:T(8,128)(2,1)}, u32[]{:S(2)}) %copy-start.5) | copy-done | bytes 393240
  8.0 0.7 copy-done.6
  8.7 0.8 shard_map.111
  9.4 1.2 %copy-done.4 = f32[1,512,512]{2,1,0:T(8,128)S(1)} copy-done((f32[1,512,512]{2,1,0:T(8,128)S(1)}, f32[1,512,512]{2,1,0:T(8,128)}, u32[]{:S(2)}) %copy-start.4) | copy-done | bytes 1048600
  10.9 1.9 %copy-done = bf16[1,384,4096]{2,1,0:T(8,128)(2,1)S(1)} copy-done((bf16[1,384,4096]{2,1,0:T(8,128)(2,1)S(1)}, bf16[1,384,4096]{2,1,0:T(8,128)(2,1)}, u32[]{:S(2)}) %copy-start) | copy-done | bytes 3145752
  12.8 2.3 %collective-permute-start.5 = (bf16[384,512]{1,0:T(8,128)(2,1)S(1)}, bf16[384,512]{1,0:T(8,128)(2,1)S(1)}, u32[]{:S(2)}, u32[]{:S(2)}) collective-permute-start(bf16[384,512]{1,0:T(8,128)(2,1)S(1)} %shard_map.113), channel_id=1, source_target_pairs={{0,1},{1,0},{2,3},{3,2},{4,5},{5,4},{6,7},{7,6},{8,9},{9,8},{10,11... | collective-permute-start | bytes 1179656 | tf_op jit(solution)/shard_map/ppermute | solution.py:243
  15.2 1.9 %collective-permute-start.13 = (bf16[256,384]{1,0:T(8,128)(2,1)S(1)}, bf16[256,384]{1,0:T(8,128)(2,1)S(1)}, u32[]{:S(2)}, u32[]{:S(2)}) collective-permute-start(bf16[256,384]{1,0:T(8,128)(2,1)S(1)} %get-tuple-element.53.own), channel_id=1, source_target_pairs={{0,1},{1,0},{2,3},{3,2},{4,5},{5,4},{6,7},{7,6},{8,9},{9,8},{10,11... | collective-permute-start | bytes 589832 | tf_op jit(solution)/shard_map/ppermute | solution.py:245
  17.4 11.9 %collective-permute-done.1.peer = bf16[256,384]{1,0:T(8,128)(2,1)S(1)} collective-permute-done((bf16[256,384]{1,0:T(8,128)(2,1)S(1)}, bf16[256,384]{1,0:T(8,128)(2,1)S(1)}, u32[]{:S(2)}, u32[]{:S(2)}) %collective-permute-start.1) | collective-permute-done | bytes 196640 | tf_op jit(solution)/shard_map/ppermute | solution.py:245
  29.3 1.9 %collective-permute-start.4 = (bf16[384,512]{1,0:T(8,128)(2,1)S(1)}, bf16[384,512]{1,0:T(8,128)(2,1)S(1)}, u32[]{:S(2)}, u32[]{:S(2)}) collective-permute-start(bf16[384,512]{1,0:T(8,128)(2,1)S(1)} %get-tuple-element.40), channel_id=1, source_target_pairs={{0,1},{1,0},{2,3},{3,2},{4,5},{5,4},{6,7},{7,6},{8,9},{9,8},{10,11... | collective-permute-start | bytes 1179656 | tf_op jit(solution)/shard_map/ppermute | solution.py:246
  31.3 0.4 shard_map.114
  31.7 1.2 %collective-permute-start.6 = (bf16[256,512]{1,0:T(8,128)(2,1)S(1)}, bf16[256,512]{1,0:T(8,128)(2,1)S(1)}, u32[]{:S(2)}, u32[]{:S(2)}) collective-permute-start(bf16[256,512]{1,0:T(8,128)(2,1)S(1)} %shard_map.114), channel_id=1, source_target_pairs={{0,2},{2,0},{1,3},{3,1},{4,6},{6,4},{5,7},{7,5},{8,10},{10,8},{9,1... | collective-permute-start | bytes 786440 | tf_op jit(solution)/shard_map/ppermute | solution.py:289
  32.9 0.6 collective-permute-done.13.peer
  33.5 0.4 shard_map.119
  34.0 2.6 %collective-permute-start.14 = (bf16[256,512]{1,0:T(8,128)(2,1)S(1)}, bf16[256,512]{1,0:T(8,128)(2,1)S(1)}, u32[]{:S(2)}, u32[]{:S(2)}) collective-permute-start(bf16[256,512]{1,0:T(8,128)(2,1)S(1)} %shard_map.119), channel_id=1, source_target_pairs={{0,2},{2,0},{1,3},{3,1},{4,6},{6,4},{5,7},{7,5},{8,10},{10,8},{9,1... | collective-permute-start | bytes 786440 | tf_op jit(solution)/shard_map/ppermute | solution.py:289
  36.6 1.6 %collective-permute-start.12 = (f32[128,512]{1,0:T(8,128)S(1)}, f32[128,512]{1,0:T(8,128)S(1)}, u32[]{:S(2)}, u32[]{:S(2)}) collective-permute-start(f32[128,512]{1,0:T(8,128)S(1)} %get-tuple-element.50), channel_id=1, source_target_pairs={{0,16},{8,24},{16,0},{24,8},{1,17},{9,25},{17,1},{25,9},{2,18},{10... | collective-permute-start | bytes 786440 | tf_op jit(solution)/shard_map/ppermute | solution.py:256
  38.2 3.8 %collective-permute-done.3.refs_1_.refs_0_ = bf16[384,512]{1,0:T(8,128)(2,1)S(1)} collective-permute-done((bf16[384,512]{1,0:T(8,128)(2,1)S(1)}, bf16[384,512]{1,0:T(8,128)(2,1)S(1)}, u32[]{:S(2)}, u32[]{:S(2)}) %collective-permute-start.3) | collective-permute-done | bytes 393248 | tf_op jit(solution)/shard_map/ppermute | solution.py:246
  42.0 1.9 %collective-permute-start.2 = (bf16[384,512]{1,0:T(8,128)(2,1)S(1)}, bf16[384,512]{1,0:T(8,128)(2,1)S(1)}, u32[]{:S(2)}, u32[]{:S(2)}) collective-permute-start(bf16[384,512]{1,0:T(8,128)(2,1)S(1)} %get-tuple-element.38), channel_id=1, source_target_pairs={{0,1},{1,0},{2,3},{3,2},{4,5},{5,4},{6,7},{7,6},{8,9},{9,8},{10,11... | collective-permute-start | bytes 1179656 | tf_op jit(solution)/shard_map/ppermute | solution.py:246
  43.9 0.5 shard_map.115
  44.4 0.8 collective-permute-start.7
  45.2 4.4 %collective-permute-start.8 = (bf16[256,512]{1,0:T(8,128)(2,1)S(1)}, bf16[256,512]{1,0:T(8,128)(2,1)S(1)}, u32[]{:S(2)}, u32[]{:S(2)}) collective-permute-start(bf16[256,512]{1,0:T(8,128)(2,1)S(1)} %get-tuple-element.43), channel_id=1, source_target_pairs={{0,2},{2,0},{1,3},{3,1},{4,6},{6,4},{5,7},{7,5},{8,10},{10,8},{9,1... | collective-permute-start | bytes 786440 | tf_op jit(solution)/shard_map/ppermute | solution.py:289
  49.7 0.5 shard_map.120
  50.1 0.3 collective-permute-done.4.refs_1_
  50.4 0.7 collective-permute-start.15
  51.1 5.8 %collective-permute-start.16 = (bf16[256,512]{1,0:T(8,128)(2,1)S(1)}, bf16[256,512]{1,0:T(8,128)(2,1)S(1)}, u32[]{:S(2)}, u32[]{:S(2)}) collective-permute-start(bf16[256,512]{1,0:T(8,128)(2,1)S(1)} %get-tuple-element.55), channel_id=1, source_target_pairs={{0,2},{2,0},{1,3},{3,1},{4,6},{6,4},{5,7},{7,5},{8,10},{10,8},{9,1... | collective-permute-start | bytes 786440 | tf_op jit(solution)/shard_map/ppermute | solution.py:289
  57.0 5.4 %collective-permute-done.16.refs_3_ = bf16[256,512]{1,0:T(8,128)(2,1)S(1)} collective-permute-done((bf16[256,512]{1,0:T(8,128)(2,1)S(1)}, bf16[256,512]{1,0:T(8,128)(2,1)S(1)}, u32[]{:S(2)}, u32[]{:S(2)}) %collective-permute-start.16) | collective-permute-done | bytes 262176 | tf_op jit(solution)/shard_map/ppermute | solution.py:289
  62.4 0.5 shard_map.121
  62.9 2.2 %collective-permute-start.17 = (bf16[256,512]{1,0:T(8,128)(2,1)S(1)}, bf16[256,512]{1,0:T(8,128)(2,1)S(1)}, u32[]{:S(2)}, u32[]{:S(2)}) collective-permute-start(bf16[256,512]{1,0:T(8,128)(2,1)S(1)} %get-tuple-element.56), channel_id=1, source_target_pairs={{0,2},{2,0},{1,3},{3,1},{4,6},{6,4},{5,7},{7,5},{8,10},{10,8},{9,1... | collective-permute-start | bytes 786440 | tf_op jit(solution)/shard_map/ppermute | solution.py:289
  65.1 0.7 collective-permute-start.18
  65.8 0.5 shard_map.116
  66.3 2.3 %collective-permute-start.9 = (bf16[256,512]{1,0:T(8,128)(2,1)S(1)}, bf16[256,512]{1,0:T(8,128)(2,1)S(1)}, u32[]{:S(2)}, u32[]{:S(2)}) collective-permute-start(bf16[256,512]{1,0:T(8,128)(2,1)S(1)} %get-tuple-element.44), channel_id=1, source_target_pairs={{0,2},{2,0},{1,3},{3,1},{4,6},{6,4},{5,7},{7,5},{8,10},{10,8},{9,1... | collective-permute-start | bytes 786440 | tf_op jit(solution)/shard_map/ppermute | solution.py:289
  68.6 0.7 collective-permute-start.10
  69.3 2.8 %collective-permute-done.17.even = bf16[256,512]{1,0:T(8,128)(2,1)S(1)} collective-permute-done((bf16[256,512]{1,0:T(8,128)(2,1)S(1)}, bf16[256,512]{1,0:T(8,128)(2,1)S(1)}, u32[]{:S(2)}, u32[]{:S(2)}) %collective-permute-start.17) | collective-permute-done | bytes 262176 | tf_op jit(solution)/shard_map/ppermute | solution.py:289
  72.1 1.8 %shard_map.122 = (f32[512,512]{1,0:T(8,128)}, f32[512,512]{1,0:T(8,128)}, bf16[2,128,256]{2,1,0:T(8,128)(2,1)S(1)}, bf16[2,128,256]{2,1,0:T(8,128)(2,1)S(1)}) custom-call(bf16[256,384]{1,0:T(8,128)(2,1)S(1)} %get-tuple-element.53.own, bf16[256,384]{1,0:T(8,128)(2,1)S(1)} %collective-permute-done.13.peer, bf16[384,4096]{1,0:T(8,128)(2,1)S(1)} %bitcast.15, ...), custom_call_target="tpu_custom_call" | custom-call | tf_op jit(solution)/shard_map/pallas_call | solution.py:201
  73.9 1.5 %collective-permute-start.21 = (f32[128,512]{1,0:T(8,128)S(1)}, f32[128,512]{1,0:T(8,128)S(1)}, u32[]{:S(2)}, u32[]{:S(2)}) collective-permute-start(f32[128,512]{1,0:T(8,128)S(1)} %get-tuple-element.71.params_base), channel_id=1, source_target_pairs={{0,16},{8,24},{16,0},{24,8},{1,17},{9,25},{17,1},{25,9},{2,18},{10... | collective-permute-start | bytes 786440 | tf_op jit(solution)/shard_map/ppermute | solution.py:263
  75.4 1.8 %shard_map.123 = (f32[512,512]{1,0:T(8,128)}, f32[512,512]{1,0:T(8,128)}, bf16[2,128,256]{2,1,0:T(8,128)(2,1)S(1)}, bf16[2,128,256]{2,1,0:T(8,128)(2,1)S(1)}) custom-call(bf16[256,384]{1,0:T(8,128)(2,1)S(1)} %get-tuple-element.37.own, bf16[256,384]{1,0:T(8,128)(2,1)S(1)} %collective-permute-done.1.peer, ...), custom_call_target="tpu_custom_call", output_to_operand_aliasing={{0}: (8, {}), {1}: (9, {})} | custom-call | tf_op jit(solution)/shard_map/pallas_call | solution.py:201
  77.2 0.2 collective-permute-start.19
  77.5 1.2 %collective-permute-start.23 = (bf16[2,128,256]{2,1,0:T(8,128)(2,1)S(1)}, bf16[2,128,256]{2,1,0:T(8,128)(2,1)S(1)}, u32[]{:S(2)}, u32[]{:S(2)}) collective-permute-start(bf16[2,128,256]{2,1,0:T(8,128)(2,1)S(1)} %add_convert_fusion.both), channel_id=1, source_target_pairs={{0,16},{8,24},{16,0},{24,8},{1,17},{9,25},{17,1},{25,9},{2,18},{10... | collective-permute-start | bytes 393224 | tf_op jit(solution)/shard_map/ppermute | solution.py:306
  78.7 1.3 %collective-permute-start.20 = (bf16[2,128,256]{2,1,0:T(8,128)(2,1)S(1)}, bf16[2,128,256]{2,1,0:T(8,128)(2,1)S(1)}, u32[]{:S(2)}, u32[]{:S(2)}) collective-permute-start(bf16[2,128,256]{2,1,0:T(8,128)(2,1)S(1)} %add_convert_fusion.1.both), channel_id=1, source_target_pairs={{0,16},{8,24},{16,0},{24,8},{1,17},{9,25},{17,1},{25,9},{2,18},{10... | collective-permute-start | bytes 393224 | tf_op jit(solution)/shard_map/ppermute | solution.py:306
  80.0 3.0 %collective-permute-done.21.far_base = f32[128,512]{1,0:T(8,128)S(1)} collective-permute-done((f32[128,512]{1,0:T(8,128)S(1)}, f32[128,512]{1,0:T(8,128)S(1)}, u32[]{:S(2)}, u32[]{:S(2)}) %collective-permute-start.21) | collective-permute-done | bytes 262176 | tf_op jit(solution)/shard_map/ppermute | solution.py:263
  83.0 2.8 %collective-permute-done.23.came = bf16[2,128,256]{2,1,0:T(8,128)(2,1)S(1)} collective-permute-done((bf16[2,128,256]{2,1,0:T(8,128)(2,1)S(1)}, bf16[2,128,256]{2,1,0:T(8,128)(2,1)S(1)}, u32[]{:S(2)}, u32[]{:S(2)}) %collective-permute-start.23) | collective-permute-done | bytes 131104 | tf_op jit(solution)/shard_map/ppermute | solution.py:306
  85.8 0.7 shard_map.124
  86.5 1.7 %collective-permute-done.20.came = bf16[2,128,256]{2,1,0:T(8,128)(2,1)S(1)} collective-permute-done((bf16[2,128,256]{2,1,0:T(8,128)(2,1)S(1)}, bf16[2,128,256]{2,1,0:T(8,128)(2,1)S(1)}, u32[]{:S(2)}, u32[]{:S(2)}) %collective-permute-start.20) | collective-permute-done | bytes 131104 | tf_op jit(solution)/shard_map/ppermute | solution.py:306
  88.2 0.7 shard_map.125
  88.9 0.8 shard_map.126.refs_0_
  89.8 0.7 collective-permute-done.24.theirs
  90.5 0.8 shard_map.127
  (42 shorter events, 0.9 us)
Async XLA Ops:
  0.6 6.3 %collective-permute-start = (s32[1,384]{1,0:T(1,128)}, s32[1,384]{1,0:T(1,128)S(1)}, u32[]{:S(2)}, u32[]{:S(2)}) collective-permute-start(s32[1,384]{1,0:T(1,128)} %doc_ref.1), channel_id=1, source_target_pairs={{0,1},{1,2},{2,3},{3,4},{4,5},{5,6},{6,7},{8,9},{9,10},{10,11},{11... | collective-permute-start | bytes 4616 | tf_op jit(solution)/shard_map/ppermute | solution.py:234
  7.0 1.0 %copy-start.5 = (bf16[1,384,512]{2,1,0:T(8,128)(2,1)S(1)}, bf16[1,384,512]{2,1,0:T(8,128)(2,1)}, u32[]{:S(2)}) copy-start(bf16[1,384,512]{2,1,0:T(8,128)(2,1)} %param.9) | copy-start | bytes 1179652
  8.0 0.7 copy-start.6
  9.4 1.2 %copy-start.4 = (f32[1,512,512]{2,1,0:T(8,128)S(1)}, f32[1,512,512]{2,1,0:T(8,128)}, u32[]{:S(2)}) copy-start(f32[1,512,512]{2,1,0:T(8,128)} %param.11) | copy-start | bytes 3145732
  10.8 25.8 %collective-permute-start.11 = (f32[2,128,512]{2,1,0:T(8,128)S(1)}, f32[2,128,512]{2,1,0:T(8,128)S(1)}, u32[]{:S(2)}, u32[]{:S(2)}) collective-permute-start(f32[2,128,512]{2,1,0:T(8,128)S(1)} %get-tuple-element.49), channel_id=1, source_target_pairs={{0,8},{8,0},{16,24},{24,16},{1,9},{9,1},{17,25},{25,17},{2,10},{10... | collective-permute-start | bytes 1572872 | tf_op jit(solution)/shard_map/ppermute | solution.py:252
  10.8 1.9 %copy-start = (bf16[1,384,4096]{2,1,0:T(8,128)(2,1)S(1)}, bf16[1,384,4096]{2,1,0:T(8,128)(2,1)}, u32[]{:S(2)}) copy-start(bf16[1,384,4096]{2,1,0:T(8,128)(2,1)} %param.8) | copy-start | bytes 9437188
  12.7 18.5 %copy-start.1 = (bf16[1,384,4096]{2,1,0:T(8,128)(2,1)S(1)}, bf16[1,384,4096]{2,1,0:T(8,128)(2,1)}, u32[]{:S(2)}) copy-start(bf16[1,384,4096]{2,1,0:T(8,128)(2,1)} %param.8) | copy-start | bytes 9437188
  12.8 18.5 %collective-permute-start.5 = (bf16[384,512]{1,0:T(8,128)(2,1)S(1)}, bf16[384,512]{1,0:T(8,128)(2,1)S(1)}, u32[]{:S(2)}, u32[]{:S(2)}) collective-permute-start(bf16[384,512]{1,0:T(8,128)(2,1)S(1)} %shard_map.113), channel_id=1, source_target_pairs={{0,1},{1,0},{2,3},{3,2},{4,5},{5,4},{6,7},{7,6},{8,9},{9,8},{10,11... | collective-permute-start | bytes 1179656 | tf_op jit(solution)/shard_map/ppermute | solution.py:243
  15.1 14.2 %collective-permute-start.1 = (bf16[256,384]{1,0:T(8,128)(2,1)S(1)}, bf16[256,384]{1,0:T(8,128)(2,1)S(1)}, u32[]{:S(2)}, u32[]{:S(2)}) collective-permute-start(bf16[256,384]{1,0:T(8,128)(2,1)S(1)} %get-tuple-element.37.own), channel_id=1, source_target_pairs={{0,1},{1,0},{2,3},{3,2},{4,5},{5,4},{6,7},{7,6},{8,9},{9,8},{10,11... | collective-permute-start | bytes 589832 | tf_op jit(solution)/shard_map/ppermute | solution.py:245
  15.2 18.3 %collective-permute-start.13 = (bf16[256,384]{1,0:T(8,128)(2,1)S(1)}, bf16[256,384]{1,0:T(8,128)(2,1)S(1)}, u32[]{:S(2)}, u32[]{:S(2)}) collective-permute-start(bf16[256,384]{1,0:T(8,128)(2,1)S(1)} %get-tuple-element.53.own), channel_id=1, source_target_pairs={{0,1},{1,0},{2,3},{3,2},{4,5},{5,4},{6,7},{7,6},{8,9},{9,8},{10,11... | collective-permute-start | bytes 589832 | tf_op jit(solution)/shard_map/ppermute | solution.py:245
  17.3 24.7 %collective-permute-start.3 = (bf16[384,512]{1,0:T(8,128)(2,1)S(1)}, bf16[384,512]{1,0:T(8,128)(2,1)S(1)}, u32[]{:S(2)}, u32[]{:S(2)}) collective-permute-start(bf16[384,512]{1,0:T(8,128)(2,1)S(1)} %get-tuple-element.39), channel_id=1, source_target_pairs={{0,1},{1,0},{2,3},{3,2},{4,5},{5,4},{6,7},{7,6},{8,9},{9,8},{10,11... | collective-permute-start | bytes 1179656 | tf_op jit(solution)/shard_map/ppermute | solution.py:246
  29.3 21.1 %collective-permute-start.4 = (bf16[384,512]{1,0:T(8,128)(2,1)S(1)}, bf16[384,512]{1,0:T(8,128)(2,1)S(1)}, u32[]{:S(2)}, u32[]{:S(2)}) collective-permute-start(bf16[384,512]{1,0:T(8,128)(2,1)S(1)} %get-tuple-element.40), channel_id=1, source_target_pairs={{0,1},{1,0},{2,3},{3,2},{4,5},{5,4},{6,7},{7,6},{8,9},{9,8},{10,11... | collective-permute-start | bytes 1179656 | tf_op jit(solution)/shard_map/ppermute | solution.py:246
  31.7 12.2 %collective-permute-start.6 = (bf16[256,512]{1,0:T(8,128)(2,1)S(1)}, bf16[256,512]{1,0:T(8,128)(2,1)S(1)}, u32[]{:S(2)}, u32[]{:S(2)}) collective-permute-start(bf16[256,512]{1,0:T(8,128)(2,1)S(1)} %shard_map.114), channel_id=1, source_target_pairs={{0,2},{2,0},{1,3},{3,1},{4,6},{6,4},{5,7},{7,5},{8,10},{10,8},{9,1... | collective-permute-start | bytes 786440 | tf_op jit(solution)/shard_map/ppermute | solution.py:289
  34.0 11.2 %collective-permute-start.14 = (bf16[256,512]{1,0:T(8,128)(2,1)S(1)}, bf16[256,512]{1,0:T(8,128)(2,1)S(1)}, u32[]{:S(2)}, u32[]{:S(2)}) collective-permute-start(bf16[256,512]{1,0:T(8,128)(2,1)S(1)} %shard_map.119), channel_id=1, source_target_pairs={{0,2},{2,0},{1,3},{3,1},{4,6},{6,4},{5,7},{7,5},{8,10},{10,8},{9,1... | collective-permute-start | bytes 786440 | tf_op jit(solution)/shard_map/ppermute | solution.py:289
  36.6 14.4 %collective-permute-start.12 = (f32[128,512]{1,0:T(8,128)S(1)}, f32[128,512]{1,0:T(8,128)S(1)}, u32[]{:S(2)}, u32[]{:S(2)}) collective-permute-start(f32[128,512]{1,0:T(8,128)S(1)} %get-tuple-element.50), channel_id=1, source_target_pairs={{0,16},{8,24},{16,0},{24,8},{1,17},{9,25},{17,1},{25,9},{2,18},{10... | collective-permute-start | bytes 786440 | tf_op jit(solution)/shard_map/ppermute | solution.py:256
  42.0 27.3 %collective-permute-start.2 = (bf16[384,512]{1,0:T(8,128)(2,1)S(1)}, bf16[384,512]{1,0:T(8,128)(2,1)S(1)}, u32[]{:S(2)}, u32[]{:S(2)}) collective-permute-start(bf16[384,512]{1,0:T(8,128)(2,1)S(1)} %get-tuple-element.38), channel_id=1, source_target_pairs={{0,1},{1,0},{2,3},{3,2},{4,5},{5,4},{6,7},{7,6},{8,9},{9,8},{10,11... | collective-permute-start | bytes 1179656 | tf_op jit(solution)/shard_map/ppermute | solution.py:246
  44.4 12.5 %copy-start.7 = (f32[128,512]{1,0:T(8,128)S(1)}, f32[128,512]{1,0:T(8,128)}, u32[]{:S(2)}) copy-start(f32[128,512]{1,0:T(8,128)} %param.15) | copy-start | bytes 786436
  44.4 12.5 %copy-start.8 = (f32[128,512]{1,0:T(8,128)S(1)}, f32[128,512]{1,0:T(8,128)}, u32[]{:S(2)}) copy-start(f32[128,512]{1,0:T(8,128)} %param.14) | copy-start | bytes 786436
  44.4 21.4 %collective-permute-start.7 = (bf16[256,512]{1,0:T(8,128)(2,1)S(1)}, bf16[256,512]{1,0:T(8,128)(2,1)S(1)}, u32[]{:S(2)}, u32[]{:S(2)}) collective-permute-start(bf16[256,512]{1,0:T(8,128)(2,1)S(1)} %get-tuple-element.42), channel_id=1, source_target_pairs={{2,4},{4,2},{3,5},{5,3},{10,12},{12,10},{11,13},{13,11},{18,20},{2... | collective-permute-start | bytes 786440 | tf_op jit(solution)/shard_map/ppermute | solution.py:290
  45.2 20.6 %collective-permute-start.8 = (bf16[256,512]{1,0:T(8,128)(2,1)S(1)}, bf16[256,512]{1,0:T(8,128)(2,1)S(1)}, u32[]{:S(2)}, u32[]{:S(2)}) collective-permute-start(bf16[256,512]{1,0:T(8,128)(2,1)S(1)} %get-tuple-element.43), channel_id=1, source_target_pairs={{0,2},{2,0},{1,3},{3,1},{4,6},{6,4},{5,7},{7,5},{8,10},{10,8},{9,1... | collective-permute-start | bytes 786440 | tf_op jit(solution)/shard_map/ppermute | solution.py:289
  50.4 6.6 %collective-permute-start.15 = (bf16[256,512]{1,0:T(8,128)(2,1)S(1)}, bf16[256,512]{1,0:T(8,128)(2,1)S(1)}, u32[]{:S(2)}, u32[]{:S(2)}) collective-permute-start(bf16[256,512]{1,0:T(8,128)(2,1)S(1)} %get-tuple-element.54), channel_id=1, source_target_pairs={{2,4},{4,2},{3,5},{5,3},{10,12},{12,10},{11,13},{13,11},{18,20},{2... | collective-permute-start | bytes 786440 | tf_op jit(solution)/shard_map/ppermute | solution.py:290
  51.1 11.3 %collective-permute-start.16 = (bf16[256,512]{1,0:T(8,128)(2,1)S(1)}, bf16[256,512]{1,0:T(8,128)(2,1)S(1)}, u32[]{:S(2)}, u32[]{:S(2)}) collective-permute-start(bf16[256,512]{1,0:T(8,128)(2,1)S(1)} %get-tuple-element.55), channel_id=1, source_target_pairs={{0,2},{2,0},{1,3},{3,1},{4,6},{6,4},{5,7},{7,5},{8,10},{10,8},{9,1... | collective-permute-start | bytes 786440 | tf_op jit(solution)/shard_map/ppermute | solution.py:289
  62.8 9.3 %copy-start.2 = (f32[1,512,512]{2,1,0:T(8,128)S(1)}, f32[1,512,512]{2,1,0:T(8,128)}, u32[]{:S(2)}) copy-start(f32[1,512,512]{2,1,0:T(8,128)} %param.12) | copy-start | bytes 3145732
  62.8 9.3 %copy-start.3 = (f32[1,512,512]{2,1,0:T(8,128)S(1)}, f32[1,512,512]{2,1,0:T(8,128)}, u32[]{:S(2)}) copy-start(f32[1,512,512]{2,1,0:T(8,128)} %param.13) | copy-start | bytes 3145732
  62.9 9.2 %collective-permute-start.17 = (bf16[256,512]{1,0:T(8,128)(2,1)S(1)}, bf16[256,512]{1,0:T(8,128)(2,1)S(1)}, u32[]{:S(2)}, u32[]{:S(2)}) collective-permute-start(bf16[256,512]{1,0:T(8,128)(2,1)S(1)} %get-tuple-element.56), channel_id=1, source_target_pairs={{0,2},{2,0},{1,3},{3,1},{4,6},{6,4},{5,7},{7,5},{8,10},{10,8},{9,1... | collective-permute-start | bytes 786440 | tf_op jit(solution)/shard_map/ppermute | solution.py:289
  65.1 7.0 %collective-permute-start.18 = (bf16[256,512]{1,0:T(8,128)(2,1)S(1)}, bf16[256,512]{1,0:T(8,128)(2,1)S(1)}, u32[]{:S(2)}, u32[]{:S(2)}) collective-permute-start(bf16[256,512]{1,0:T(8,128)(2,1)S(1)} %get-tuple-element.57), channel_id=1, source_target_pairs={{2,4},{4,2},{3,5},{5,3},{10,12},{12,10},{11,13},{13,11},{18,20},{2... | collective-permute-start | bytes 786440 | tf_op jit(solution)/shard_map/ppermute | solution.py:290
  66.3 9.1 %collective-permute-start.9 = (bf16[256,512]{1,0:T(8,128)(2,1)S(1)}, bf16[256,512]{1,0:T(8,128)(2,1)S(1)}, u32[]{:S(2)}, u32[]{:S(2)}) collective-permute-start(bf16[256,512]{1,0:T(8,128)(2,1)S(1)} %get-tuple-element.44), channel_id=1, source_target_pairs={{0,2},{2,0},{1,3},{3,1},{4,6},{6,4},{5,7},{7,5},{8,10},{10,8},{9,1... | collective-permute-start | bytes 786440 | tf_op jit(solution)/shard_map/ppermute | solution.py:289
  68.6 6.8 %collective-permute-start.10 = (bf16[256,512]{1,0:T(8,128)(2,1)S(1)}, bf16[256,512]{1,0:T(8,128)(2,1)S(1)}, u32[]{:S(2)}, u32[]{:S(2)}) collective-permute-start(bf16[256,512]{1,0:T(8,128)(2,1)S(1)} %get-tuple-element.45), channel_id=1, source_target_pairs={{2,4},{4,2},{3,5},{5,3},{10,12},{12,10},{11,13},{13,11},{18,20},{2... | collective-permute-start | bytes 786440 | tf_op jit(solution)/shard_map/ppermute | solution.py:290
  73.9 3.5 %collective-permute-start.22 = (bf16[2,128,256]{2,1,0:T(8,128)(2,1)S(1)}, bf16[2,128,256]{2,1,0:T(8,128)(2,1)S(1)}, u32[]{:S(2)}, u32[]{:S(2)}) collective-permute-start(bf16[2,128,256]{2,1,0:T(8,128)(2,1)S(1)} %get-tuple-element.65), channel_id=1, source_target_pairs={{0,8},{8,0},{16,24},{24,16},{1,9},{9,1},{17,25},{25,17},{2,10},{10... | collective-permute-start | bytes 393224 | tf_op jit(solution)/shard_map/ppermute | solution.py:303
  73.9 9.1 %collective-permute-start.21 = (f32[128,512]{1,0:T(8,128)S(1)}, f32[128,512]{1,0:T(8,128)S(1)}, u32[]{:S(2)}, u32[]{:S(2)}) collective-permute-start(f32[128,512]{1,0:T(8,128)S(1)} %get-tuple-element.71.params_base), channel_id=1, source_target_pairs={{0,16},{8,24},{16,0},{24,8},{1,17},{9,25},{17,1},{25,9},{2,18},{10... | collective-permute-start | bytes 786440 | tf_op jit(solution)/shard_map/ppermute | solution.py:263
  77.2 1.5 %collective-permute-start.19 = (bf16[2,128,256]{2,1,0:T(8,128)(2,1)S(1)}, bf16[2,128,256]{2,1,0:T(8,128)(2,1)S(1)}, u32[]{:S(2)}, u32[]{:S(2)}) collective-permute-start(bf16[2,128,256]{2,1,0:T(8,128)(2,1)S(1)} %get-tuple-element.63), channel_id=1, source_target_pairs={{0,8},{8,0},{16,24},{24,16},{1,9},{9,1},{17,25},{25,17},{2,10},{10... | collective-permute-start | bytes 393224 | tf_op jit(solution)/shard_map/ppermute | solution.py:303
  77.5 8.3 %collective-permute-start.23 = (bf16[2,128,256]{2,1,0:T(8,128)(2,1)S(1)}, bf16[2,128,256]{2,1,0:T(8,128)(2,1)S(1)}, u32[]{:S(2)}, u32[]{:S(2)}) collective-permute-start(bf16[2,128,256]{2,1,0:T(8,128)(2,1)S(1)} %add_convert_fusion.both), channel_id=1, source_target_pairs={{0,16},{8,24},{16,0},{24,8},{1,17},{9,25},{17,1},{25,9},{2,18},{10... | collective-permute-start | bytes 393224 | tf_op jit(solution)/shard_map/ppermute | solution.py:306
  78.7 9.5 %collective-permute-start.20 = (bf16[2,128,256]{2,1,0:T(8,128)(2,1)S(1)}, bf16[2,128,256]{2,1,0:T(8,128)(2,1)S(1)}, u32[]{:S(2)}, u32[]{:S(2)}) collective-permute-start(bf16[2,128,256]{2,1,0:T(8,128)(2,1)S(1)} %add_convert_fusion.1.both), channel_id=1, source_target_pairs={{0,16},{8,24},{16,0},{24,8},{1,17},{9,25},{17,1},{25,9},{2,18},{10... | collective-permute-start | bytes 393224 | tf_op jit(solution)/shard_map/ppermute | solution.py:306
  86.5 2.4 %collective-permute-start.25 = (f32[2,128,256]{2,1,0:T(8,128)S(1)}, f32[2,128,256]{2,1,0:T(8,128)S(1)}, u32[]{:S(2)}, u32[]{:S(2)}) collective-permute-start(f32[2,128,256]{2,1,0:T(8,128)S(1)} %get-tuple-element.69.mine), channel_id=1, source_target_pairs={{0,8},{8,0},{16,24},{24,16},{1,9},{9,1},{17,25},{25,17},{2,10},{10... | collective-permute-start | bytes 786440 | tf_op jit(solution)/shard_map/ppermute | solution.py:318
  88.9 1.5 %collective-permute-start.24 = (f32[2,128,256]{2,1,0:T(8,128)S(1)}, f32[2,128,256]{2,1,0:T(8,128)S(1)}, u32[]{:S(2)}, u32[]{:S(2)}) collective-permute-start(f32[2,128,256]{2,1,0:T(8,128)S(1)} %get-tuple-element.68.mine), channel_id=1, source_target_pairs={{0,8},{8,0},{16,24},{24,16},{1,9},{9,1},{17,25},{25,17},{2,10},{10... | collective-permute-start | bytes 786440 | tf_op jit(solution)/shard_map/ppermute | solution.py:318

commit v3 on v2

--- a/solution.py
+++ b/solution.py
@@ -99,51 +99,52 @@
             out[head * HEAD + half : (head + 1) * HEAD, :] = (high * cosine - low * sine).astype(BF16)
 
 
-def send_kernel(line, streams, chunks, own, peer, features, *refs):
+def send_kernel(chunk, place, options, own, peer, features, *refs):
     z, x = spot()
-    pieces = dict(zip(chunks, refs))
-    befores = refs[len(chunks) : len(refs) - len(streams)]
-    outs = refs[len(refs) - len(streams) :]
-    at = 0
-    for (chunk, place, options, has_before), out in zip(streams, outs):
-        rows = out.shape[1]
-        before = befores[at] if has_before else None
-        at += int(has_before)
-        valid = pick(z, [int(d >= 0) for d in chunk])
-        where = pick(z, place)
-        mine = columns(pick(z, [max(d, 0) for d in chunk]), x, rows)
-
-        @pl.when(valid == 0)
+    pieces = dict(zip(options, refs))
+    befores, out = refs[len(options) : -1], refs[-1]
+    valid = pick(z, [int(d >= 0) for d in chunk])
+    where = pick(z, place)
+    mine = columns(pick(z, [max(d, 0) for d in chunk]), x, out.shape[1])
+
+    @pl.when(valid == 0)
+    def _():
+        out[...] = jnp.zeros_like(out)
+
+    for k in options:
+
+        @pl.when((valid == 1) & (where == k))
         def _():
-            out[...] = jnp.zeros_like(out)
-
-        for k in options:
-
-            @pl.when((valid == 1) & (where == k))
-            def _():
-                total = dot(own[...], features[:, mine]) + dot(peer[...], pieces[k][...])
-                if before is not None:
-                    total = total + before[...].astype(F32)
-                out[...] = total.astype(BF16)
-
-
-def final_kernel(scale, part, own, peer, features, theirs, even, odd, first, second, *refs):
-    new_first, new_second, keep, give = refs[-4:]
+            total = dot(own[...], features[:, mine]) + dot(peer[...], pieces[k][...])
+            for before in befores:
+                total = total + before[...].astype(F32)
+            out[...] = total.astype(BF16)
+
+
+def own_kernel(own, peer, features, theirs, out):
     z, x = spot()
-    rows = theirs.shape[1]
-    count, share, width = keep.shape
-    total = dot(own[...], features[:, columns(z, x, rows)]) + dot(peer[...], theirs[...])
-    total = total + even[...].astype(F32) + odd[...].astype(F32)
-    grad = total.T * scale
-    cols = slice(part * width, (part + 1) * width)
+    out[...] = dot(own[...], features[:, columns(z, x, theirs.shape[1])]) + dot(peer[...], theirs[...])
+
+
+def inner(scale, cols, total, even, odd, first, second):
+    grad = (total[...] + even[...].astype(F32) + odd[...].astype(F32)).T * scale
     fresh_first = 0.9 * first[:, cols] + 0.1 * grad
     fresh_second = 0.95 * second[:, cols] + 0.05 * grad * grad
-    new_first[...] = fresh_first
-    new_second[...] = fresh_second
-    update = fresh_first / (jnp.sqrt(fresh_second) + 1e-08)
-    ours, theirs = halves(update, count, share)
+    return fresh_first, fresh_second
+
+
+def update_kernel(scale, cols, total, even, odd, first, second, keep, give):
+    fresh_first, fresh_second = inner(scale, cols, total, even, odd, first, second)
+    count, share, _ = keep.shape
+    ours, theirs = halves(fresh_first / (jnp.sqrt(fresh_second) + 1e-08), count, share)
     keep[...] = ours.astype(keep.dtype)
     give[...] = theirs.astype(give.dtype)
+
+
+def moments_kernel(scale, cols, total, even, odd, first, second, *refs):
+    new_first, new_second, done = refs[-3:]
+    new_first[...], new_second[...] = inner(scale, cols, total, even, odd, first, second)
+    done[...] = jnp.zeros_like(done)
 
 
 def halves(value, count, share):
@@ -152,16 +153,21 @@
     return jnp.where(zero, pairs[:, 0], pairs[:, 1]), jnp.where(zero, pairs[:, 1], pairs[:, 0])
 
 
-def split_kernel(params, stay, give):
-    count, share, _ = stay.shape
-    stay[...], give[...] = halves(params[...], count, share)
-
-
-def partial_kernel(stay, came, mine, other):
-    near = lax.div(lax.axis_index("rep"), 2) == 0
-    held = stay[...] + came[...]
-    mine[...] = jnp.where(near, held[0], held[1])
-    other[...] = jnp.where(near, held[1], held[0])
+def held_kernel(params, came, out):
+    count, share, _ = out.shape
+    out[...] = halves(params[...], count, share)[0] + halves(came[...], count, share)[0]
+
+
+def partial_kernel(params, came, mine, other):
+    share = mine.shape[0]
+    core, near = lax.rem(lax.axis_index("rep"), 2), lax.div(lax.axis_index("rep"), 2)
+
+    def block(at):
+        part = pl.ds(pl.multiple_of((2 * at + core) * share, share), share)
+        return params[part, :] + came[part, :]
+
+    mine[...] = block(near)
+    other[...] = block(1 - near)
 
 
 def outer_kernel(part, reps, both, came, params_base, far_base, momentum_base, *refs):
@@ -184,11 +190,15 @@
     out[...] = both.reshape(out.shape)
 
 
+def here(value):
+    return pltpu.with_memory_space_constraint(value, pltpu.HBM)
+
+
 def after(value, *others):
     return lax.optimization_barrier((value, *others))[0]
 
 
-def call(kernel, ins, outs, scratch=(), into=None, places=None):
+def call(kernel, ins, outs, scratch=(), into=None, places=None, cost=1):
     into = into or []
     spaces = list(places or [pltpu.VMEM] * len(ins)) + [pl.ANY] * len(into)
     out_specs, shapes = [], []
@@ -206,6 +216,7 @@
         out_shape=shapes,
         scratch_shapes=list(scratch),
         input_output_aliases={len(ins) + i: i for i in range(len(into))},
+        cost_estimate=pl.CostEstimate(flops=1, transcendentals=0, bytes_accessed=cost),
         compiler_params=pltpu.CompilerParams(vmem_limit_bytes=VMEM_LIMIT),
     )(*ins, *into)
 
@@ -235,27 +246,35 @@
 
     def packed(source, which):
         return call(
-            functools.partial(pack_kernel, order, which), [source],
+            functools.partial(pack_kernel, order, which), [here(source)],
             [((tokens, rows), BF16)] * len(which),
-            scratch=[pltpu.SemaphoreType.DMA((len(which),))], places=[pl.ANY],
+            scratch=[pltpu.SemaphoreType.DMA((len(which),))], places=[pltpu.HBM],
         )
 
-    pieces = [lax.ppermute(after(packed(features, [0])[0], prev), "fsdp", pair)]
-    own = list(call(rotate_kernel, [doc_ids, prev, cotangent], [((width, tokens), BF16)] * HALVES))
-    peer = [lax.ppermute(part, "fsdp", pair) for part in own]
-    pieces += [lax.ppermute(piece, "fsdp", pair) for piece in packed(features, list(range(1, line)))]
+    (first_piece,) = packed(features, [0])
+    pieces = [lax.ppermute(first_piece, "fsdp", pair)]
 
     decay = 1.0 - 0.2 * 0.1
     groups = [[2 * q + c for q in range(outer)] for c in range(2)]
     block = ((outer, share, keys), F32)
-    stay, give = call(split_kernel, [after(params, own[0])], [block] * 2)
-    crossed = lax.ppermute(give, "rep", cores)
-    ready = None
+    crossed = lax.ppermute(params, "rep", cores)
     if outer == 2:
-        mine, ready = call(partial_kernel, [stay, crossed], [((share, keys), F32)] * 2)
+        mine, ready = call(partial_kernel, [params, crossed], [((share, keys), F32)] * 2)
         summed = mine + lax.ppermute(ready, "rep", across)
     else:
-        summed = lax.psum_scatter(stay + crossed, "rep", scatter_dimension=0, axis_index_groups=groups, tiled=False)
+        (held,) = call(held_kernel, [params, crossed], [block])
+        summed = lax.psum_scatter(held, "rep", scatter_dimension=0, axis_index_groups=groups, tiled=False)
+    own = list(call(rotate_kernel, [here(doc_ids), prev, after(cotangent, pieces[0])], [((width, tokens), BF16)] * HALVES))
+    peer = [lax.ppermute(part, "fsdp", pair) for part in own]
+    later = packed(features, list(range(1, line)))
+
+    def exchange(k, *done):
+        pieces.append(lax.ppermute(after(later[k - 1], *done), "fsdp", pair))
+
+    exchange(1)
+    if line > 2:
+        exchange(2, peer[0])
+
     base = anchor - (decay / reps) * summed
     momentum_base = 0.9 * momentum + base
     params_base = anchor - 0.7 * (base + 0.9 * momentum_base)
@@ -264,46 +283,60 @@
     else:
         bases = lax.all_gather(params_base, "rep", axis_index_groups=groups)
 
-    came = [(None, None)] * HALVES
+    came = [[None, None] for _ in range(HALVES)]
     for t, streams in enumerate(sends, 1):
-        for h in range(HALVES):
-            kept, chunks, before = [], set(), []
-            for chunk, arrived in zip(streams, came[h][::-1]):
-                options = sorted({int(place[z][d]) for z, d in enumerate(chunk) if d >= 0})
-                if not options:
-                    continue
-                chunks.update(options)
-                kept.append((chunk, [int(place[z][max(d, 0)]) for z, d in enumerate(chunk)], options, arrived is not None))
-                if arrived is not None:
-                    before.append(arrived)
-            if outer == 2 and h == 0:
-                if t == 2:
-                    own[h] = after(own[h], ready)
-                if t == 3:
-                    own[h] = after(own[h], params_base)
-            sent = call(
-                functools.partial(send_kernel, line, kept, sorted(chunks)),
-                [own[h], peer[h], features] + [pieces[k] for k in sorted(chunks)] + before,
-                [((width, rows), BF16)] * len(kept),
-            )
-            even = lax.ppermute(sent[0], "fsdp", evens)
-            odd = lax.ppermute(sent[1], "fsdp", odds) if len(sent) > 1 else None
-            came[h] = (even, odd)
+        arrived = [half[::-1] for half in came]
+        sent = {}
+        for side in (1, 0) if t == 2 else (0, 1):
+            chunk = streams[side]
+            options = sorted({int(place[z][d]) for z, d in enumerate(chunk) if d >= 0})
+            if not options:
+                continue
+            spots = [int(place[z][max(d, 0)]) for z, d in enumerate(chunk)]
+            for h in range(HALVES):
+                mine = own[h]
+                if (t, side) == (2, 0):
+                    mine = after(mine, *sent.values())
+                if (t, side, h) == (3, 0, 0):
+                    mine = after(mine, arrived[1][0])
+                if outer == 2 and (side, h) == (0, 0):
+                    mine = after(mine, *([ready] if t == 1 else [far_base] if t == 2 else []))
+                if outer == 2 and (t, side, h) == (2, 1, 0):
+                    mine = after(mine, params_base)
+                before = [] if arrived[h][side] is None else [arrived[h][side]]
+                (sent[side, h],) = call(
+                    functools.partial(send_kernel, chunk, spots, options),
+                    [mine, peer[h], features] + [pieces[k] for k in options] + before,
+                    [((width, rows), BF16)],
+                )
+                came[h][side] = lax.ppermute(sent[side, h], "fsdp", odds if side else evens)
+        if 2 <= t < line - 1:
+            exchange(t + 1, sent[0, 0])
 
     scale = 1.0 / math.sqrt(tokens * fsdp)
     new_first = new_second = new_params = new_momentum = None
-    momenta = []
+    momenta, tokens_done = [], []
     for h in range(HALVES):
-        ins = [own[h], peer[h], features, pieces[line - 1], *came[h], first, second]
-        new_first, new_second, keep, give = call(
-            functools.partial(final_kernel, scale, h), ins,
-            [((rows, keys), F32, h, width)] * 2 + [((outer, share, width), BF16)] * 2,
-            into=[new_first, new_second] if h else None,
+        cols = slice(h * width, (h + 1) * width)
+        mine = after(own[h], *sent.values()) if h == 0 else own[h]
+        (total,) = call(own_kernel, [mine, peer[h], features, pieces[line - 1]], [((width, rows), F32)])
+        if outer == 2:
+            total = after(total, far_base)
+        keep, give = call(
+            functools.partial(update_kernel, scale, cols), [total, *came[h], first, second],
+            [((outer, share, width), BF16)] * 2,
         )
         both = keep.astype(F32) + lax.ppermute(give, "rep", cores).astype(F32)
         if outer == 2:
             both = both.astype(BF16)
-            ins = [both, lax.ppermute(both, "rep", across), params_base, far_base, momentum_base]
+        new_first, new_second, done = call(
+            functools.partial(moments_kernel, scale, cols), [after(total, both), *came[h], first, second],
+            [((rows, keys), F32, h, width)] * 2 + [((8, 128), F32)], into=[new_first, new_second] if h else None,
+            cost=3 * rows * keys * 4,
+        )
+        tokens_done.append(done)
+        if outer == 2:
+            ins = [both if h == 0 else after(both, *tokens_done), lax.ppermute(both, "rep", across), params_base, far_base, momentum_base]
             new_momentum, fresh = call(
                 functools.partial(outer_kernel, h, reps), ins,
                 [((share, keys), F32, h, width), ((outer, share, width), F32)],

time: 92.9 us -> 77.8 us (0.84); the launches traced: 91.3 us -> 77.3 us
  waiting for transfers between devices: 34.4 us -> 23.6 us
  local copies, waits for them, and re-layouts: 4.81 us -> 0.05 us
  Pallas kernels: 10.5 us -> 13.7 us
  starting transfers between devices: 40.6 us -> 38.8 us
    ppermute x2, waiting for transfers between devices: 12.5 us -> 4.84 us  [local(): peer = [lax.ppermute(part, 'fsdp', pair) for part in own]]
    unnamed x18 -> x16, local copies, waits for them, and re-layouts: 4.81 us -> 0.05 us
    pallas_call x17 -> x24, Pallas kernels: 10.5 us -> 13.7 us  [call(): pl.pallas_call(kernel, grid=(1,), in_specs=[pl.BlockSpec(memory_space=spa...]
    ppermute x1, waiting for transfers between devices: 2.96 us -> 0.01 us  [local(): far_base = lax.ppermute(params_base, 'rep', across)]
    ppermute x1, waiting for transfers between devices: 1.5 us -> 0.01 us  [local(): prev = lax.ppermute(doc_ids, 'fsdp', [(f, f + 1) for f in range(fsdp - 1)])]
    ppermute x1, starting transfers between devices: 4.84 us -> 3.38 us  [local(): prev = lax.ppermute(doc_ids, 'fsdp', [(f, f + 1) for f in range(fsdp - 1)])]
    ppermute x15, waiting for transfers between devices: 12.2 us -> 13.6 us  [the longest x10 9.08 us: local(): came[h][side] = lax.ppermute(sent[side, h], 'fsdp', odds if side else evens)]
  transfers between devices with their start and end apart: 26 -> 26, of which waited for: 11 -> 9; matrix products, arithmetic and copies ran while one was open for 0% -> 0% of each run, Pallas kernels for 10% -> 17%
where the time goes in v3:
time: 77.8 us; the launch traced here: 77.3 us
  starting transfers between devices  38.8 us (50%)
  waiting for transfers between devices  23.6 us (30%)
  Pallas kernels  13.7 us (18%)
  between operations  0.97 us (1%)
    ppermute x10, starting transfers between devices, local(): came[h][side] = lax.ppermute(sent[side, h], 'fsdp', odds if side else evens)  18.9 us
    pallas_call x24, Pallas kernels, call(): pl.pallas_call(kernel, grid=(1,), in_specs=[pl.BlockSpec(memory_space=spa...  13.7 us
    ppermute x10, waiting for transfers between devices, local(): came[h][side] = lax.ppermute(sent[side, h], 'fsdp', odds if side else evens)  9.08 us
    ppermute x2, waiting for transfers between devices, local(): lax.ppermute(both, 'rep', across)  5.14 us
    ppermute x3, starting transfers between devices, exchange(): pieces.append(lax.ppermute(after(later[k - 1], *done), 'fsdp', pair))  4.9 us
    ppermute x2, waiting for transfers between devices, local(): peer = [lax.ppermute(part, 'fsdp', pair) for part in own]  4.84 us
    ppermute x1, waiting for transfers between devices, local(): pieces = [lax.ppermute(first_piece, 'fsdp', pair)]  4.46 us
    ppermute x1, starting transfers between devices, local(): prev = lax.ppermute(doc_ids, 'fsdp', [(f, f + 1) for f in range(fsdp - 1)])  3.38 us
  transfers between devices with their start and end apart: 26, of which 9 were waited for; matrix products, arithmetic and copies ran while one was open for 0% of the time, Pallas kernels for 17%

profile of v3, /device:TPU:0, one launch (start us, length us, event | category | flops | bytes accessed | tf_op | source)
XLA Modules:
  0.0 77.3 jit_solution(7661362360306729909)
XLA Ops:
  0.7 0.5 collective-permute-start.3
  1.2 1.0 %shard_map.111 = bf16[384,512]{1,0:T(8,128)(2,1)S(1)} custom-call(bf16[384,4096]{1,0:T(8,128)(2,1)} %bitcast.7), custom_call_target="tpu_custom_call" | custom-call | flops 1 | bytes 1 | tf_op jit(solution)/shard_map/pallas_call | solution.py:211
  2.2 2.7 %collective-permute-start.1 = (bf16[384,512]{1,0:T(8,128)(2,1)S(1)}, bf16[384,512]{1,0:T(8,128)(2,1)S(1)}, u32[]{:S(2)}, u32[]{:S(2)}) collective-permute-start(bf16[384,512]{1,0:T(8,128)(2,1)S(1)} %shard_map.111), channel_id=1, source_target_pairs={{0,1},{1,0},{2,3},{3,2},{4,5},{5,4},{6,7},{7,6},{8,9},{9,8},{10,11... | collective-permute-start | bytes 1179656 | tf_op jit(solution)/shard_map/ppermute | solution.py:255
  5.0 1.7 %collective-permute-start.4 = (f32[128,512]{1,0:T(8,128)S(1)}, f32[128,512]{1,0:T(8,128)S(1)}, u32[]{:S(2)}, u32[]{:S(2)}) collective-permute-start(f32[128,512]{1,0:T(8,128)S(1)} %get-tuple-element.42), channel_id=1, source_target_pairs={{0,16},{8,24},{16,0},{24,8},{1,17},{9,25},{17,1},{25,9},{2,18},{10... | collective-permute-start | bytes 786440 | tf_op jit(solution)/shard_map/ppermute | solution.py:263
  6.7 3.4 %collective-permute-start = (s32[1,384]{1,0:T(1,128)S(1)}, s32[1,384]{1,0:T(1,128)S(1)}, u32[]{:S(2)}, u32[]{:S(2)}) collective-permute-start(s32[1,384]{1,0:T(1,128)S(1)} %copy-done.7), channel_id=1, source_target_pairs={{0,1},{1,2},{2,3},{3,4},{4,5},{5,6},{6,7},{8,9},{9,10},{10,11},{11... | collective-permute-start | bytes 4616 | tf_op jit(solution)/shard_map/ppermute | solution.py:245
  10.1 4.5 %collective-permute-done.1.refs_0_ = bf16[384,512]{1,0:T(8,128)(2,1)S(1)} collective-permute-done((bf16[384,512]{1,0:T(8,128)(2,1)S(1)}, bf16[384,512]{1,0:T(8,128)(2,1)S(1)}, u32[]{:S(2)}, u32[]{:S(2)}) %collective-permute-start.1) | collective-permute-done | bytes 393248 | tf_op jit(solution)/shard_map/ppermute | solution.py:255
  14.6 1.4 %shard_map.112 = (bf16[256,384]{1,0:T(8,128)(2,1)S(1)}, bf16[256,384]{1,0:T(8,128)(2,1)S(1)}) custom-call(s32[1,384]{1,0:T(1,128)} %doc_ref.1, s32[1,384]{1,0:T(1,128)S(1)} %collective-permute-done.prev_ref, bf16[384,512]{1,0:T(8,128)(2,1)S(1)} %bitcast.31), custom_call_target="tpu_custom_call" | custom-call | flops 1 | bytes 1 | tf_op jit(solution)/shard_map/pallas_call | solution.py:211
  16.0 1.9 %collective-permute-start.2 = (bf16[256,384]{1,0:T(8,128)(2,1)S(1)}, bf16[256,384]{1,0:T(8,128)(2,1)S(1)}, u32[]{:S(2)}, u32[]{:S(2)}) collective-permute-start(bf16[256,384]{1,0:T(8,128)(2,1)S(1)} %get-tuple-element.52.own), channel_id=1, source_target_pairs={{0,1},{1,0},{2,3},{3,2},{4,5},{5,4},{6,7},{7,6},{8,9},{9,8},{10,11... | collective-permute-start | bytes 589832 | tf_op jit(solution)/shard_map/ppermute | solution.py:268
  18.1 1.3 %shard_map.113 = (bf16[384,512]{1,0:T(8,128)(2,1)S(1)}, bf16[384,512]{1,0:T(8,128)(2,1)S(1)}, bf16[384,512]{1,0:T(8,128)(2,1)S(1)}) custom-call(bf16[384,4096]{1,0:T(8,128)(2,1)} %bitcast.8), custom_call_target="tpu_custom_call" | custom-call | flops 1 | bytes 1 | tf_op jit(solution)/shard_map/pallas_call | solution.py:211
  19.4 1.9 %collective-permute-start.9 = (bf16[384,512]{1,0:T(8,128)(2,1)S(1)}, bf16[384,512]{1,0:T(8,128)(2,1)S(1)}, u32[]{:S(2)}, u32[]{:S(2)}) collective-permute-start(bf16[384,512]{1,0:T(8,128)(2,1)S(1)} %get-tuple-element.47), channel_id=1, source_target_pairs={{0,1},{1,0},{2,3},{3,2},{4,5},{5,4},{6,7},{7,6},{8,9},{9,8},{10,11... | collective-permute-start | bytes 1179656 | tf_op jit(solution)/shard_map/ppermute | solution.py:272
  21.2 2.6 %collective-permute-done.2.peer = bf16[256,384]{1,0:T(8,128)(2,1)S(1)} collective-permute-done((bf16[256,384]{1,0:T(8,128)(2,1)S(1)}, bf16[256,384]{1,0:T(8,128)(2,1)S(1)}, u32[]{:S(2)}, u32[]{:S(2)}) %collective-permute-start.2) | collective-permute-done | bytes 196640 | tf_op jit(solution)/shard_map/ppermute | solution.py:268
  23.9 0.4 shard_map.117
  24.3 1.6 %collective-permute-start.7 = (bf16[256,512]{1,0:T(8,128)(2,1)S(1)}, bf16[256,512]{1,0:T(8,128)(2,1)S(1)}, u32[]{:S(2)}, u32[]{:S(2)}) collective-permute-start(bf16[256,512]{1,0:T(8,128)(2,1)S(1)} %shard_map.117), channel_id=1, source_target_pairs={{0,2},{2,0},{1,3},{3,1},{4,6},{6,4},{5,7},{7,5},{8,10},{10,8},{9,1... | collective-permute-start | bytes 786440 | tf_op jit(solution)/shard_map/ppermute | solution.py:312
  25.9 2.2 %collective-permute-done.5.peer = bf16[256,384]{1,0:T(8,128)(2,1)S(1)} collective-permute-done((bf16[256,384]{1,0:T(8,128)(2,1)S(1)}, bf16[256,384]{1,0:T(8,128)(2,1)S(1)}, u32[]{:S(2)}, u32[]{:S(2)}) %collective-permute-start.5) | collective-permute-done | bytes 196640 | tf_op jit(solution)/shard_map/ppermute | solution.py:268
  28.1 0.4 shard_map.115
  28.5 1.6 %collective-permute-start.6 = (bf16[256,512]{1,0:T(8,128)(2,1)S(1)}, bf16[256,512]{1,0:T(8,128)(2,1)S(1)}, u32[]{:S(2)}, u32[]{:S(2)}) collective-permute-start(bf16[256,512]{1,0:T(8,128)(2,1)S(1)} %shard_map.115), channel_id=1, source_target_pairs={{0,2},{2,0},{1,3},{3,1},{4,6},{6,4},{5,7},{7,5},{8,10},{10,8},{9,1... | collective-permute-start | bytes 786440 | tf_op jit(solution)/shard_map/ppermute | solution.py:312
  30.2 1.6 %collective-permute-start.8 = (f32[128,512]{1,0:T(8,128)S(1)}, f32[128,512]{1,0:T(8,128)S(1)}, u32[]{:S(2)}, u32[]{:S(2)}) collective-permute-start(f32[128,512]{1,0:T(8,128)S(1)} %get-tuple-element.71.params_base), channel_id=1, source_target_pairs={{0,16},{8,24},{16,0},{24,8},{1,17},{9,25},{17,1},{25,9},{2,18},{10... | collective-permute-start | bytes 786440 | tf_op jit(solution)/shard_map/ppermute | solution.py:282
  31.8 1.5 %collective-permute-start.11 = (bf16[384,512]{1,0:T(8,128)(2,1)S(1)}, bf16[384,512]{1,0:T(8,128)(2,1)S(1)}, u32[]{:S(2)}, u32[]{:S(2)}) collective-permute-start(bf16[384,512]{1,0:T(8,128)(2,1)S(1)} %get-tuple-element.51), channel_id=1, source_target_pairs={{0,1},{1,0},{2,3},{3,2},{4,5},{5,4},{6,7},{7,6},{8,9},{9,8},{10,11... | collective-permute-start | bytes 1179656 | tf_op jit(solution)/shard_map/ppermute | solution.py:272
  33.3 0.7 collective-permute-start.12
  34.0 2.4 %collective-permute-done.6.refs_1_ = bf16[256,512]{1,0:T(8,128)(2,1)S(1)} collective-permute-done((bf16[256,512]{1,0:T(8,128)(2,1)S(1)}, bf16[256,512]{1,0:T(8,128)(2,1)S(1)}, u32[]{:S(2)}, u32[]{:S(2)}) %collective-permute-start.6) | collective-permute-done | bytes 262176 | tf_op jit(solution)/shard_map/ppermute | solution.py:312
  36.4 0.7 collective-permute-start.17
  37.1 0.4 shard_map.119
  37.6 4.4 %collective-permute-start.18 = (bf16[256,512]{1,0:T(8,128)(2,1)S(1)}, bf16[256,512]{1,0:T(8,128)(2,1)S(1)}, u32[]{:S(2)}, u32[]{:S(2)}) collective-permute-start(bf16[256,512]{1,0:T(8,128)(2,1)S(1)} %shard_map.119), channel_id=1, source_target_pairs={{0,2},{2,0},{1,3},{3,1},{4,6},{6,4},{5,7},{7,5},{8,10},{10,8},{9,1... | collective-permute-start | bytes 786440 | tf_op jit(solution)/shard_map/ppermute | solution.py:312
  41.9 1.5 %collective-permute-start.10 = (bf16[384,512]{1,0:T(8,128)(2,1)S(1)}, bf16[384,512]{1,0:T(8,128)(2,1)S(1)}, u32[]{:S(2)}, u32[]{:S(2)}) collective-permute-start(bf16[384,512]{1,0:T(8,128)(2,1)S(1)} %get-tuple-element.48), channel_id=1, source_target_pairs={{0,1},{1,0},{2,3},{3,2},{4,5},{5,4},{6,7},{7,6},{8,9},{9,8},{10,11... | collective-permute-start | bytes 1179656 | tf_op jit(solution)/shard_map/ppermute | solution.py:272
  43.4 0.4 shard_map.122
  43.9 2.3 %collective-permute-start.14 = (bf16[256,512]{1,0:T(8,128)(2,1)S(1)}, bf16[256,512]{1,0:T(8,128)(2,1)S(1)}, u32[]{:S(2)}, u32[]{:S(2)}) collective-permute-start(bf16[256,512]{1,0:T(8,128)(2,1)S(1)} %shard_map.122), channel_id=1, source_target_pairs={{0,2},{2,0},{1,3},{3,1},{4,6},{6,4},{5,7},{7,5},{8,10},{10,8},{9,1... | collective-permute-start | bytes 786440 | tf_op jit(solution)/shard_map/ppermute | solution.py:312
  46.2 0.4 shard_map.125
  46.6 2.9 %collective-permute-start.19 = (bf16[256,512]{1,0:T(8,128)(2,1)S(1)}, bf16[256,512]{1,0:T(8,128)(2,1)S(1)}, u32[]{:S(2)}, u32[]{:S(2)}) collective-permute-start(bf16[256,512]{1,0:T(8,128)(2,1)S(1)} %shard_map.125), channel_id=1, source_target_pairs={{0,2},{2,0},{1,3},{3,1},{4,6},{6,4},{5,7},{7,5},{8,10},{10,8},{9,1... | collective-permute-start | bytes 786440 | tf_op jit(solution)/shard_map/ppermute | solution.py:312
  49.5 0.7 collective-permute-start.20
  50.2 0.5 shard_map.121
  50.7 3.5 %collective-permute-start.13 = (bf16[256,512]{1,0:T(8,128)(2,1)S(1)}, bf16[256,512]{1,0:T(8,128)(2,1)S(1)}, u32[]{:S(2)}, u32[]{:S(2)}) collective-permute-start(bf16[256,512]{1,0:T(8,128)(2,1)S(1)} %shard_map.121), channel_id=1, source_target_pairs={{0,2},{2,0},{1,3},{3,1},{4,6},{6,4},{5,7},{7,5},{8,10},{10,8},{9,1... | collective-permute-start | bytes 786440 | tf_op jit(solution)/shard_map/ppermute | solution.py:312
  54.1 0.5 collective-permute-done.14.refs_2_
  54.7 0.8 %collective-permute-start.15 = (bf16[256,512]{1,0:T(8,128)(2,1)S(1)}, bf16[256,512]{1,0:T(8,128)(2,1)S(1)}, u32[]{:S(2)}, u32[]{:S(2)}) collective-permute-start(bf16[256,512]{1,0:T(8,128)(2,1)S(1)} %shard_map.123), channel_id=1, source_target_pairs={{2,4},{4,2},{3,5},{5,3},{10,12},{12,10},{11,13},{13,11},{18,20},{2... | collective-permute-start | bytes 786440 | tf_op jit(solution)/shard_map/ppermute | solution.py:312
  55.9 4.3 %collective-permute-done.19.even = bf16[256,512]{1,0:T(8,128)(2,1)S(1)} collective-permute-done((bf16[256,512]{1,0:T(8,128)(2,1)S(1)}, bf16[256,512]{1,0:T(8,128)(2,1)S(1)}, u32[]{:S(2)}, u32[]{:S(2)}) %collective-permute-start.19) | collective-permute-done | bytes 262176 | tf_op jit(solution)/shard_map/ppermute | solution.py:312
  60.3 0.4 shard_map.128
  60.8 0.4 shard_map.120.total
  61.2 1.9 %collective-permute-done.13.even = bf16[256,512]{1,0:T(8,128)(2,1)S(1)} collective-permute-done((bf16[256,512]{1,0:T(8,128)(2,1)S(1)}, bf16[256,512]{1,0:T(8,128)(2,1)S(1)}, u32[]{:S(2)}, u32[]{:S(2)}) %collective-permute-start.13) | collective-permute-done | bytes 262176 | tf_op jit(solution)/shard_map/ppermute | solution.py:312
  63.1 0.4 shard_map.124
  63.7 1.6 %collective-permute-start.23 = (bf16[2,128,256]{2,1,0:T(8,128)(2,1)S(1)}, bf16[2,128,256]{2,1,0:T(8,128)(2,1)S(1)}, u32[]{:S(2)}, u32[]{:S(2)}) collective-permute-start(bf16[2,128,256]{2,1,0:T(8,128)(2,1)S(1)} %add_convert_fusion.both), channel_id=1, source_target_pairs={{0,16},{8,24},{16,0},{24,8},{1,17},{9,25},{17,1},{25,9},{2,18},{10... | collective-permute-start | bytes 393224 | tf_op jit(solution)/shard_map/ppermute | solution.py:339
  65.3 1.3 %collective-permute-start.22 = (bf16[2,128,256]{2,1,0:T(8,128)(2,1)S(1)}, bf16[2,128,256]{2,1,0:T(8,128)(2,1)S(1)}, u32[]{:S(2)}, u32[]{:S(2)}) collective-permute-start(bf16[2,128,256]{2,1,0:T(8,128)(2,1)S(1)} %add_convert_fusion.1.both), channel_id=1, source_target_pairs={{0,16},{8,24},{16,0},{24,8},{1,17},{9,25},{17,1},{25,9},{2,18},{10... | collective-permute-start | bytes 393224 | tf_op jit(solution)/shard_map/ppermute | solution.py:339
  66.6 3.5 %collective-permute-done.23.came = bf16[2,128,256]{2,1,0:T(8,128)(2,1)S(1)} collective-permute-done((bf16[2,128,256]{2,1,0:T(8,128)(2,1)S(1)}, bf16[2,128,256]{2,1,0:T(8,128)(2,1)S(1)}, u32[]{:S(2)}, u32[]{:S(2)}) %collective-permute-start.23) | collective-permute-done | bytes 131104 | tf_op jit(solution)/shard_map/ppermute | solution.py:339
  70.1 0.7 shard_map.131
  70.8 1.7 %collective-permute-done.22.came = bf16[2,128,256]{2,1,0:T(8,128)(2,1)S(1)} collective-permute-done((bf16[2,128,256]{2,1,0:T(8,128)(2,1)S(1)}, bf16[2,128,256]{2,1,0:T(8,128)(2,1)S(1)}, u32[]{:S(2)}, u32[]{:S(2)}) %collective-permute-start.22) | collective-permute-done | bytes 131104 | tf_op jit(solution)/shard_map/ppermute | solution.py:339
  72.5 0.7 shard_map.132
  73.2 1.2 %shard_map.129 = (f32[512,512]{1,0:T(8,128)}, f32[512,512]{1,0:T(8,128)}, f32[8,128]{1,0:T(8,128)}) custom-call(f32[256,512]{1,0:T(8,128)S(1)} %shard_map.127.total, bf16[256,512]{1,0:T(8,128)(2,1)S(1)} %collective-permute-done.19.even, bf16[256,512]{1,0:T(8,128)(2,1)S(1)} %collective-permute-done.20.odd, f32[512,512]{1,0:T(8,128)S(1)} %bitcast.23, ...), custom_call_target="tpu_custom_call" | custom-call | flops 1 | bytes 3145728 | tf_op jit(solution)/shard_map/pallas_call | solution.py:211
  74.4 1.2 %shard_map.130 = (f32[512,512]{1,0:T(8,128)}, f32[512,512]{1,0:T(8,128)}, f32[8,128]{1,0:T(8,128)}) custom-call(f32[256,512]{1,0:T(8,128)S(1)} %shard_map.120.total, bf16[256,512]{1,0:T(8,128)(2,1)S(1)} %collective-permute-done.13.even, bf16[256,512]{1,0:T(8,128)(2,1)S(1)} %collective-permute-done.15.odd, ...), custom_call_target="tpu_custom_call", output_to_operand_aliasing={{0}: (5, {}), {1}: (6, {})} | custom-call | flops 1 | bytes 3145728 | tf_op jit(solution)/shard_map/pallas_call | solution.py:211
  75.6 0.8 %shard_map.133.refs_0_ = f32[512,512]{1,0:T(8,128)} custom-call(f32[2,128,256]{2,1,0:T(8,128)S(1)} %get-tuple-element.69.mine, f32[2,128,256]{2,1,0:T(8,128)S(1)} %collective-permute-done.25.theirs), custom_call_target="tpu_custom_call" | custom-call | flops 1 | bytes 1 | tf_op jit(solution)/shard_map/pallas_call | solution.py:211
  76.5 0.8 %shard_map.134 = f32[512,512]{1,0:T(8,128)} custom-call(f32[2,128,256]{2,1,0:T(8,128)S(1)} %get-tuple-element.68.mine, f32[2,128,256]{2,1,0:T(8,128)S(1)} %collective-permute-done.24.theirs, f32[512,512]{1,0:T(8,128)} %shard_map.133.refs_0_), custom_call_target="tpu_custom_call", output_to_operand_aliasing={{}: (2, {})} | custom-call | flops 1 | bytes 1 | tf_op jit(solution)/shard_map/pallas_call | solution.py:211
  (47 shorter events, 1.2 us)
Async XLA Ops:
  0.6 4.3 %copy-start.3 = (f32[1,512,512]{2,1,0:T(8,128)S(1)}, f32[1,512,512]{2,1,0:T(8,128)}, u32[]{:S(2)}) copy-start(f32[1,512,512]{2,1,0:T(8,128)} %param.11) | copy-start | bytes 3145732
  0.6 6.1 %copy-start.7 = (s32[1,384]{1,0:T(1,128)S(1)}, s32[1,384]{1,0:T(1,128)}, u32[]{:S(2)}) copy-start(s32[1,384]{1,0:T(1,128)} %doc_ref.1) | copy-start | bytes 4612
  0.7 13.9 %copy-start.4 = (bf16[1,384,512]{2,1,0:T(8,128)(2,1)S(1)}, bf16[1,384,512]{2,1,0:T(8,128)(2,1)}, u32[]{:S(2)}) copy-start(bf16[1,384,512]{2,1,0:T(8,128)(2,1)} %param.9) | copy-start | bytes 1179652
  0.7 4.2 %collective-permute-start.3 = (f32[512,512]{1,0:T(8,128)}, f32[512,512]{1,0:T(8,128)S(1)}, u32[]{:S(2)}, u32[]{:S(2)}) collective-permute-start(f32[512,512]{1,0:T(8,128)} %bitcast.29), channel_id=1, source_target_pairs={{0,8},{8,0},{16,24},{24,16},{1,9},{9,1},{17,25},{25,17},{2,10},{10... | collective-permute-start | bytes 3145736 | tf_op jit(solution)/shard_map/ppermute | solution.py:260
  2.2 21.7 %copy-start = (bf16[1,384,4096]{2,1,0:T(8,128)(2,1)S(1)}, bf16[1,384,4096]{2,1,0:T(8,128)(2,1)}, u32[]{:S(2)}) copy-start(bf16[1,384,4096]{2,1,0:T(8,128)(2,1)} %param.8) | copy-start | bytes 9437188
  2.2 12.3 %collective-permute-start.1 = (bf16[384,512]{1,0:T(8,128)(2,1)S(1)}, bf16[384,512]{1,0:T(8,128)(2,1)S(1)}, u32[]{:S(2)}, u32[]{:S(2)}) collective-permute-start(bf16[384,512]{1,0:T(8,128)(2,1)S(1)} %shard_map.111), channel_id=1, source_target_pairs={{0,1},{1,0},{2,3},{3,2},{4,5},{5,4},{6,7},{7,6},{8,9},{9,8},{10,11... | collective-permute-start | bytes 1179656 | tf_op jit(solution)/shard_map/ppermute | solution.py:255
  5.0 25.1 %collective-permute-start.4 = (f32[128,512]{1,0:T(8,128)S(1)}, f32[128,512]{1,0:T(8,128)S(1)}, u32[]{:S(2)}, u32[]{:S(2)}) collective-permute-start(f32[128,512]{1,0:T(8,128)S(1)} %get-tuple-element.42), channel_id=1, source_target_pairs={{0,16},{8,24},{16,0},{24,8},{1,17},{9,25},{17,1},{25,9},{2,18},{10... | collective-permute-start | bytes 786440 | tf_op jit(solution)/shard_map/ppermute | solution.py:263
  6.7 7.9 %collective-permute-start = (s32[1,384]{1,0:T(1,128)S(1)}, s32[1,384]{1,0:T(1,128)S(1)}, u32[]{:S(2)}, u32[]{:S(2)}) collective-permute-start(s32[1,384]{1,0:T(1,128)S(1)} %copy-done.7), channel_id=1, source_target_pairs={{0,1},{1,2},{2,3},{3,4},{4,5},{5,6},{6,7},{8,9},{9,10},{10,11},{11... | collective-permute-start | bytes 4616 | tf_op jit(solution)/shard_map/ppermute | solution.py:245
  16.0 7.9 %collective-permute-start.2 = (bf16[256,384]{1,0:T(8,128)(2,1)S(1)}, bf16[256,384]{1,0:T(8,128)(2,1)S(1)}, u32[]{:S(2)}, u32[]{:S(2)}) collective-permute-start(bf16[256,384]{1,0:T(8,128)(2,1)S(1)} %get-tuple-element.52.own), channel_id=1, source_target_pairs={{0,1},{1,0},{2,3},{3,2},{4,5},{5,4},{6,7},{7,6},{8,9},{9,8},{10,11... | collective-permute-start | bytes 589832 | tf_op jit(solution)/shard_map/ppermute | solution.py:268
  17.9 10.2 %collective-permute-start.5 = (bf16[256,384]{1,0:T(8,128)(2,1)S(1)}, bf16[256,384]{1,0:T(8,128)(2,1)S(1)}, u32[]{:S(2)}, u32[]{:S(2)}) collective-permute-start(bf16[256,384]{1,0:T(8,128)(2,1)S(1)} %get-tuple-element.57.own), channel_id=1, source_target_pairs={{0,1},{1,0},{2,3},{3,2},{4,5},{5,4},{6,7},{7,6},{8,9},{9,8},{10,11... | collective-permute-start | bytes 589832 | tf_op jit(solution)/shard_map/ppermute | solution.py:268
  19.4 17.7 %collective-permute-start.9 = (bf16[384,512]{1,0:T(8,128)(2,1)S(1)}, bf16[384,512]{1,0:T(8,128)(2,1)S(1)}, u32[]{:S(2)}, u32[]{:S(2)}) collective-permute-start(bf16[384,512]{1,0:T(8,128)(2,1)S(1)} %get-tuple-element.47), channel_id=1, source_target_pairs={{0,1},{1,0},{2,3},{3,2},{4,5},{5,4},{6,7},{7,6},{8,9},{9,8},{10,11... | collective-permute-start | bytes 1179656 | tf_op jit(solution)/shard_map/ppermute | solution.py:272
  24.3 5.8 %copy-start.5 = (f32[128,512]{1,0:T(8,128)S(1)}, f32[128,512]{1,0:T(8,128)}, u32[]{:S(2)}) copy-start(f32[128,512]{1,0:T(8,128)} %param.15) | copy-start | bytes 786436
  24.3 5.8 %copy-start.6 = (f32[128,512]{1,0:T(8,128)S(1)}, f32[128,512]{1,0:T(8,128)}, u32[]{:S(2)}) copy-start(f32[128,512]{1,0:T(8,128)} %param.14) | copy-start | bytes 786436
  24.3 9.0 %collective-permute-start.7 = (bf16[256,512]{1,0:T(8,128)(2,1)S(1)}, bf16[256,512]{1,0:T(8,128)(2,1)S(1)}, u32[]{:S(2)}, u32[]{:S(2)}) collective-permute-start(bf16[256,512]{1,0:T(8,128)(2,1)S(1)} %shard_map.117), channel_id=1, source_target_pairs={{0,2},{2,0},{1,3},{3,1},{4,6},{6,4},{5,7},{7,5},{8,10},{10,8},{9,1... | collective-permute-start | bytes 786440 | tf_op jit(solution)/shard_map/ppermute | solution.py:312
  28.5 7.9 %collective-permute-start.6 = (bf16[256,512]{1,0:T(8,128)(2,1)S(1)}, bf16[256,512]{1,0:T(8,128)(2,1)S(1)}, u32[]{:S(2)}, u32[]{:S(2)}) collective-permute-start(bf16[256,512]{1,0:T(8,128)(2,1)S(1)} %shard_map.115), channel_id=1, source_target_pairs={{0,2},{2,0},{1,3},{3,1},{4,6},{6,4},{5,7},{7,5},{8,10},{10,8},{9,1... | collective-permute-start | bytes 786440 | tf_op jit(solution)/shard_map/ppermute | solution.py:312
  30.2 6.9 %collective-permute-start.8 = (f32[128,512]{1,0:T(8,128)S(1)}, f32[128,512]{1,0:T(8,128)S(1)}, u32[]{:S(2)}, u32[]{:S(2)}) collective-permute-start(f32[128,512]{1,0:T(8,128)S(1)} %get-tuple-element.71.params_base), channel_id=1, source_target_pairs={{0,16},{8,24},{16,0},{24,8},{1,17},{9,25},{17,1},{25,9},{2,18},{10... | collective-permute-start | bytes 786440 | tf_op jit(solution)/shard_map/ppermute | solution.py:282
  31.8 14.4 %collective-permute-start.11 = (bf16[384,512]{1,0:T(8,128)(2,1)S(1)}, bf16[384,512]{1,0:T(8,128)(2,1)S(1)}, u32[]{:S(2)}, u32[]{:S(2)}) collective-permute-start(bf16[384,512]{1,0:T(8,128)(2,1)S(1)} %get-tuple-element.51), channel_id=1, source_target_pairs={{0,1},{1,0},{2,3},{3,2},{4,5},{5,4},{6,7},{7,6},{8,9},{9,8},{10,11... | collective-permute-start | bytes 1179656 | tf_op jit(solution)/shard_map/ppermute | solution.py:272
  33.3 10.5 %collective-permute-start.12 = (bf16[256,512]{1,0:T(8,128)(2,1)S(1)}, bf16[256,512]{1,0:T(8,128)(2,1)S(1)}, u32[]{:S(2)}, u32[]{:S(2)}) collective-permute-start(bf16[256,512]{1,0:T(8,128)(2,1)S(1)} %shard_map.118), channel_id=1, source_target_pairs={{2,4},{4,2},{3,5},{5,3},{10,12},{12,10},{11,13},{13,11},{18,20},{2... | collective-permute-start | bytes 786440 | tf_op jit(solution)/shard_map/ppermute | solution.py:312
  36.4 9.8 %collective-permute-start.17 = (bf16[256,512]{1,0:T(8,128)(2,1)S(1)}, bf16[256,512]{1,0:T(8,128)(2,1)S(1)}, u32[]{:S(2)}, u32[]{:S(2)}) collective-permute-start(bf16[256,512]{1,0:T(8,128)(2,1)S(1)} %shard_map.116), channel_id=1, source_target_pairs={{2,4},{4,2},{3,5},{5,3},{10,12},{12,10},{11,13},{13,11},{18,20},{2... | collective-permute-start | bytes 786440 | tf_op jit(solution)/shard_map/ppermute | solution.py:312
  37.6 11.9 %collective-permute-start.18 = (bf16[256,512]{1,0:T(8,128)(2,1)S(1)}, bf16[256,512]{1,0:T(8,128)(2,1)S(1)}, u32[]{:S(2)}, u32[]{:S(2)}) collective-permute-start(bf16[256,512]{1,0:T(8,128)(2,1)S(1)} %shard_map.119), channel_id=1, source_target_pairs={{0,2},{2,0},{1,3},{3,1},{4,6},{6,4},{5,7},{7,5},{8,10},{10,8},{9,1... | collective-permute-start | bytes 786440 | tf_op jit(solution)/shard_map/ppermute | solution.py:312
  41.9 13.6 %collective-permute-start.10 = (bf16[384,512]{1,0:T(8,128)(2,1)S(1)}, bf16[384,512]{1,0:T(8,128)(2,1)S(1)}, u32[]{:S(2)}, u32[]{:S(2)}) collective-permute-start(bf16[384,512]{1,0:T(8,128)(2,1)S(1)} %get-tuple-element.48), channel_id=1, source_target_pairs={{0,1},{1,0},{2,3},{3,2},{4,5},{5,4},{6,7},{7,6},{8,9},{9,8},{10,11... | collective-permute-start | bytes 1179656 | tf_op jit(solution)/shard_map/ppermute | solution.py:272
  43.9 10.7 %collective-permute-start.14 = (bf16[256,512]{1,0:T(8,128)(2,1)S(1)}, bf16[256,512]{1,0:T(8,128)(2,1)S(1)}, u32[]{:S(2)}, u32[]{:S(2)}) collective-permute-start(bf16[256,512]{1,0:T(8,128)(2,1)S(1)} %shard_map.122), channel_id=1, source_target_pairs={{0,2},{2,0},{1,3},{3,1},{4,6},{6,4},{5,7},{7,5},{8,10},{10,8},{9,1... | collective-permute-start | bytes 786440 | tf_op jit(solution)/shard_map/ppermute | solution.py:312
  46.6 13.7 %collective-permute-start.19 = (bf16[256,512]{1,0:T(8,128)(2,1)S(1)}, bf16[256,512]{1,0:T(8,128)(2,1)S(1)}, u32[]{:S(2)}, u32[]{:S(2)}) collective-permute-start(bf16[256,512]{1,0:T(8,128)(2,1)S(1)} %shard_map.125), channel_id=1, source_target_pairs={{0,2},{2,0},{1,3},{3,1},{4,6},{6,4},{5,7},{7,5},{8,10},{10,8},{9,1... | collective-permute-start | bytes 786440 | tf_op jit(solution)/shard_map/ppermute | solution.py:312
  49.5 10.8 %collective-permute-start.20 = (bf16[256,512]{1,0:T(8,128)(2,1)S(1)}, bf16[256,512]{1,0:T(8,128)(2,1)S(1)}, u32[]{:S(2)}, u32[]{:S(2)}) collective-permute-start(bf16[256,512]{1,0:T(8,128)(2,1)S(1)} %shard_map.126), channel_id=1, source_target_pairs={{2,4},{4,2},{3,5},{5,3},{10,12},{12,10},{11,13},{13,11},{18,20},{2... | collective-permute-start | bytes 786440 | tf_op jit(solution)/shard_map/ppermute | solution.py:312
  50.7 12.5 %collective-permute-start.13 = (bf16[256,512]{1,0:T(8,128)(2,1)S(1)}, bf16[256,512]{1,0:T(8,128)(2,1)S(1)}, u32[]{:S(2)}, u32[]{:S(2)}) collective-permute-start(bf16[256,512]{1,0:T(8,128)(2,1)S(1)} %shard_map.121), channel_id=1, source_target_pairs={{0,2},{2,0},{1,3},{3,1},{4,6},{6,4},{5,7},{7,5},{8,10},{10,8},{9,1... | collective-permute-start | bytes 786440 | tf_op jit(solution)/shard_map/ppermute | solution.py:312
  54.7 5.6 %copy-start.1 = (f32[1,512,512]{2,1,0:T(8,128)S(1)}, f32[1,512,512]{2,1,0:T(8,128)}, u32[]{:S(2)}) copy-start(f32[1,512,512]{2,1,0:T(8,128)} %param.12) | copy-start | bytes 3145732
  54.7 5.6 %copy-start.2 = (f32[1,512,512]{2,1,0:T(8,128)S(1)}, f32[1,512,512]{2,1,0:T(8,128)}, u32[]{:S(2)}) copy-start(f32[1,512,512]{2,1,0:T(8,128)} %param.13) | copy-start | bytes 3145732
  54.7 8.4 %collective-permute-start.15 = (bf16[256,512]{1,0:T(8,128)(2,1)S(1)}, bf16[256,512]{1,0:T(8,128)(2,1)S(1)}, u32[]{:S(2)}, u32[]{:S(2)}) collective-permute-start(bf16[256,512]{1,0:T(8,128)(2,1)S(1)} %shard_map.123), channel_id=1, source_target_pairs={{2,4},{4,2},{3,5},{5,3},{10,12},{12,10},{11,13},{13,11},{18,20},{2... | collective-permute-start | bytes 786440 | tf_op jit(solution)/shard_map/ppermute | solution.py:312
  60.7 2.9 %collective-permute-start.21 = (bf16[2,128,256]{2,1,0:T(8,128)(2,1)S(1)}, bf16[2,128,256]{2,1,0:T(8,128)(2,1)S(1)}, u32[]{:S(2)}, u32[]{:S(2)}) collective-permute-start(bf16[2,128,256]{2,1,0:T(8,128)(2,1)S(1)} %get-tuple-element.60), channel_id=1, source_target_pairs={{0,8},{8,0},{16,24},{24,16},{1,9},{9,1},{17,25},{25,17},{2,10},{10... | collective-permute-start | bytes 393224 | tf_op jit(solution)/shard_map/ppermute | solution.py:329
  63.6 1.7 %collective-permute-start.16 = (bf16[2,128,256]{2,1,0:T(8,128)(2,1)S(1)}, bf16[2,128,256]{2,1,0:T(8,128)(2,1)S(1)}, u32[]{:S(2)}, u32[]{:S(2)}) collective-permute-start(bf16[2,128,256]{2,1,0:T(8,128)(2,1)S(1)} %get-tuple-element.54), channel_id=1, source_target_pairs={{0,8},{8,0},{16,24},{24,16},{1,9},{9,1},{17,25},{25,17},{2,10},{10... | collective-permute-start | bytes 393224 | tf_op jit(solution)/shard_map/ppermute | solution.py:329
  63.7 6.4 %collective-permute-start.23 = (bf16[2,128,256]{2,1,0:T(8,128)(2,1)S(1)}, bf16[2,128,256]{2,1,0:T(8,128)(2,1)S(1)}, u32[]{:S(2)}, u32[]{:S(2)}) collective-permute-start(bf16[2,128,256]{2,1,0:T(8,128)(2,1)S(1)} %add_convert_fusion.both), channel_id=1, source_target_pairs={{0,16},{8,24},{16,0},{24,8},{1,17},{9,25},{17,1},{25,9},{2,18},{10... | collective-permute-start | bytes 393224 | tf_op jit(solution)/shard_map/ppermute | solution.py:339
  65.3 7.1 %collective-permute-start.22 = (bf16[2,128,256]{2,1,0:T(8,128)(2,1)S(1)}, bf16[2,128,256]{2,1,0:T(8,128)(2,1)S(1)}, u32[]{:S(2)}, u32[]{:S(2)}) collective-permute-start(bf16[2,128,256]{2,1,0:T(8,128)(2,1)S(1)} %add_convert_fusion.1.both), channel_id=1, source_target_pairs={{0,16},{8,24},{16,0},{24,8},{1,17},{9,25},{17,1},{25,9},{2,18},{10... | collective-permute-start | bytes 393224 | tf_op jit(solution)/shard_map/ppermute | solution.py:339
  70.8 4.9 %collective-permute-start.25 = (f32[2,128,256]{2,1,0:T(8,128)S(1)}, f32[2,128,256]{2,1,0:T(8,128)S(1)}, u32[]{:S(2)}, u32[]{:S(2)}) collective-permute-start(f32[2,128,256]{2,1,0:T(8,128)S(1)} %get-tuple-element.69.mine), channel_id=1, source_target_pairs={{0,8},{8,0},{16,24},{24,16},{1,9},{9,1},{17,25},{25,17},{2,10},{10... | collective-permute-start | bytes 786440 | tf_op jit(solution)/shard_map/ppermute | solution.py:351
  73.2 3.3 %collective-permute-start.24 = (f32[2,128,256]{2,1,0:T(8,128)S(1)}, f32[2,128,256]{2,1,0:T(8,128)S(1)}, u32[]{:S(2)}, u32[]{:S(2)}) collective-permute-start(f32[2,128,256]{2,1,0:T(8,128)S(1)} %get-tuple-element.68.mine), channel_id=1, source_target_pairs={{0,8},{8,0},{16,24},{24,16},{1,9},{9,1},{17,25},{25,17},{2,10},{10... | collective-permute-start | bytes 786440 | tf_op jit(solution)/shard_map/ppermute | solution.py:351

commit v4 on v3

--- a/solution.py
+++ b/solution.py
@@ -61,42 +61,65 @@
 
 def pack_kernel(order, which, features, *refs):
     z, x = spot()
-    outs, sems = refs[:-1], refs[-1]
-    rows = outs[0].shape[1]
-    copies = []
-    for i, (k, out) in enumerate(zip(which, outs)):
+    sems = refs[-1]
+    source, outs = (refs[0], refs[1:-1]) if which == [0] else (None, refs[:-1])
+    rows = features.shape[1] // (2 * len(order))
+    moves = []
+    for k, out in zip(which, outs):
         chunk = pick(z, [int(order[p][k]) for p in range(len(order))])
-        copies.append(pltpu.make_async_copy(features.at[:, columns(chunk, 1 - x, rows)], out, sems.at[i]))
+        moves.append((features.at[:, columns(chunk, 1 - x, rows)], out.at[:, :rows]))
+    if source is not None:
+        width = source.shape[1] // len(outs)
+        for at, out in enumerate(outs):
+            target = out.at[:, rows:] if at == 0 else out
+            moves.append((source.at[:, at * width : (at + 1) * width], target))
+    copies = [pltpu.make_async_copy(*move, sems.at[i]) for i, move in enumerate(moves)]
     for copy in copies:
         copy.start()
     for copy in copies:
         copy.wait()
 
 
-def rotate_kernel(doc_ref, prev_ref, cot_ref, *outs):
-    tokens = doc_ref.shape[1]
+def turn(cosine, sine, source, out):
+    half = HEAD // 2
+    flipped = source.astype(F32).T
+    for head in range(out.shape[0] // HEAD):
+        low = flipped[head * HEAD : head * HEAD + half]
+        high = flipped[head * HEAD + half : (head + 1) * HEAD]
+        out[head * HEAD : head * HEAD + half, :] = (low * cosine + high * sine).astype(BF16)
+        out[head * HEAD + half : (head + 1) * HEAD, :] = (high * cosine - low * sine).astype(BF16)
+
+
+def rotate_kernel(own_doc, peer_doc, before_low, before_high, cotangent, peer_cosine, peer_sine, *outs):
+    tokens = own_doc.shape[1]
+    x = lax.rem(lax.axis_index("fsdp"), 2)
 
     def start(doc):
         last = jnp.max(doc, axis=1, keepdims=True)
         return tokens - jnp.sum((doc == last).astype(jnp.int32), axis=1, keepdims=True)
 
+    own, peer = start(own_doc[...]), start(peer_doc[...])
+    before = start(jnp.where(x == 0, before_low[...], before_high[...]))
     places = lax.broadcasted_iota(jnp.int32, (1, tokens), 1)
-    own = start(doc_ref[...])
-    before = start(prev_ref[...])
-    offsets = jnp.where(places >= own, places - own, places + tokens - before).astype(F32)
     half = HEAD // 2
     steps = lax.broadcasted_iota(jnp.int32, (half, 1), 0).astype(F32)
     frequency = jnp.exp(steps * (-math.log(ROPE_BASE) / half))
-    angles = frequency * offsets
-    cosine, sine = jnp.cos(angles), jnp.sin(angles)
+
+    def angles(first, carried):
+        offsets = jnp.where(places >= first, places - first, places + tokens - carried)
+        return frequency * offsets.astype(F32)
+
+    turned = angles(own, jnp.where(x == 0, before, peer))
+    cosine, sine = jnp.cos(turned), jnp.sin(turned)
     width = outs[0].shape[0]
     for part, out in enumerate(outs):
-        turned = cot_ref[:, part * width : (part + 1) * width].astype(F32).T
-        for head in range(width // HEAD):
-            low = turned[head * HEAD : head * HEAD + half]
-            high = turned[head * HEAD + half : (head + 1) * HEAD]
-            out[head * HEAD : head * HEAD + half, :] = (low * cosine + high * sine).astype(BF16)
-            out[head * HEAD + half : (head + 1) * HEAD, :] = (high * cosine - low * sine).astype(BF16)
+        turn(cosine, sine, cotangent[:, part * width : (part + 1) * width], out)
+    turned = angles(peer, jnp.where(x == 0, own, before))
+    peer_cosine[...], peer_sine[...] = jnp.cos(turned), jnp.sin(turned)
+
+
+def peer_kernel(cosine, sine, source, out):
+    turn(cosine[...], sine[...], source[:, source.shape[1] - out.shape[0] :], out)
 
 
 def send_kernel(chunk, place, options, own, peer, features, *refs):
@@ -115,7 +138,7 @@
 
         @pl.when((valid == 1) & (where == k))
         def _():
-            total = dot(own[...], features[:, mine]) + dot(peer[...], pieces[k][...])
+            total = dot(own[...], features[:, mine]) + dot(peer[...], pieces[k][:, : out.shape[1]])
             for before in befores:
                 total = total + before[...].astype(F32)
             out[...] = total.astype(BF16)
@@ -242,17 +265,15 @@
             a, b = 2 * z + x, 2 * z + 2 + x
             (evens if z % 2 == 0 else odds).extend([(a, b), (b, a)])
 
-    prev = lax.ppermute(doc_ids, "fsdp", [(f, f + 1) for f in range(fsdp - 1)])
-
-    def packed(source, which):
-        return call(
-            functools.partial(pack_kernel, order, which), [here(source)],
-            [((tokens, rows), BF16)] * len(which),
-            scratch=[pltpu.SemaphoreType.DMA((len(which),))], places=[pltpu.HBM],
-        )
-
-    (first_piece,) = packed(features, [0])
+    first_piece, *raw = call(
+        functools.partial(pack_kernel, order, [0]), [here(features), here(cotangent)],
+        [((tokens, rows + width), BF16)] + [((tokens, width), BF16)] * (HALVES - 1),
+        scratch=[pltpu.SemaphoreType.DMA((1 + HALVES,))], places=[pltpu.HBM] * 2,
+    )
     pieces = [lax.ppermute(first_piece, "fsdp", pair)]
+    peer_doc = lax.ppermute(doc_ids, "fsdp", pair)
+    before_low = lax.ppermute(doc_ids, "fsdp", [(f, f + 1) for f in range(1, fsdp - 1, 2)])
+    before_high = lax.ppermute(doc_ids, "fsdp", [(f, f + 2) for f in range(1, fsdp - 2, 2)])
 
     decay = 1.0 - 0.2 * 0.1
     groups = [[2 * q + c for q in range(outer)] for c in range(2)]
@@ -264,17 +285,6 @@
     else:
         (held,) = call(held_kernel, [params, crossed], [block])
         summed = lax.psum_scatter(held, "rep", scatter_dimension=0, axis_index_groups=groups, tiled=False)
-    own = list(call(rotate_kernel, [here(doc_ids), prev, after(cotangent, pieces[0])], [((width, tokens), BF16)] * HALVES))
-    peer = [lax.ppermute(part, "fsdp", pair) for part in own]
-    later = packed(features, list(range(1, line)))
-
-    def exchange(k, *done):
-        pieces.append(lax.ppermute(after(later[k - 1], *done), "fsdp", pair))
-
-    exchange(1)
-    if line > 2:
-        exchange(2, peer[0])
-
     base = anchor - (decay / reps) * summed
     momentum_base = 0.9 * momentum + base
     params_base = anchor - 0.7 * (base + 0.9 * momentum_base)
@@ -283,45 +293,57 @@
     else:
         bases = lax.all_gather(params_base, "rep", axis_index_groups=groups)
 
+    half = ((HEAD // 2, tokens), F32)
+    peer_cosine, peer_sine, *own = call(
+        rotate_kernel, [doc_ids, peer_doc, before_low, before_high, after(cotangent, pieces[0], params_base)],
+        [half, half] + [((width, tokens), BF16)] * HALVES,
+    )
+    raw = [pieces[0]] + [lax.ppermute(part, "fsdp", pair) for part in raw]
+    peer = [call(peer_kernel, [peer_cosine, peer_sine, part], [((width, tokens), BF16)])[0] for part in raw]
+    later = call(
+        functools.partial(pack_kernel, order, list(range(1, line))), [here(features)],
+        [((tokens, rows), BF16)] * (line - 1),
+        scratch=[pltpu.SemaphoreType.DMA((line - 1,))], places=[pltpu.HBM],
+    )
+
+    def exchange(k, *done):
+        pieces.append(lax.ppermute(after(later[k - 1], *done), "fsdp", pair))
+
+    exchange(1)
+    if line > 2:
+        exchange(2, peer[0])
+
     came = [[None, None] for _ in range(HALVES)]
+    last = None
     for t, streams in enumerate(sends, 1):
         arrived = [half[::-1] for half in came]
-        sent = {}
-        for side in (1, 0) if t == 2 else (0, 1):
-            chunk = streams[side]
-            options = sorted({int(place[z][d]) for z, d in enumerate(chunk) if d >= 0})
-            if not options:
-                continue
+        choices = [sorted({int(place[z][d]) for z, d in enumerate(chunk) if d >= 0}) for chunk in streams]
+        turns = [(side, h) for h in range(HALVES) for side in (0, 1) if choices[side]]
+        if t == 2:
+            turns.sort(key=lambda turn: (turn[1], -turn[0]))
+        for side, h in turns:
+            chunk, options = streams[side], choices[side]
             spots = [int(place[z][max(d, 0)]) for z, d in enumerate(chunk)]
-            for h in range(HALVES):
-                mine = own[h]
-                if (t, side) == (2, 0):
-                    mine = after(mine, *sent.values())
-                if (t, side, h) == (3, 0, 0):
-                    mine = after(mine, arrived[1][0])
-                if outer == 2 and (side, h) == (0, 0):
-                    mine = after(mine, *([ready] if t == 1 else [far_base] if t == 2 else []))
-                if outer == 2 and (t, side, h) == (2, 1, 0):
-                    mine = after(mine, params_base)
-                before = [] if arrived[h][side] is None else [arrived[h][side]]
-                (sent[side, h],) = call(
-                    functools.partial(send_kernel, chunk, spots, options),
-                    [mine, peer[h], features] + [pieces[k] for k in options] + before,
-                    [((width, rows), BF16)],
-                )
-                came[h][side] = lax.ppermute(sent[side, h], "fsdp", odds if side else evens)
-        if 2 <= t < line - 1:
-            exchange(t + 1, sent[0, 0])
+            waits = [] if last is None else [last]
+            if outer == 2 and t == 2:
+                waits.append(far_base)
+            before = [] if arrived[h][side] is None else [arrived[h][side]]
+            (last,) = call(
+                functools.partial(send_kernel, chunk, spots, options),
+                [after(own[h], *waits), peer[h], features] + [pieces[k] for k in options] + before,
+                [((width, rows), BF16)],
+            )
+            came[h][side] = lax.ppermute(last, "fsdp", odds if side else evens)
+            if 2 <= t < line - 1 and (side, h) == (0, 0):
+                exchange(t + 1, last)
 
     scale = 1.0 / math.sqrt(tokens * fsdp)
     new_first = new_second = new_params = new_momentum = None
     momenta, tokens_done = [], []
     for h in range(HALVES):
         cols = slice(h * width, (h + 1) * width)
-        mine = after(own[h], *sent.values()) if h == 0 else own[h]
+        mine = after(own[h], last) if h == 0 else own[h]
         (total,) = call(own_kernel, [mine, peer[h], features, pieces[line - 1]], [((width, rows), F32)])
-        if outer == 2:
-            total = after(total, far_base)
         keep, give = call(
             functools.partial(update_kernel, scale, cols), [total, *came[h], first, second],
             [((outer, share, width), BF16)] * 2,
@@ -336,7 +358,9 @@
         )
         tokens_done.append(done)
         if outer == 2:
-            ins = [both if h == 0 else after(both, *tokens_done), lax.ppermute(both, "rep", across), params_base, far_base, momentum_base]
+            ins = [both, lax.ppermute(both, "rep", across), params_base, far_base, momentum_base]
+            if h == HALVES - 1:
+                ins += tokens_done
             new_momentum, fresh = call(
                 functools.partial(outer_kernel, h, reps), ins,
                 [((share, keys), F32, h, width), ((outer, share, width), F32)],

time: 77.8 us -> 73.6 us (0.946)
  starting transfers between devices: 38.8 us -> 33.1 us
  waiting for transfers between devices: 23.6 us -> 24.9 us
    ppermute x13 -> x14, starting transfers between devices: 24.4 us -> 20.5 us  [the longest x10 15.9 us: local(): came[h][side] = lax.ppermute(last, 'fsdp', odds if side else evens)]
    ppermute x1, waiting for transfers between devices: 4.46 us -> 8.14 us  [local(): pieces = [lax.ppermute(first_piece, 'fsdp', pair)]]
    ppermute x13 -> x14, waiting for transfers between devices: 13.9 us -> 11.2 us  [the longest x10 11.2 us: local(): came[h][side] = lax.ppermute(last, 'fsdp', odds if side else evens)]
    ppermute x2, waiting for transfers between devices: 5.14 us -> 2.84 us  [local(): lax.ppermute(both, 'rep', across)]
    ppermute x3, waiting for transfers between devices: 0.01 us -> 2.05 us  [exchange(): pieces.append(lax.ppermute(after(later[k - 1], *done), 'fsdp', pair))]
    ppermute x3, starting transfers between devices: 4.9 us -> 3.19 us  [exchange(): pieces.append(lax.ppermute(after(later[k - 1], *done), 'fsdp', pair))]
    pallas_call x24 -> x26, Pallas kernels: 13.7 us -> 14 us  [call(): pl.pallas_call(kernel, grid=(1,), in_specs=[pl.BlockSpec(memory_space=spa...]
  transfers between devices with their start and end apart: 26 -> 27, of which waited for: 9 -> 10; matrix products, arithmetic and copies ran while one was open for 0% -> 0% of each run, Pallas kernels for 17% -> 18%
where the time goes in v4:
time: 73.6 us; the launch traced here: 73.2 us
  starting transfers between devices  33.1 us (45%)
  waiting for transfers between devices  24.9 us (34%)
  Pallas kernels  14 us (19%)
  between operations  0.99 us (1%)
    ppermute x10, starting transfers between devices, local(): came[h][side] = lax.ppermute(last, 'fsdp', odds if side else evens)  15.9 us
    pallas_call x26, Pallas kernels, call(): pl.pallas_call(kernel, grid=(1,), in_specs=[pl.BlockSpec(memory_space=spa...  14 us
    ppermute x10, waiting for transfers between devices, local(): came[h][side] = lax.ppermute(last, 'fsdp', odds if side else evens)  11.2 us
    ppermute x1, waiting for transfers between devices, local(): pieces = [lax.ppermute(first_piece, 'fsdp', pair)]  8.14 us
    ppermute x3, starting transfers between devices, exchange(): pieces.append(lax.ppermute(after(later[k - 1], *done), 'fsdp', pair))  3.19 us
    ppermute x2, waiting for transfers between devices, local(): lax.ppermute(both, 'rep', across)  2.84 us
    ppermute x2, starting transfers between devices, local(): lax.ppermute(both, 'rep', across)  2.71 us
    ppermute x1, starting transfers between devices, local(): pieces = [lax.ppermute(first_piece, 'fsdp', pair)]  2.65 us
  transfers between devices with their start and end apart: 27, of which 10 were waited for; matrix products, arithmetic and copies ran while one was open for 0% of the time, Pallas kernels for 18%

profile of v4, /device:TPU:0, one launch (start us, length us, event | category | flops | bytes accessed | tf_op | source)
XLA Modules:
  0.0 73.2 jit_solution(4830023508233663607)
XLA Ops:
  0.7 0.5 collective-permute-start.4
  1.2 1.2 %shard_map.111 = (bf16[384,768]{1,0:T(8,128)(2,1)S(1)}, bf16[384,256]{1,0:T(8,128)(2,1)S(1)}) custom-call(bf16[384,4096]{1,0:T(8,128)(2,1)} %bitcast.7, bf16[384,512]{1,0:T(8,128)(2,1)} %bitcast.29), custom_call_target="tpu_custom_call" | custom-call | flops 1 | bytes 1 | tf_op jit(solution)/shard_map/pallas_call | solution.py:234
  2.4 2.6 %collective-permute-start.3 = (bf16[384,768]{1,0:T(8,128)(2,1)S(1)}, bf16[384,768]{1,0:T(8,128)(2,1)S(1)}, u32[]{:S(2)}, u32[]{:S(2)}) collective-permute-start(bf16[384,768]{1,0:T(8,128)(2,1)S(1)} %get-tuple-element.44), channel_id=1, source_target_pairs={{0,1},{1,0},{2,3},{3,2},{4,5},{5,4},{6,7},{7,6},{8,9},{9,8},{10,11... | collective-permute-start | bytes 1769480 | tf_op jit(solution)/shard_map/ppermute | solution.py:273
  5.1 1.6 %collective-permute-start.5 = (f32[128,512]{1,0:T(8,128)S(1)}, f32[128,512]{1,0:T(8,128)S(1)}, u32[]{:S(2)}, u32[]{:S(2)}) collective-permute-start(f32[128,512]{1,0:T(8,128)S(1)} %get-tuple-element.46), channel_id=1, source_target_pairs={{0,16},{8,24},{16,0},{24,8},{1,17},{9,25},{17,1},{25,9},{2,18},{10... | collective-permute-start | bytes 786440 | tf_op jit(solution)/shard_map/ppermute | solution.py:284
  6.7 1.5 %collective-permute-start = (s32[1,384]{1,0:T(1,128)S(1)}, s32[1,384]{1,0:T(1,128)S(1)}, u32[]{:S(2)}, u32[]{:S(2)}) collective-permute-start(s32[1,384]{1,0:T(1,128)S(1)} %copy-done.5), channel_id=1, source_target_pairs={{0,1},{1,0},{2,3},{3,2},{4,5},{5,4},{6,7},{7,6},{8,9},{9,8},{10,11... | collective-permute-start | bytes 4616 | tf_op jit(solution)/shard_map/ppermute | solution.py:274
  8.2 0.6 collective-permute-start.1
  8.8 0.7 collective-permute-start.2
  9.5 1.3 %shard_map.115 = (bf16[384,512]{1,0:T(8,128)(2,1)S(1)}, bf16[384,512]{1,0:T(8,128)(2,1)S(1)}, bf16[384,512]{1,0:T(8,128)(2,1)S(1)}) custom-call(bf16[384,4096]{1,0:T(8,128)(2,1)} %bitcast.8), custom_call_target="tpu_custom_call" | custom-call | flops 1 | bytes 1 | tf_op jit(solution)/shard_map/pallas_call | solution.py:234
  10.8 8.1 %collective-permute-done.3.source.refs_0_ = bf16[384,768]{1,0:T(8,128)(2,1)S(1)} collective-permute-done((bf16[384,768]{1,0:T(8,128)(2,1)S(1)}, bf16[384,768]{1,0:T(8,128)(2,1)S(1)}, u32[]{:S(2)}, u32[]{:S(2)}) %collective-permute-start.3) | collective-permute-done | bytes 589856 | tf_op jit(solution)/shard_map/ppermute | solution.py:273
  19.0 1.8 %collective-permute-start.6 = (bf16[384,256]{1,0:T(8,128)(2,1)S(1)}, bf16[384,256]{1,0:T(8,128)(2,1)S(1)}, u32[]{:S(2)}, u32[]{:S(2)}) collective-permute-start(bf16[384,256]{1,0:T(8,128)(2,1)S(1)} %get-tuple-element.51), channel_id=1, source_target_pairs={{0,1},{1,0},{2,3},{3,2},{4,5},{5,4},{6,7},{7,6},{8,9},{9,8},{10,11... | collective-permute-start | bytes 589832 | tf_op jit(solution)/shard_map/ppermute | solution.py:301
  21.1 1.9 %collective-permute-start.7 = (f32[128,512]{1,0:T(8,128)S(1)}, f32[128,512]{1,0:T(8,128)S(1)}, u32[]{:S(2)}, u32[]{:S(2)}) collective-permute-start(f32[128,512]{1,0:T(8,128)S(1)} %get-tuple-element.85.params_base), channel_id=1, source_target_pairs={{0,16},{8,24},{16,0},{24,8},{1,17},{9,25},{17,1},{25,9},{2,18},{10... | collective-permute-start | bytes 786440 | tf_op jit(solution)/shard_map/ppermute | solution.py:292
  23.0 1.1 %shard_map.113 = (f32[64,384]{1,0:T(8,128)S(1)}, f32[64,384]{1,0:T(8,128)S(1)}, bf16[256,384]{1,0:T(8,128)(2,1)S(1)}, bf16[256,384]{1,0:T(8,128)(2,1)S(1)}) custom-call(s32[1,384]{1,0:T(1,128)S(1)} %copy-done.5, s32[1,384]{1,0:T(1,128)S(1)} %collective-permute-done.peer_doc, s32[1,384]{1,0:T(1,128)S(1)} %collective-permute-done.1.before_low, ...), custom_call_target="tpu_custom_call" | custom-call | flops 1 | bytes 1 | tf_op jit(solution)/shard_map/pallas_call | solution.py:234
  24.3 0.5 shard_map.117
  24.7 1.3 %collective-permute-start.8 = (bf16[256,512]{1,0:T(8,128)(2,1)S(1)}, bf16[256,512]{1,0:T(8,128)(2,1)S(1)}, u32[]{:S(2)}, u32[]{:S(2)}) collective-permute-start(bf16[256,512]{1,0:T(8,128)(2,1)S(1)} %shard_map.117), channel_id=1, source_target_pairs={{0,2},{2,0},{1,3},{3,1},{4,6},{6,4},{5,7},{7,5},{8,10},{10,8},{9,1... | collective-permute-start | bytes 786440 | tf_op jit(solution)/shard_map/ppermute | solution.py:336
  26.0 1.5 %collective-permute-start.12 = (bf16[384,512]{1,0:T(8,128)(2,1)S(1)}, bf16[384,512]{1,0:T(8,128)(2,1)S(1)}, u32[]{:S(2)}, u32[]{:S(2)}) collective-permute-start(bf16[384,512]{1,0:T(8,128)(2,1)S(1)} %get-tuple-element.63), channel_id=1, source_target_pairs={{0,1},{1,0},{2,3},{3,2},{4,5},{5,4},{6,7},{7,6},{8,9},{9,8},{10,11... | collective-permute-start | bytes 1179656 | tf_op jit(solution)/shard_map/ppermute | solution.py:310
  27.6 0.5 shard_map.118
  28.1 0.8 %collective-permute-start.11 = (bf16[256,512]{1,0:T(8,128)(2,1)S(1)}, bf16[256,512]{1,0:T(8,128)(2,1)S(1)}, u32[]{:S(2)}, u32[]{:S(2)}) collective-permute-start(bf16[256,512]{1,0:T(8,128)(2,1)S(1)} %shard_map.118), channel_id=1, source_target_pairs={{0,2},{2,0},{1,3},{3,1},{4,6},{6,4},{5,7},{7,5},{8,10},{10,8},{9,1... | collective-permute-start | bytes 786440 | tf_op jit(solution)/shard_map/ppermute | solution.py:336
  28.9 5.1 %collective-permute-done.8.refs_1_ = bf16[256,512]{1,0:T(8,128)(2,1)S(1)} collective-permute-done((bf16[256,512]{1,0:T(8,128)(2,1)S(1)}, bf16[256,512]{1,0:T(8,128)(2,1)S(1)}, u32[]{:S(2)}, u32[]{:S(2)}) %collective-permute-start.8) | collective-permute-done | bytes 262176 | tf_op jit(solution)/shard_map/ppermute | solution.py:336
  34.1 0.7 collective-permute-start.13
  35.2 0.4 shard_map.120
  35.6 3.7 %collective-permute-start.14 = (bf16[256,512]{1,0:T(8,128)(2,1)S(1)}, bf16[256,512]{1,0:T(8,128)(2,1)S(1)}, u32[]{:S(2)}, u32[]{:S(2)}) collective-permute-start(bf16[256,512]{1,0:T(8,128)(2,1)S(1)} %shard_map.120), channel_id=1, source_target_pairs={{0,2},{2,0},{1,3},{3,1},{4,6},{6,4},{5,7},{7,5},{8,10},{10,8},{9,1... | collective-permute-start | bytes 786440 | tf_op jit(solution)/shard_map/ppermute | solution.py:336
  39.3 1.5 %collective-permute-start.10 = (bf16[384,512]{1,0:T(8,128)(2,1)S(1)}, bf16[384,512]{1,0:T(8,128)(2,1)S(1)}, u32[]{:S(2)}, u32[]{:S(2)}) collective-permute-start(bf16[384,512]{1,0:T(8,128)(2,1)S(1)} %get-tuple-element.58), channel_id=1, source_target_pairs={{0,1},{1,0},{2,3},{3,2},{4,5},{5,4},{6,7},{7,6},{8,9},{9,8},{10,11... | collective-permute-start | bytes 1179656 | tf_op jit(solution)/shard_map/ppermute | solution.py:310
  40.8 0.7 collective-permute-start.15
  41.5 0.5 shard_map.123
  41.9 1.6 %collective-permute-done.12.refs_1_ = bf16[384,512]{1,0:T(8,128)(2,1)S(1)} collective-permute-done((bf16[384,512]{1,0:T(8,128)(2,1)S(1)}, bf16[384,512]{1,0:T(8,128)(2,1)S(1)}, u32[]{:S(2)}, u32[]{:S(2)}) %collective-permute-start.12) | collective-permute-done | bytes 393248 | tf_op jit(solution)/shard_map/ppermute | solution.py:310
  43.6 1.9 %collective-permute-start.17 = (bf16[256,512]{1,0:T(8,128)(2,1)S(1)}, bf16[256,512]{1,0:T(8,128)(2,1)S(1)}, u32[]{:S(2)}, u32[]{:S(2)}) collective-permute-start(bf16[256,512]{1,0:T(8,128)(2,1)S(1)} %shard_map.123), channel_id=1, source_target_pairs={{0,2},{2,0},{1,3},{3,1},{4,6},{6,4},{5,7},{7,5},{8,10},{10,8},{9,1... | collective-permute-start | bytes 786440 | tf_op jit(solution)/shard_map/ppermute | solution.py:336
  45.5 0.4 shard_map.124
  46.3 0.7 collective-permute-start.21
  47.0 0.5 shard_map.126
  47.5 5.0 %collective-permute-start.16 = (bf16[256,512]{1,0:T(8,128)(2,1)S(1)}, bf16[256,512]{1,0:T(8,128)(2,1)S(1)}, u32[]{:S(2)}, u32[]{:S(2)}) collective-permute-start(bf16[256,512]{1,0:T(8,128)(2,1)S(1)} %shard_map.126), channel_id=1, source_target_pairs={{0,2},{2,0},{1,3},{3,1},{4,6},{6,4},{5,7},{7,5},{8,10},{10,8},{9,1... | collective-permute-start | bytes 786440 | tf_op jit(solution)/shard_map/ppermute | solution.py:336
  52.9 0.8 %collective-permute-start.18 = (bf16[256,512]{1,0:T(8,128)(2,1)S(1)}, bf16[256,512]{1,0:T(8,128)(2,1)S(1)}, u32[]{:S(2)}, u32[]{:S(2)}) collective-permute-start(bf16[256,512]{1,0:T(8,128)(2,1)S(1)} %shard_map.127), channel_id=1, source_target_pairs={{2,4},{4,2},{3,5},{5,3},{10,12},{12,10},{11,13},{13,11},{18,20},{2... | collective-permute-start | bytes 786440 | tf_op jit(solution)/shard_map/ppermute | solution.py:336
  53.7 0.4 shard_map.129.total
  54.2 3.9 %collective-permute-done.20.even = bf16[256,512]{1,0:T(8,128)(2,1)S(1)} collective-permute-done((bf16[256,512]{1,0:T(8,128)(2,1)S(1)}, bf16[256,512]{1,0:T(8,128)(2,1)S(1)}, u32[]{:S(2)}, u32[]{:S(2)}) %collective-permute-start.20) | collective-permute-done | bytes 262176 | tf_op jit(solution)/shard_map/ppermute | solution.py:336
  58.0 0.4 shard_map.130
  58.6 0.4 shard_map.121.total
  59.0 1.8 %collective-permute-done.16.even = bf16[256,512]{1,0:T(8,128)(2,1)S(1)} collective-permute-done((bf16[256,512]{1,0:T(8,128)(2,1)S(1)}, bf16[256,512]{1,0:T(8,128)(2,1)S(1)}, u32[]{:S(2)}, u32[]{:S(2)}) %collective-permute-start.16) | collective-permute-done | bytes 262176 | tf_op jit(solution)/shard_map/ppermute | solution.py:336
  60.8 0.4 shard_map.128
  61.4 1.4 %collective-permute-start.24 = (bf16[2,128,256]{2,1,0:T(8,128)(2,1)S(1)}, bf16[2,128,256]{2,1,0:T(8,128)(2,1)S(1)}, u32[]{:S(2)}, u32[]{:S(2)}) collective-permute-start(bf16[2,128,256]{2,1,0:T(8,128)(2,1)S(1)} %add_convert_fusion.both), channel_id=1, source_target_pairs={{0,16},{8,24},{16,0},{24,8},{1,17},{9,25},{17,1},{25,9},{2,18},{10... | collective-permute-start | bytes 393224 | tf_op jit(solution)/shard_map/ppermute | solution.py:361
  62.9 1.3 %collective-permute-start.23 = (bf16[2,128,256]{2,1,0:T(8,128)(2,1)S(1)}, bf16[2,128,256]{2,1,0:T(8,128)(2,1)S(1)}, u32[]{:S(2)}, u32[]{:S(2)}) collective-permute-start(bf16[2,128,256]{2,1,0:T(8,128)(2,1)S(1)} %add_convert_fusion.1.both), channel_id=1, source_target_pairs={{0,16},{8,24},{16,0},{24,8},{1,17},{9,25},{17,1},{25,9},{2,18},{10... | collective-permute-start | bytes 393224 | tf_op jit(solution)/shard_map/ppermute | solution.py:361
  64.1 1.2 %shard_map.131 = (f32[512,512]{1,0:T(8,128)}, f32[512,512]{1,0:T(8,128)}, f32[8,128]{1,0:T(8,128)S(1)}) custom-call(f32[256,512]{1,0:T(8,128)S(1)} %shard_map.129.total, bf16[256,512]{1,0:T(8,128)(2,1)S(1)} %collective-permute-done.20.even, bf16[256,512]{1,0:T(8,128)(2,1)S(1)} %collective-permute-done.21.odd, f32[512,512]{1,0:T(8,128)S(1)} %bitcast.23, ...), custom_call_target="tpu_custom_call" | custom-call | flops 1 | bytes 3145728 | tf_op jit(solution)/shard_map/pallas_call | solution.py:234
  65.4 1.2 %shard_map.132 = (f32[512,512]{1,0:T(8,128)}, f32[512,512]{1,0:T(8,128)}, f32[8,128]{1,0:T(8,128)S(1)}) custom-call(f32[256,512]{1,0:T(8,128)S(1)} %shard_map.121.total, bf16[256,512]{1,0:T(8,128)(2,1)S(1)} %collective-permute-done.16.even, bf16[256,512]{1,0:T(8,128)(2,1)S(1)} %collective-permute-done.18.odd, ...), custom_call_target="tpu_custom_call", output_to_operand_aliasing={{0}: (5, {}), {1}: (6, {})} | custom-call | flops 1 | bytes 3145728 | tf_op jit(solution)/shard_map/pallas_call | solution.py:234
  66.6 1.2 %collective-permute-done.24.came = bf16[2,128,256]{2,1,0:T(8,128)(2,1)S(1)} collective-permute-done((bf16[2,128,256]{2,1,0:T(8,128)(2,1)S(1)}, bf16[2,128,256]{2,1,0:T(8,128)(2,1)S(1)}, u32[]{:S(2)}, u32[]{:S(2)}) %collective-permute-start.24) | collective-permute-done | bytes 131104 | tf_op jit(solution)/shard_map/ppermute | solution.py:361
  67.8 0.7 shard_map.133
  68.5 1.7 %collective-permute-done.23.came = bf16[2,128,256]{2,1,0:T(8,128)(2,1)S(1)} collective-permute-done((bf16[2,128,256]{2,1,0:T(8,128)(2,1)S(1)}, bf16[2,128,256]{2,1,0:T(8,128)(2,1)S(1)}, u32[]{:S(2)}, u32[]{:S(2)}) %collective-permute-start.23) | collective-permute-done | bytes 131104 | tf_op jit(solution)/shard_map/ppermute | solution.py:361
  70.2 0.7 shard_map.134
  70.9 0.8 %shard_map.135.refs_0_ = f32[512,512]{1,0:T(8,128)} custom-call(f32[2,128,256]{2,1,0:T(8,128)S(1)} %get-tuple-element.83.mine, f32[2,128,256]{2,1,0:T(8,128)S(1)} %collective-permute-done.26.theirs), custom_call_target="tpu_custom_call" | custom-call | flops 1 | bytes 1 | tf_op jit(solution)/shard_map/pallas_call | solution.py:234
  71.7 0.7 collective-permute-done.25.theirs
  72.4 0.8 %shard_map.136 = f32[512,512]{1,0:T(8,128)} custom-call(f32[2,128,256]{2,1,0:T(8,128)S(1)} %get-tuple-element.82.mine, f32[2,128,256]{2,1,0:T(8,128)S(1)} %collective-permute-done.25.theirs, f32[512,512]{1,0:T(8,128)} %shard_map.135.refs_0_), custom_call_target="tpu_custom_call", output_to_operand_aliasing={{}: (2, {})} | custom-call | flops 1 | bytes 1 | tf_op jit(solution)/shard_map/pallas_call | solution.py:234
  (51 shorter events, 2.2 us)
Async XLA Ops:
  0.6 4.4 %copy-start.4 = (f32[1,512,512]{2,1,0:T(8,128)S(1)}, f32[1,512,512]{2,1,0:T(8,128)}, u32[]{:S(2)}) copy-start(f32[1,512,512]{2,1,0:T(8,128)} %param.11) | copy-start | bytes 3145732
  0.6 6.1 %copy-start.5 = (s32[1,384]{1,0:T(1,128)S(1)}, s32[1,384]{1,0:T(1,128)}, u32[]{:S(2)}) copy-start(s32[1,384]{1,0:T(1,128)} %own_doc.1) | copy-start | bytes 4612
  0.7 4.4 %collective-permute-start.4 = (f32[512,512]{1,0:T(8,128)}, f32[512,512]{1,0:T(8,128)S(1)}, u32[]{:S(2)}, u32[]{:S(2)}) collective-permute-start(f32[512,512]{1,0:T(8,128)} %bitcast.31), channel_id=1, source_target_pairs={{0,8},{8,0},{16,24},{24,16},{1,9},{9,1},{17,25},{25,17},{2,10},{10... | collective-permute-start | bytes 3145736 | tf_op jit(solution)/shard_map/ppermute | solution.py:281
  2.3 18.6 %copy-start.6 = (f32[128,512]{1,0:T(8,128)S(1)}, f32[128,512]{1,0:T(8,128)}, u32[]{:S(2)}) copy-start(f32[128,512]{1,0:T(8,128)} %param.15) | copy-start | bytes 786436
  2.4 18.6 %copy-start.7 = (f32[128,512]{1,0:T(8,128)S(1)}, f32[128,512]{1,0:T(8,128)}, u32[]{:S(2)}) copy-start(f32[128,512]{1,0:T(8,128)} %param.14) | copy-start | bytes 786436
  2.4 20.6 %copy-start.3 = (bf16[1,384,512]{2,1,0:T(8,128)(2,1)S(1)}, bf16[1,384,512]{2,1,0:T(8,128)(2,1)}, u32[]{:S(2)}) copy-start(bf16[1,384,512]{2,1,0:T(8,128)(2,1)} %param.9) | copy-start | bytes 1179652
  2.4 16.6 %collective-permute-start.3 = (bf16[384,768]{1,0:T(8,128)(2,1)S(1)}, bf16[384,768]{1,0:T(8,128)(2,1)S(1)}, u32[]{:S(2)}, u32[]{:S(2)}) collective-permute-start(bf16[384,768]{1,0:T(8,128)(2,1)S(1)} %get-tuple-element.44), channel_id=1, source_target_pairs={{0,1},{1,0},{2,3},{3,2},{4,5},{5,4},{6,7},{7,6},{8,9},{9,8},{10,11... | collective-permute-start | bytes 1769480 | tf_op jit(solution)/shard_map/ppermute | solution.py:273
  5.1 19.2 %copy-start = (bf16[1,384,4096]{2,1,0:T(8,128)(2,1)S(1)}, bf16[1,384,4096]{2,1,0:T(8,128)(2,1)}, u32[]{:S(2)}) copy-start(bf16[1,384,4096]{2,1,0:T(8,128)(2,1)} %param.8) | copy-start | bytes 9437188
  5.1 15.6 %collective-permute-start.5 = (f32[128,512]{1,0:T(8,128)S(1)}, f32[128,512]{1,0:T(8,128)S(1)}, u32[]{:S(2)}, u32[]{:S(2)}) collective-permute-start(f32[128,512]{1,0:T(8,128)S(1)} %get-tuple-element.46), channel_id=1, source_target_pairs={{0,16},{8,24},{16,0},{24,8},{1,17},{9,25},{17,1},{25,9},{2,18},{10... | collective-permute-start | bytes 786440 | tf_op jit(solution)/shard_map/ppermute | solution.py:284
  6.7 14.4 %collective-permute-start = (s32[1,384]{1,0:T(1,128)S(1)}, s32[1,384]{1,0:T(1,128)S(1)}, u32[]{:S(2)}, u32[]{:S(2)}) collective-permute-start(s32[1,384]{1,0:T(1,128)S(1)} %copy-done.5), channel_id=1, source_target_pairs={{0,1},{1,0},{2,3},{3,2},{4,5},{5,4},{6,7},{7,6},{8,9},{9,8},{10,11... | collective-permute-start | bytes 4616 | tf_op jit(solution)/shard_map/ppermute | solution.py:274
  8.2 14.8 %collective-permute-start.1 = (s32[1,384]{1,0:T(1,128)S(1)}, s32[1,384]{1,0:T(1,128)S(1)}, u32[]{:S(2)}, u32[]{:S(2)}) collective-permute-start(s32[1,384]{1,0:T(1,128)S(1)} %copy-done.5), channel_id=1, source_target_pairs={{1,2},{3,4},{5,6},{9,10},{11,12},{13,14},{17,18},{19,20},{21,22},{... | collective-permute-start | bytes 4616 | tf_op jit(solution)/shard_map/ppermute | solution.py:275
  8.8 14.1 %collective-permute-start.2 = (s32[1,384]{1,0:T(1,128)S(1)}, s32[1,384]{1,0:T(1,128)S(1)}, u32[]{:S(2)}, u32[]{:S(2)}) collective-permute-start(s32[1,384]{1,0:T(1,128)S(1)} %copy-done.5), channel_id=1, source_target_pairs={{1,3},{3,5},{5,7},{9,11},{11,13},{13,15},{17,19},{19,21},{21,23},{... | collective-permute-start | bytes 4616 | tf_op jit(solution)/shard_map/ppermute | solution.py:276
  19.0 8.5 %collective-permute-start.6 = (bf16[384,256]{1,0:T(8,128)(2,1)S(1)}, bf16[384,256]{1,0:T(8,128)(2,1)S(1)}, u32[]{:S(2)}, u32[]{:S(2)}) collective-permute-start(bf16[384,256]{1,0:T(8,128)(2,1)S(1)} %get-tuple-element.51), channel_id=1, source_target_pairs={{0,1},{1,0},{2,3},{3,2},{4,5},{5,4},{6,7},{7,6},{8,9},{9,8},{10,11... | collective-permute-start | bytes 589832 | tf_op jit(solution)/shard_map/ppermute | solution.py:301
  20.7 14.5 %collective-permute-start.9 = (bf16[384,512]{1,0:T(8,128)(2,1)S(1)}, bf16[384,512]{1,0:T(8,128)(2,1)S(1)}, u32[]{:S(2)}, u32[]{:S(2)}) collective-permute-start(bf16[384,512]{1,0:T(8,128)(2,1)S(1)} %get-tuple-element.57), channel_id=1, source_target_pairs={{0,1},{1,0},{2,3},{3,2},{4,5},{5,4},{6,7},{7,6},{8,9},{9,8},{10,11... | collective-permute-start | bytes 1179656 | tf_op jit(solution)/shard_map/ppermute | solution.py:310
  21.1 7.8 %collective-permute-start.7 = (f32[128,512]{1,0:T(8,128)S(1)}, f32[128,512]{1,0:T(8,128)S(1)}, u32[]{:S(2)}, u32[]{:S(2)}) collective-permute-start(f32[128,512]{1,0:T(8,128)S(1)} %get-tuple-element.85.params_base), channel_id=1, source_target_pairs={{0,16},{8,24},{16,0},{24,8},{1,17},{9,25},{17,1},{25,9},{2,18},{10... | collective-permute-start | bytes 786440 | tf_op jit(solution)/shard_map/ppermute | solution.py:292
  24.7 9.3 %collective-permute-start.8 = (bf16[256,512]{1,0:T(8,128)(2,1)S(1)}, bf16[256,512]{1,0:T(8,128)(2,1)S(1)}, u32[]{:S(2)}, u32[]{:S(2)}) collective-permute-start(bf16[256,512]{1,0:T(8,128)(2,1)S(1)} %shard_map.117), channel_id=1, source_target_pairs={{0,2},{2,0},{1,3},{3,1},{4,6},{6,4},{5,7},{7,5},{8,10},{10,8},{9,1... | collective-permute-start | bytes 786440 | tf_op jit(solution)/shard_map/ppermute | solution.py:336
  26.0 17.6 %collective-permute-start.12 = (bf16[384,512]{1,0:T(8,128)(2,1)S(1)}, bf16[384,512]{1,0:T(8,128)(2,1)S(1)}, u32[]{:S(2)}, u32[]{:S(2)}) collective-permute-start(bf16[384,512]{1,0:T(8,128)(2,1)S(1)} %get-tuple-element.63), channel_id=1, source_target_pairs={{0,1},{1,0},{2,3},{3,2},{4,5},{5,4},{6,7},{7,6},{8,9},{9,8},{10,11... | collective-permute-start | bytes 1179656 | tf_op jit(solution)/shard_map/ppermute | solution.py:310
  28.1 12.7 %collective-permute-start.11 = (bf16[256,512]{1,0:T(8,128)(2,1)S(1)}, bf16[256,512]{1,0:T(8,128)(2,1)S(1)}, u32[]{:S(2)}, u32[]{:S(2)}) collective-permute-start(bf16[256,512]{1,0:T(8,128)(2,1)S(1)} %shard_map.118), channel_id=1, source_target_pairs={{0,2},{2,0},{1,3},{3,1},{4,6},{6,4},{5,7},{7,5},{8,10},{10,8},{9,1... | collective-permute-start | bytes 786440 | tf_op jit(solution)/shard_map/ppermute | solution.py:336
  34.1 11.4 %collective-permute-start.13 = (bf16[256,512]{1,0:T(8,128)(2,1)S(1)}, bf16[256,512]{1,0:T(8,128)(2,1)S(1)}, u32[]{:S(2)}, u32[]{:S(2)}) collective-permute-start(bf16[256,512]{1,0:T(8,128)(2,1)S(1)} %shard_map.119), channel_id=1, source_target_pairs={{2,4},{4,2},{3,5},{5,3},{10,12},{12,10},{11,13},{13,11},{18,20},{2... | collective-permute-start | bytes 786440 | tf_op jit(solution)/shard_map/ppermute | solution.py:336
  35.6 10.7 %collective-permute-start.14 = (bf16[256,512]{1,0:T(8,128)(2,1)S(1)}, bf16[256,512]{1,0:T(8,128)(2,1)S(1)}, u32[]{:S(2)}, u32[]{:S(2)}) collective-permute-start(bf16[256,512]{1,0:T(8,128)(2,1)S(1)} %shard_map.120), channel_id=1, source_target_pairs={{0,2},{2,0},{1,3},{3,1},{4,6},{6,4},{5,7},{7,5},{8,10},{10,8},{9,1... | collective-permute-start | bytes 786440 | tf_op jit(solution)/shard_map/ppermute | solution.py:336
  39.3 14.4 %collective-permute-start.10 = (bf16[384,512]{1,0:T(8,128)(2,1)S(1)}, bf16[384,512]{1,0:T(8,128)(2,1)S(1)}, u32[]{:S(2)}, u32[]{:S(2)}) collective-permute-start(bf16[384,512]{1,0:T(8,128)(2,1)S(1)} %get-tuple-element.58), channel_id=1, source_target_pairs={{0,1},{1,0},{2,3},{3,2},{4,5},{5,4},{6,7},{7,6},{8,9},{9,8},{10,11... | collective-permute-start | bytes 1179656 | tf_op jit(solution)/shard_map/ppermute | solution.py:310
  40.8 6.2 %collective-permute-start.15 = (bf16[256,512]{1,0:T(8,128)(2,1)S(1)}, bf16[256,512]{1,0:T(8,128)(2,1)S(1)}, u32[]{:S(2)}, u32[]{:S(2)}) collective-permute-start(bf16[256,512]{1,0:T(8,128)(2,1)S(1)} %shard_map.122), channel_id=1, source_target_pairs={{2,4},{4,2},{3,5},{5,3},{10,12},{12,10},{11,13},{13,11},{18,20},{2... | collective-permute-start | bytes 786440 | tf_op jit(solution)/shard_map/ppermute | solution.py:336
  43.6 9.2 %collective-permute-start.17 = (bf16[256,512]{1,0:T(8,128)(2,1)S(1)}, bf16[256,512]{1,0:T(8,128)(2,1)S(1)}, u32[]{:S(2)}, u32[]{:S(2)}) collective-permute-start(bf16[256,512]{1,0:T(8,128)(2,1)S(1)} %shard_map.123), channel_id=1, source_target_pairs={{0,2},{2,0},{1,3},{3,1},{4,6},{6,4},{5,7},{7,5},{8,10},{10,8},{9,1... | collective-permute-start | bytes 786440 | tf_op jit(solution)/shard_map/ppermute | solution.py:336
  45.9 12.1 %collective-permute-start.20 = (bf16[256,512]{1,0:T(8,128)(2,1)S(1)}, bf16[256,512]{1,0:T(8,128)(2,1)S(1)}, u32[]{:S(2)}, u32[]{:S(2)}) collective-permute-start(bf16[256,512]{1,0:T(8,128)(2,1)S(1)} %shard_map.124), channel_id=1, source_target_pairs={{0,2},{2,0},{1,3},{3,1},{4,6},{6,4},{5,7},{7,5},{8,10},{10,8},{9,1... | collective-permute-start | bytes 786440 | tf_op jit(solution)/shard_map/ppermute | solution.py:336
  46.3 11.7 %collective-permute-start.21 = (bf16[256,512]{1,0:T(8,128)(2,1)S(1)}, bf16[256,512]{1,0:T(8,128)(2,1)S(1)}, u32[]{:S(2)}, u32[]{:S(2)}) collective-permute-start(bf16[256,512]{1,0:T(8,128)(2,1)S(1)} %shard_map.125), channel_id=1, source_target_pairs={{2,4},{4,2},{3,5},{5,3},{10,12},{12,10},{11,13},{13,11},{18,20},{2... | collective-permute-start | bytes 786440 | tf_op jit(solution)/shard_map/ppermute | solution.py:336
  47.5 13.4 %collective-permute-start.16 = (bf16[256,512]{1,0:T(8,128)(2,1)S(1)}, bf16[256,512]{1,0:T(8,128)(2,1)S(1)}, u32[]{:S(2)}, u32[]{:S(2)}) collective-permute-start(bf16[256,512]{1,0:T(8,128)(2,1)S(1)} %shard_map.126), channel_id=1, source_target_pairs={{0,2},{2,0},{1,3},{3,1},{4,6},{6,4},{5,7},{7,5},{8,10},{10,8},{9,1... | collective-permute-start | bytes 786440 | tf_op jit(solution)/shard_map/ppermute | solution.py:336
  52.9 5.2 %copy-start.1 = (f32[1,512,512]{2,1,0:T(8,128)S(1)}, f32[1,512,512]{2,1,0:T(8,128)}, u32[]{:S(2)}) copy-start(f32[1,512,512]{2,1,0:T(8,128)} %param.12) | copy-start | bytes 3145732
  52.9 5.1 %copy-start.2 = (f32[1,512,512]{2,1,0:T(8,128)S(1)}, f32[1,512,512]{2,1,0:T(8,128)}, u32[]{:S(2)}) copy-start(f32[1,512,512]{2,1,0:T(8,128)} %param.13) | copy-start | bytes 3145732
  52.9 7.9 %collective-permute-start.18 = (bf16[256,512]{1,0:T(8,128)(2,1)S(1)}, bf16[256,512]{1,0:T(8,128)(2,1)S(1)}, u32[]{:S(2)}, u32[]{:S(2)}) collective-permute-start(bf16[256,512]{1,0:T(8,128)(2,1)S(1)} %shard_map.127), channel_id=1, source_target_pairs={{2,4},{4,2},{3,5},{5,3},{10,12},{12,10},{11,13},{13,11},{18,20},{2... | collective-permute-start | bytes 786440 | tf_op jit(solution)/shard_map/ppermute | solution.py:336
  58.5 2.9 %collective-permute-start.22 = (bf16[2,128,256]{2,1,0:T(8,128)(2,1)S(1)}, bf16[2,128,256]{2,1,0:T(8,128)(2,1)S(1)}, u32[]{:S(2)}, u32[]{:S(2)}) collective-permute-start(bf16[2,128,256]{2,1,0:T(8,128)(2,1)S(1)} %get-tuple-element.72), channel_id=1, source_target_pairs={{0,8},{8,0},{16,24},{24,16},{1,9},{9,1},{17,25},{25,17},{2,10},{10... | collective-permute-start | bytes 393224 | tf_op jit(solution)/shard_map/ppermute | solution.py:351
  61.3 1.6 %collective-permute-start.19 = (bf16[2,128,256]{2,1,0:T(8,128)(2,1)S(1)}, bf16[2,128,256]{2,1,0:T(8,128)(2,1)S(1)}, u32[]{:S(2)}, u32[]{:S(2)}) collective-permute-start(bf16[2,128,256]{2,1,0:T(8,128)(2,1)S(1)} %get-tuple-element.68), channel_id=1, source_target_pairs={{0,8},{8,0},{16,24},{24,16},{1,9},{9,1},{17,25},{25,17},{2,10},{10... | collective-permute-start | bytes 393224 | tf_op jit(solution)/shard_map/ppermute | solution.py:351
  61.4 6.4 %collective-permute-start.24 = (bf16[2,128,256]{2,1,0:T(8,128)(2,1)S(1)}, bf16[2,128,256]{2,1,0:T(8,128)(2,1)S(1)}, u32[]{:S(2)}, u32[]{:S(2)}) collective-permute-start(bf16[2,128,256]{2,1,0:T(8,128)(2,1)S(1)} %add_convert_fusion.both), channel_id=1, source_target_pairs={{0,16},{8,24},{16,0},{24,8},{1,17},{9,25},{17,1},{25,9},{2,18},{10... | collective-permute-start | bytes 393224 | tf_op jit(solution)/shard_map/ppermute | solution.py:361
  62.9 7.3 %collective-permute-start.23 = (bf16[2,128,256]{2,1,0:T(8,128)(2,1)S(1)}, bf16[2,128,256]{2,1,0:T(8,128)(2,1)S(1)}, u32[]{:S(2)}, u32[]{:S(2)}) collective-permute-start(bf16[2,128,256]{2,1,0:T(8,128)(2,1)S(1)} %add_convert_fusion.1.both), channel_id=1, source_target_pairs={{0,16},{8,24},{16,0},{24,8},{1,17},{9,25},{17,1},{25,9},{2,18},{10... | collective-permute-start | bytes 393224 | tf_op jit(solution)/shard_map/ppermute | solution.py:361
  68.5 2.4 %collective-permute-start.26 = (f32[2,128,256]{2,1,0:T(8,128)S(1)}, f32[2,128,256]{2,1,0:T(8,128)S(1)}, u32[]{:S(2)}, u32[]{:S(2)}) collective-permute-start(f32[2,128,256]{2,1,0:T(8,128)S(1)} %get-tuple-element.83.mine), channel_id=1, source_target_pairs={{0,8},{8,0},{16,24},{24,16},{1,9},{9,1},{17,25},{25,17},{2,10},{10... | collective-permute-start | bytes 786440 | tf_op jit(solution)/shard_map/ppermute | solution.py:375
  70.9 1.5 %collective-permute-start.25 = (f32[2,128,256]{2,1,0:T(8,128)S(1)}, f32[2,128,256]{2,1,0:T(8,128)S(1)}, u32[]{:S(2)}, u32[]{:S(2)}) collective-permute-start(f32[2,128,256]{2,1,0:T(8,128)S(1)} %get-tuple-element.82.mine), channel_id=1, source_target_pairs={{0,8},{8,0},{16,24},{24,16},{1,9},{9,1},{17,25},{25,17},{2,10},{10... | collective-permute-start | bytes 786440 | tf_op jit(solution)/shard_map/ppermute | solution.py:375

commit v5 on v4

--- a/solution.py
+++ b/solution.py
@@ -90,7 +90,18 @@
         out[head * HEAD + half : (head + 1) * HEAD, :] = (high * cosine - low * sine).astype(BF16)
 
 
-def rotate_kernel(own_doc, peer_doc, before_low, before_high, cotangent, peer_cosine, peer_sine, *outs):
+def frequencies():
+    half = HEAD // 2
+    steps = lax.broadcasted_iota(jnp.int32, (half, 1), 0).astype(F32)
+    return jnp.exp(steps * (-math.log(ROPE_BASE) / half))
+
+
+def table_kernel(doc, cosine, sine):
+    angles = frequencies() * lax.broadcasted_iota(jnp.int32, (1, doc.shape[1]), 1).astype(F32)
+    cosine[...], sine[...] = jnp.cos(angles), jnp.sin(angles)
+
+
+def rotate_kernel(own_doc, peer_doc, before_low, before_high, cotangent, cosines, sines, peer_cosine, peer_sine, *outs):
     tokens = own_doc.shape[1]
     x = lax.rem(lax.axis_index("fsdp"), 2)
 
@@ -101,21 +112,24 @@
     own, peer = start(own_doc[...]), start(peer_doc[...])
     before = start(jnp.where(x == 0, before_low[...], before_high[...]))
     places = lax.broadcasted_iota(jnp.int32, (1, tokens), 1)
-    half = HEAD // 2
-    steps = lax.broadcasted_iota(jnp.int32, (half, 1), 0).astype(F32)
-    frequency = jnp.exp(steps * (-math.log(ROPE_BASE) / half))
-
-    def angles(first, carried):
-        offsets = jnp.where(places >= first, places - first, places + tokens - carried)
-        return frequency * offsets.astype(F32)
-
-    turned = angles(own, jnp.where(x == 0, before, peer))
-    cosine, sine = jnp.cos(turned), jnp.sin(turned)
+    lanes = lax.broadcasted_iota(jnp.int32, (1, 128), 1)
+    own_far = tokens - jnp.where(x == 0, before, peer)
+    peer_far = tokens - jnp.where(x == 0, own, before)
+    shifts = jnp.where(lanes == 0, -own, jnp.where(lanes == 1, own_far, jnp.where(lanes == 2, -peer, peer_far)))
+    turns = frequencies() * shifts.astype(F32)
+    shift_cosine, shift_sine = jnp.cos(turns), jnp.sin(turns)
+
+    def table(first, lane):
+        late = places >= first
+        c = jnp.where(late, shift_cosine[:, lane : lane + 1], shift_cosine[:, lane + 1 : lane + 2])
+        s = jnp.where(late, shift_sine[:, lane : lane + 1], shift_sine[:, lane + 1 : lane + 2])
+        return cosines[...] * c - sines[...] * s, sines[...] * c + cosines[...] * s
+
+    cosine, sine = table(own, 0)
     width = outs[0].shape[0]
     for part, out in enumerate(outs):
         turn(cosine, sine, cotangent[:, part * width : (part + 1) * width], out)
-    turned = angles(peer, jnp.where(x == 0, own, before))
-    peer_cosine[...], peer_sine[...] = jnp.cos(turned), jnp.sin(turned)
+    peer_cosine[...], peer_sine[...] = table(peer, 2)
 
 
 def peer_kernel(cosine, sine, source, out):
@@ -294,8 +308,9 @@
         bases = lax.all_gather(params_base, "rep", axis_index_groups=groups)
 
     half = ((HEAD // 2, tokens), F32)
+    cosines, sines = call(table_kernel, [doc_ids], [half] * 2)
     peer_cosine, peer_sine, *own = call(
-        rotate_kernel, [doc_ids, peer_doc, before_low, before_high, after(cotangent, pieces[0], params_base)],
+        rotate_kernel, [doc_ids, peer_doc, before_low, before_high, after(cotangent, pieces[0], params_base), cosines, sines],
         [half, half] + [((width, tokens), BF16)] * HALVES,
     )
     raw = [pieces[0]] + [lax.ppermute(part, "fsdp", pair) for part in raw]

time: 73.6 us -> 73.6 us (level)
    pallas_call x26 -> x27, Pallas kernels: 14 us -> 14.2 us  [call(): pl.pallas_call(kernel, grid=(1,), in_specs=[pl.BlockSpec(memory_space=spa...]
where the time goes in v5:
time: 73.6 us; the launch traced here: 73.2 us
  starting transfers between devices  33.1 us (45%)
  waiting for transfers between devices  24.7 us (34%)
  Pallas kernels  14.2 us (19%)
  between operations  1 us (1%)
    ppermute x10, starting transfers between devices, local(): came[h][side] = lax.ppermute(last, 'fsdp', odds if side else evens)  15.9 us
    pallas_call x27, Pallas kernels, call(): pl.pallas_call(kernel, grid=(1,), in_specs=[pl.BlockSpec(memory_space=spa...  14.2 us
    ppermute x10, waiting for transfers between devices, local(): came[h][side] = lax.ppermute(last, 'fsdp', odds if side else evens)  10.9 us
    ppermute x1, waiting for transfers between devices, local(): pieces = [lax.ppermute(first_piece, 'fsdp', pair)]  7.62 us
    ppermute x3, starting transfers between devices, exchange(): pieces.append(lax.ppermute(after(later[k - 1], *done), 'fsdp', pair))  3.19 us
    ppermute x2, waiting for transfers between devices, local(): lax.ppermute(both, 'rep', across)  2.84 us
    ppermute x2, starting transfers between devices, local(): lax.ppermute(both, 'rep', across)  2.71 us
    ppermute x3, waiting for transfers between devices, exchange(): pieces.append(lax.ppermute(after(later[k - 1], *done), 'fsdp', pair))  2.69 us
  transfers between devices with their start and end apart: 27, of which 10 were waited for; matrix products, arithmetic and copies ran while one was open for 0% of the time, Pallas kernels for 18%

profile of v5, /device:TPU:0, one launch (start us, length us, event | category | flops | bytes accessed | tf_op | source)
XLA Modules:
  0.0 73.2 jit_solution(14420584796472660561)
XLA Ops:
  0.7 0.5 collective-permute-start.4
  1.2 1.2 %shard_map.111 = (bf16[384,768]{1,0:T(8,128)(2,1)S(1)}, bf16[384,256]{1,0:T(8,128)(2,1)S(1)}) custom-call(bf16[384,4096]{1,0:T(8,128)(2,1)} %bitcast.7, bf16[384,512]{1,0:T(8,128)(2,1)} %bitcast.29), custom_call_target="tpu_custom_call" | custom-call | flops 1 | bytes 1 | tf_op jit(solution)/shard_map/pallas_call | solution.py:248
  2.4 2.6 %collective-permute-start.3 = (bf16[384,768]{1,0:T(8,128)(2,1)S(1)}, bf16[384,768]{1,0:T(8,128)(2,1)S(1)}, u32[]{:S(2)}, u32[]{:S(2)}) collective-permute-start(bf16[384,768]{1,0:T(8,128)(2,1)S(1)} %get-tuple-element.46), channel_id=1, source_target_pairs={{0,1},{1,0},{2,3},{3,2},{4,5},{5,4},{6,7},{7,6},{8,9},{9,8},{10,11... | collective-permute-start | bytes 1769480 | tf_op jit(solution)/shard_map/ppermute | solution.py:287
  5.1 1.6 %collective-permute-start.5 = (f32[128,512]{1,0:T(8,128)S(1)}, f32[128,512]{1,0:T(8,128)S(1)}, u32[]{:S(2)}, u32[]{:S(2)}) collective-permute-start(f32[128,512]{1,0:T(8,128)S(1)} %get-tuple-element.48), channel_id=1, source_target_pairs={{0,16},{8,24},{16,0},{24,8},{1,17},{9,25},{17,1},{25,9},{2,18},{10... | collective-permute-start | bytes 786440 | tf_op jit(solution)/shard_map/ppermute | solution.py:298
  6.7 1.5 %collective-permute-start = (s32[1,384]{1,0:T(1,128)S(1)}, s32[1,384]{1,0:T(1,128)S(1)}, u32[]{:S(2)}, u32[]{:S(2)}) collective-permute-start(s32[1,384]{1,0:T(1,128)S(1)} %copy-done.5), channel_id=1, source_target_pairs={{0,1},{1,0},{2,3},{3,2},{4,5},{5,4},{6,7},{7,6},{8,9},{9,8},{10,11... | collective-permute-start | bytes 4616 | tf_op jit(solution)/shard_map/ppermute | solution.py:288
  8.2 0.6 collective-permute-start.1
  8.8 0.7 collective-permute-start.2
  9.9 1.4 %shard_map.116 = (bf16[384,512]{1,0:T(8,128)(2,1)S(1)}, bf16[384,512]{1,0:T(8,128)(2,1)S(1)}, bf16[384,512]{1,0:T(8,128)(2,1)S(1)}) custom-call(bf16[384,4096]{1,0:T(8,128)(2,1)} %bitcast.8), custom_call_target="tpu_custom_call" | custom-call | flops 1 | bytes 1 | tf_op jit(solution)/shard_map/pallas_call | solution.py:248
  11.3 7.6 %collective-permute-done.3.source.refs_0_ = bf16[384,768]{1,0:T(8,128)(2,1)S(1)} collective-permute-done((bf16[384,768]{1,0:T(8,128)(2,1)S(1)}, bf16[384,768]{1,0:T(8,128)(2,1)S(1)}, u32[]{:S(2)}, u32[]{:S(2)}) %collective-permute-start.3) | collective-permute-done | bytes 589856 | tf_op jit(solution)/shard_map/ppermute | solution.py:287
  19.0 1.8 %collective-permute-start.6 = (bf16[384,256]{1,0:T(8,128)(2,1)S(1)}, bf16[384,256]{1,0:T(8,128)(2,1)S(1)}, u32[]{:S(2)}, u32[]{:S(2)}) collective-permute-start(bf16[384,256]{1,0:T(8,128)(2,1)S(1)} %get-tuple-element.55), channel_id=1, source_target_pairs={{0,1},{1,0},{2,3},{3,2},{4,5},{5,4},{6,7},{7,6},{8,9},{9,8},{10,11... | collective-permute-start | bytes 589832 | tf_op jit(solution)/shard_map/ppermute | solution.py:316
  21.1 1.9 %collective-permute-start.7 = (f32[128,512]{1,0:T(8,128)S(1)}, f32[128,512]{1,0:T(8,128)S(1)}, u32[]{:S(2)}, u32[]{:S(2)}) collective-permute-start(f32[128,512]{1,0:T(8,128)S(1)} %get-tuple-element.89.params_base), channel_id=1, source_target_pairs={{0,16},{8,24},{16,0},{24,8},{1,17},{9,25},{17,1},{25,9},{2,18},{10... | collective-permute-start | bytes 786440 | tf_op jit(solution)/shard_map/ppermute | solution.py:306
  23.0 0.8 %shard_map.114 = (f32[64,384]{1,0:T(8,128)S(1)}, f32[64,384]{1,0:T(8,128)S(1)}, bf16[256,384]{1,0:T(8,128)(2,1)S(1)}, bf16[256,384]{1,0:T(8,128)(2,1)S(1)}) custom-call(s32[1,384]{1,0:T(1,128)S(1)} %copy-done.5, s32[1,384]{1,0:T(1,128)S(1)} %collective-permute-done.peer_doc, s32[1,384]{1,0:T(1,128)S(1)} %collective-permute-done.1.before_low, ...), custom_call_target="tpu_custom_call" | custom-call | flops 1 | bytes 1 | tf_op jit(solution)/shard_map/pallas_call | solution.py:248
  24.0 0.5 shard_map.118
  24.4 1.3 %collective-permute-start.8 = (bf16[256,512]{1,0:T(8,128)(2,1)S(1)}, bf16[256,512]{1,0:T(8,128)(2,1)S(1)}, u32[]{:S(2)}, u32[]{:S(2)}) collective-permute-start(bf16[256,512]{1,0:T(8,128)(2,1)S(1)} %shard_map.118), channel_id=1, source_target_pairs={{0,2},{2,0},{1,3},{3,1},{4,6},{6,4},{5,7},{7,5},{8,10},{10,8},{9,1... | collective-permute-start | bytes 786440 | tf_op jit(solution)/shard_map/ppermute | solution.py:351
  25.7 1.5 %collective-permute-start.12 = (bf16[384,512]{1,0:T(8,128)(2,1)S(1)}, bf16[384,512]{1,0:T(8,128)(2,1)S(1)}, u32[]{:S(2)}, u32[]{:S(2)}) collective-permute-start(bf16[384,512]{1,0:T(8,128)(2,1)S(1)} %get-tuple-element.67), channel_id=1, source_target_pairs={{0,1},{1,0},{2,3},{3,2},{4,5},{5,4},{6,7},{7,6},{8,9},{9,8},{10,11... | collective-permute-start | bytes 1179656 | tf_op jit(solution)/shard_map/ppermute | solution.py:325
  27.3 0.5 shard_map.119
  27.8 1.1 %collective-permute-start.11 = (bf16[256,512]{1,0:T(8,128)(2,1)S(1)}, bf16[256,512]{1,0:T(8,128)(2,1)S(1)}, u32[]{:S(2)}, u32[]{:S(2)}) collective-permute-start(bf16[256,512]{1,0:T(8,128)(2,1)S(1)} %shard_map.119), channel_id=1, source_target_pairs={{0,2},{2,0},{1,3},{3,1},{4,6},{6,4},{5,7},{7,5},{8,10},{10,8},{9,1... | collective-permute-start | bytes 786440 | tf_op jit(solution)/shard_map/ppermute | solution.py:351
  28.9 4.8 %collective-permute-done.8.refs_1_ = bf16[256,512]{1,0:T(8,128)(2,1)S(1)} collective-permute-done((bf16[256,512]{1,0:T(8,128)(2,1)S(1)}, bf16[256,512]{1,0:T(8,128)(2,1)S(1)}, u32[]{:S(2)}, u32[]{:S(2)}) %collective-permute-start.8) | collective-permute-done | bytes 262176 | tf_op jit(solution)/shard_map/ppermute | solution.py:351
  33.8 0.7 collective-permute-start.13
  34.4 0.7 collective-permute-done.9.refs_0_
  35.2 0.4 shard_map.121
  35.6 3.4 %collective-permute-start.14 = (bf16[256,512]{1,0:T(8,128)(2,1)S(1)}, bf16[256,512]{1,0:T(8,128)(2,1)S(1)}, u32[]{:S(2)}, u32[]{:S(2)}) collective-permute-start(bf16[256,512]{1,0:T(8,128)(2,1)S(1)} %shard_map.121), channel_id=1, source_target_pairs={{0,2},{2,0},{1,3},{3,1},{4,6},{6,4},{5,7},{7,5},{8,10},{10,8},{9,1... | collective-permute-start | bytes 786440 | tf_op jit(solution)/shard_map/ppermute | solution.py:351
  39.0 1.5 %collective-permute-start.10 = (bf16[384,512]{1,0:T(8,128)(2,1)S(1)}, bf16[384,512]{1,0:T(8,128)(2,1)S(1)}, u32[]{:S(2)}, u32[]{:S(2)}) collective-permute-start(bf16[384,512]{1,0:T(8,128)(2,1)S(1)} %get-tuple-element.62), channel_id=1, source_target_pairs={{0,1},{1,0},{2,3},{3,2},{4,5},{5,4},{6,7},{7,6},{8,9},{9,8},{10,11... | collective-permute-start | bytes 1179656 | tf_op jit(solution)/shard_map/ppermute | solution.py:325
  40.5 0.7 collective-permute-start.15
  41.2 0.4 shard_map.124
  41.6 2.0 %collective-permute-done.12.refs_1_ = bf16[384,512]{1,0:T(8,128)(2,1)S(1)} collective-permute-done((bf16[384,512]{1,0:T(8,128)(2,1)S(1)}, bf16[384,512]{1,0:T(8,128)(2,1)S(1)}, u32[]{:S(2)}, u32[]{:S(2)}) %collective-permute-start.12) | collective-permute-done | bytes 393248 | tf_op jit(solution)/shard_map/ppermute | solution.py:325
  43.6 1.9 %collective-permute-start.17 = (bf16[256,512]{1,0:T(8,128)(2,1)S(1)}, bf16[256,512]{1,0:T(8,128)(2,1)S(1)}, u32[]{:S(2)}, u32[]{:S(2)}) collective-permute-start(bf16[256,512]{1,0:T(8,128)(2,1)S(1)} %shard_map.124), channel_id=1, source_target_pairs={{0,2},{2,0},{1,3},{3,1},{4,6},{6,4},{5,7},{7,5},{8,10},{10,8},{9,1... | collective-permute-start | bytes 786440 | tf_op jit(solution)/shard_map/ppermute | solution.py:351
  45.5 0.4 shard_map.125
  46.2 0.7 collective-permute-start.21
  46.9 0.5 shard_map.127
  47.3 5.2 %collective-permute-start.16 = (bf16[256,512]{1,0:T(8,128)(2,1)S(1)}, bf16[256,512]{1,0:T(8,128)(2,1)S(1)}, u32[]{:S(2)}, u32[]{:S(2)}) collective-permute-start(bf16[256,512]{1,0:T(8,128)(2,1)S(1)} %shard_map.127), channel_id=1, source_target_pairs={{0,2},{2,0},{1,3},{3,1},{4,6},{6,4},{5,7},{7,5},{8,10},{10,8},{9,1... | collective-permute-start | bytes 786440 | tf_op jit(solution)/shard_map/ppermute | solution.py:351
  52.9 0.8 %collective-permute-start.18 = (bf16[256,512]{1,0:T(8,128)(2,1)S(1)}, bf16[256,512]{1,0:T(8,128)(2,1)S(1)}, u32[]{:S(2)}, u32[]{:S(2)}) collective-permute-start(bf16[256,512]{1,0:T(8,128)(2,1)S(1)} %shard_map.128), channel_id=1, source_target_pairs={{2,4},{4,2},{3,5},{5,3},{10,12},{12,10},{11,13},{13,11},{18,20},{2... | collective-permute-start | bytes 786440 | tf_op jit(solution)/shard_map/ppermute | solution.py:351
  54.2 3.9 %collective-permute-done.20.even = bf16[256,512]{1,0:T(8,128)(2,1)S(1)} collective-permute-done((bf16[256,512]{1,0:T(8,128)(2,1)S(1)}, bf16[256,512]{1,0:T(8,128)(2,1)S(1)}, u32[]{:S(2)}, u32[]{:S(2)}) %collective-permute-start.20) | collective-permute-done | bytes 262176 | tf_op jit(solution)/shard_map/ppermute | solution.py:351
  58.0 0.4 shard_map.131
  58.6 0.4 shard_map.122.total
  59.0 1.8 %collective-permute-done.16.even = bf16[256,512]{1,0:T(8,128)(2,1)S(1)} collective-permute-done((bf16[256,512]{1,0:T(8,128)(2,1)S(1)}, bf16[256,512]{1,0:T(8,128)(2,1)S(1)}, u32[]{:S(2)}, u32[]{:S(2)}) %collective-permute-start.16) | collective-permute-done | bytes 262176 | tf_op jit(solution)/shard_map/ppermute | solution.py:351
  60.8 0.4 shard_map.129
  61.4 1.4 %collective-permute-start.24 = (bf16[2,128,256]{2,1,0:T(8,128)(2,1)S(1)}, bf16[2,128,256]{2,1,0:T(8,128)(2,1)S(1)}, u32[]{:S(2)}, u32[]{:S(2)}) collective-permute-start(bf16[2,128,256]{2,1,0:T(8,128)(2,1)S(1)} %add_convert_fusion.both), channel_id=1, source_target_pairs={{0,16},{8,24},{16,0},{24,8},{1,17},{9,25},{17,1},{25,9},{2,18},{10... | collective-permute-start | bytes 393224 | tf_op jit(solution)/shard_map/ppermute | solution.py:376
  62.9 1.3 %collective-permute-start.23 = (bf16[2,128,256]{2,1,0:T(8,128)(2,1)S(1)}, bf16[2,128,256]{2,1,0:T(8,128)(2,1)S(1)}, u32[]{:S(2)}, u32[]{:S(2)}) collective-permute-start(bf16[2,128,256]{2,1,0:T(8,128)(2,1)S(1)} %add_convert_fusion.1.both), channel_id=1, source_target_pairs={{0,16},{8,24},{16,0},{24,8},{1,17},{9,25},{17,1},{25,9},{2,18},{10... | collective-permute-start | bytes 393224 | tf_op jit(solution)/shard_map/ppermute | solution.py:376
  64.1 1.2 %shard_map.132 = (f32[512,512]{1,0:T(8,128)}, f32[512,512]{1,0:T(8,128)}, f32[8,128]{1,0:T(8,128)S(1)}) custom-call(f32[256,512]{1,0:T(8,128)S(1)} %shard_map.130.total, bf16[256,512]{1,0:T(8,128)(2,1)S(1)} %collective-permute-done.20.even, bf16[256,512]{1,0:T(8,128)(2,1)S(1)} %collective-permute-done.21.odd, f32[512,512]{1,0:T(8,128)S(1)} %bitcast.23, ...), custom_call_target="tpu_custom_call" | custom-call | flops 1 | bytes 3145728 | tf_op jit(solution)/shard_map/pallas_call | solution.py:248
  65.4 1.2 %shard_map.133 = (f32[512,512]{1,0:T(8,128)}, f32[512,512]{1,0:T(8,128)}, f32[8,128]{1,0:T(8,128)S(1)}) custom-call(f32[256,512]{1,0:T(8,128)S(1)} %shard_map.122.total, bf16[256,512]{1,0:T(8,128)(2,1)S(1)} %collective-permute-done.16.even, bf16[256,512]{1,0:T(8,128)(2,1)S(1)} %collective-permute-done.18.odd, ...), custom_call_target="tpu_custom_call", output_to_operand_aliasing={{0}: (5, {}), {1}: (6, {})} | custom-call | flops 1 | bytes 3145728 | tf_op jit(solution)/shard_map/pallas_call | solution.py:248
  66.6 1.2 %collective-permute-done.24.came = bf16[2,128,256]{2,1,0:T(8,128)(2,1)S(1)} collective-permute-done((bf16[2,128,256]{2,1,0:T(8,128)(2,1)S(1)}, bf16[2,128,256]{2,1,0:T(8,128)(2,1)S(1)}, u32[]{:S(2)}, u32[]{:S(2)}) %collective-permute-start.24) | collective-permute-done | bytes 131104 | tf_op jit(solution)/shard_map/ppermute | solution.py:376
  67.8 0.7 shard_map.134
  68.5 1.7 %collective-permute-done.23.came = bf16[2,128,256]{2,1,0:T(8,128)(2,1)S(1)} collective-permute-done((bf16[2,128,256]{2,1,0:T(8,128)(2,1)S(1)}, bf16[2,128,256]{2,1,0:T(8,128)(2,1)S(1)}, u32[]{:S(2)}, u32[]{:S(2)}) %collective-permute-start.23) | collective-permute-done | bytes 131104 | tf_op jit(solution)/shard_map/ppermute | solution.py:376
  70.2 0.7 shard_map.135
  70.9 0.8 %shard_map.136.refs_0_ = f32[512,512]{1,0:T(8,128)} custom-call(f32[2,128,256]{2,1,0:T(8,128)S(1)} %get-tuple-element.87.mine, f32[2,128,256]{2,1,0:T(8,128)S(1)} %collective-permute-done.26.theirs), custom_call_target="tpu_custom_call" | custom-call | flops 1 | bytes 1 | tf_op jit(solution)/shard_map/pallas_call | solution.py:248
  71.7 0.7 collective-permute-done.25.theirs
  72.4 0.8 %shard_map.137 = f32[512,512]{1,0:T(8,128)} custom-call(f32[2,128,256]{2,1,0:T(8,128)S(1)} %get-tuple-element.86.mine, f32[2,128,256]{2,1,0:T(8,128)S(1)} %collective-permute-done.25.theirs, f32[512,512]{1,0:T(8,128)} %shard_map.136.refs_0_), custom_call_target="tpu_custom_call", output_to_operand_aliasing={{}: (2, {})} | custom-call | flops 1 | bytes 1 | tf_op jit(solution)/shard_map/pallas_call | solution.py:248
  (52 shorter events, 2.4 us)
Async XLA Ops:
  0.6 4.4 %copy-start.4 = (f32[1,512,512]{2,1,0:T(8,128)S(1)}, f32[1,512,512]{2,1,0:T(8,128)}, u32[]{:S(2)}) copy-start(f32[1,512,512]{2,1,0:T(8,128)} %param.11) | copy-start | bytes 3145732
  0.6 6.0 %copy-start.5 = (s32[1,384]{1,0:T(1,128)S(1)}, s32[1,384]{1,0:T(1,128)}, u32[]{:S(2)}) copy-start(s32[1,384]{1,0:T(1,128)} %own_doc.1) | copy-start | bytes 4612
  0.7 4.4 %collective-permute-start.4 = (f32[512,512]{1,0:T(8,128)}, f32[512,512]{1,0:T(8,128)S(1)}, u32[]{:S(2)}, u32[]{:S(2)}) collective-permute-start(f32[512,512]{1,0:T(8,128)} %bitcast.31), channel_id=1, source_target_pairs={{0,8},{8,0},{16,24},{24,16},{1,9},{9,1},{17,25},{25,17},{2,10},{10... | collective-permute-start | bytes 3145736 | tf_op jit(solution)/shard_map/ppermute | solution.py:295
  2.3 18.6 %copy-start.6 = (f32[128,512]{1,0:T(8,128)S(1)}, f32[128,512]{1,0:T(8,128)}, u32[]{:S(2)}) copy-start(f32[128,512]{1,0:T(8,128)} %param.15) | copy-start | bytes 786436
  2.4 18.6 %copy-start.7 = (f32[128,512]{1,0:T(8,128)S(1)}, f32[128,512]{1,0:T(8,128)}, u32[]{:S(2)}) copy-start(f32[128,512]{1,0:T(8,128)} %param.14) | copy-start | bytes 786436
  2.4 20.6 %copy-start.3 = (bf16[1,384,512]{2,1,0:T(8,128)(2,1)S(1)}, bf16[1,384,512]{2,1,0:T(8,128)(2,1)}, u32[]{:S(2)}) copy-start(bf16[1,384,512]{2,1,0:T(8,128)(2,1)} %param.9) | copy-start | bytes 1179652
  2.4 16.6 %collective-permute-start.3 = (bf16[384,768]{1,0:T(8,128)(2,1)S(1)}, bf16[384,768]{1,0:T(8,128)(2,1)S(1)}, u32[]{:S(2)}, u32[]{:S(2)}) collective-permute-start(bf16[384,768]{1,0:T(8,128)(2,1)S(1)} %get-tuple-element.46), channel_id=1, source_target_pairs={{0,1},{1,0},{2,3},{3,2},{4,5},{5,4},{6,7},{7,6},{8,9},{9,8},{10,11... | collective-permute-start | bytes 1769480 | tf_op jit(solution)/shard_map/ppermute | solution.py:287
  5.1 15.6 %collective-permute-start.5 = (f32[128,512]{1,0:T(8,128)S(1)}, f32[128,512]{1,0:T(8,128)S(1)}, u32[]{:S(2)}, u32[]{:S(2)}) collective-permute-start(f32[128,512]{1,0:T(8,128)S(1)} %get-tuple-element.48), channel_id=1, source_target_pairs={{0,16},{8,24},{16,0},{24,8},{1,17},{9,25},{17,1},{25,9},{2,18},{10... | collective-permute-start | bytes 786440 | tf_op jit(solution)/shard_map/ppermute | solution.py:298
  6.7 14.4 %collective-permute-start = (s32[1,384]{1,0:T(1,128)S(1)}, s32[1,384]{1,0:T(1,128)S(1)}, u32[]{:S(2)}, u32[]{:S(2)}) collective-permute-start(s32[1,384]{1,0:T(1,128)S(1)} %copy-done.5), channel_id=1, source_target_pairs={{0,1},{1,0},{2,3},{3,2},{4,5},{5,4},{6,7},{7,6},{8,9},{9,8},{10,11... | collective-permute-start | bytes 4616 | tf_op jit(solution)/shard_map/ppermute | solution.py:288
  8.2 14.8 %collective-permute-start.1 = (s32[1,384]{1,0:T(1,128)S(1)}, s32[1,384]{1,0:T(1,128)S(1)}, u32[]{:S(2)}, u32[]{:S(2)}) collective-permute-start(s32[1,384]{1,0:T(1,128)S(1)} %copy-done.5), channel_id=1, source_target_pairs={{1,2},{3,4},{5,6},{9,10},{11,12},{13,14},{17,18},{19,20},{21,22},{... | collective-permute-start | bytes 4616 | tf_op jit(solution)/shard_map/ppermute | solution.py:289
  8.8 14.1 %collective-permute-start.2 = (s32[1,384]{1,0:T(1,128)S(1)}, s32[1,384]{1,0:T(1,128)S(1)}, u32[]{:S(2)}, u32[]{:S(2)}) collective-permute-start(s32[1,384]{1,0:T(1,128)S(1)} %copy-done.5), channel_id=1, source_target_pairs={{1,3},{3,5},{5,7},{9,11},{11,13},{13,15},{17,19},{19,21},{21,23},{... | collective-permute-start | bytes 4616 | tf_op jit(solution)/shard_map/ppermute | solution.py:290
  9.9 14.1 %copy-start = (bf16[1,384,4096]{2,1,0:T(8,128)(2,1)S(1)}, bf16[1,384,4096]{2,1,0:T(8,128)(2,1)}, u32[]{:S(2)}) copy-start(bf16[1,384,4096]{2,1,0:T(8,128)(2,1)} %param.8) | copy-start | bytes 9437188
  19.0 8.2 %collective-permute-start.6 = (bf16[384,256]{1,0:T(8,128)(2,1)S(1)}, bf16[384,256]{1,0:T(8,128)(2,1)S(1)}, u32[]{:S(2)}, u32[]{:S(2)}) collective-permute-start(bf16[384,256]{1,0:T(8,128)(2,1)S(1)} %get-tuple-element.55), channel_id=1, source_target_pairs={{0,1},{1,0},{2,3},{3,2},{4,5},{5,4},{6,7},{7,6},{8,9},{9,8},{10,11... | collective-permute-start | bytes 589832 | tf_op jit(solution)/shard_map/ppermute | solution.py:316
  20.7 14.5 %collective-permute-start.9 = (bf16[384,512]{1,0:T(8,128)(2,1)S(1)}, bf16[384,512]{1,0:T(8,128)(2,1)S(1)}, u32[]{:S(2)}, u32[]{:S(2)}) collective-permute-start(bf16[384,512]{1,0:T(8,128)(2,1)S(1)} %get-tuple-element.61), channel_id=1, source_target_pairs={{0,1},{1,0},{2,3},{3,2},{4,5},{5,4},{6,7},{7,6},{8,9},{9,8},{10,11... | collective-permute-start | bytes 1179656 | tf_op jit(solution)/shard_map/ppermute | solution.py:325
  21.1 7.8 %collective-permute-start.7 = (f32[128,512]{1,0:T(8,128)S(1)}, f32[128,512]{1,0:T(8,128)S(1)}, u32[]{:S(2)}, u32[]{:S(2)}) collective-permute-start(f32[128,512]{1,0:T(8,128)S(1)} %get-tuple-element.89.params_base), channel_id=1, source_target_pairs={{0,16},{8,24},{16,0},{24,8},{1,17},{9,25},{17,1},{25,9},{2,18},{10... | collective-permute-start | bytes 786440 | tf_op jit(solution)/shard_map/ppermute | solution.py:306
  24.4 9.3 %collective-permute-start.8 = (bf16[256,512]{1,0:T(8,128)(2,1)S(1)}, bf16[256,512]{1,0:T(8,128)(2,1)S(1)}, u32[]{:S(2)}, u32[]{:S(2)}) collective-permute-start(bf16[256,512]{1,0:T(8,128)(2,1)S(1)} %shard_map.118), channel_id=1, source_target_pairs={{0,2},{2,0},{1,3},{3,1},{4,6},{6,4},{5,7},{7,5},{8,10},{10,8},{9,1... | collective-permute-start | bytes 786440 | tf_op jit(solution)/shard_map/ppermute | solution.py:351
  25.7 17.9 %collective-permute-start.12 = (bf16[384,512]{1,0:T(8,128)(2,1)S(1)}, bf16[384,512]{1,0:T(8,128)(2,1)S(1)}, u32[]{:S(2)}, u32[]{:S(2)}) collective-permute-start(bf16[384,512]{1,0:T(8,128)(2,1)S(1)} %get-tuple-element.67), channel_id=1, source_target_pairs={{0,1},{1,0},{2,3},{3,2},{4,5},{5,4},{6,7},{7,6},{8,9},{9,8},{10,11... | collective-permute-start | bytes 1179656 | tf_op jit(solution)/shard_map/ppermute | solution.py:325
  27.8 12.7 %collective-permute-start.11 = (bf16[256,512]{1,0:T(8,128)(2,1)S(1)}, bf16[256,512]{1,0:T(8,128)(2,1)S(1)}, u32[]{:S(2)}, u32[]{:S(2)}) collective-permute-start(bf16[256,512]{1,0:T(8,128)(2,1)S(1)} %shard_map.119), channel_id=1, source_target_pairs={{0,2},{2,0},{1,3},{3,1},{4,6},{6,4},{5,7},{7,5},{8,10},{10,8},{9,1... | collective-permute-start | bytes 786440 | tf_op jit(solution)/shard_map/ppermute | solution.py:351
  33.8 11.7 %collective-permute-start.13 = (bf16[256,512]{1,0:T(8,128)(2,1)S(1)}, bf16[256,512]{1,0:T(8,128)(2,1)S(1)}, u32[]{:S(2)}, u32[]{:S(2)}) collective-permute-start(bf16[256,512]{1,0:T(8,128)(2,1)S(1)} %shard_map.120), channel_id=1, source_target_pairs={{2,4},{4,2},{3,5},{5,3},{10,12},{12,10},{11,13},{13,11},{18,20},{2... | collective-permute-start | bytes 786440 | tf_op jit(solution)/shard_map/ppermute | solution.py:351
  35.6 10.5 %collective-permute-start.14 = (bf16[256,512]{1,0:T(8,128)(2,1)S(1)}, bf16[256,512]{1,0:T(8,128)(2,1)S(1)}, u32[]{:S(2)}, u32[]{:S(2)}) collective-permute-start(bf16[256,512]{1,0:T(8,128)(2,1)S(1)} %shard_map.121), channel_id=1, source_target_pairs={{0,2},{2,0},{1,3},{3,1},{4,6},{6,4},{5,7},{7,5},{8,10},{10,8},{9,1... | collective-permute-start | bytes 786440 | tf_op jit(solution)/shard_map/ppermute | solution.py:351
  39.0 14.7 %collective-permute-start.10 = (bf16[384,512]{1,0:T(8,128)(2,1)S(1)}, bf16[384,512]{1,0:T(8,128)(2,1)S(1)}, u32[]{:S(2)}, u32[]{:S(2)}) collective-permute-start(bf16[384,512]{1,0:T(8,128)(2,1)S(1)} %get-tuple-element.62), channel_id=1, source_target_pairs={{0,1},{1,0},{2,3},{3,2},{4,5},{5,4},{6,7},{7,6},{8,9},{9,8},{10,11... | collective-permute-start | bytes 1179656 | tf_op jit(solution)/shard_map/ppermute | solution.py:325
  40.5 6.4 %collective-permute-start.15 = (bf16[256,512]{1,0:T(8,128)(2,1)S(1)}, bf16[256,512]{1,0:T(8,128)(2,1)S(1)}, u32[]{:S(2)}, u32[]{:S(2)}) collective-permute-start(bf16[256,512]{1,0:T(8,128)(2,1)S(1)} %shard_map.123), channel_id=1, source_target_pairs={{2,4},{4,2},{3,5},{5,3},{10,12},{12,10},{11,13},{13,11},{18,20},{2... | collective-permute-start | bytes 786440 | tf_op jit(solution)/shard_map/ppermute | solution.py:351
  43.6 9.2 %collective-permute-start.17 = (bf16[256,512]{1,0:T(8,128)(2,1)S(1)}, bf16[256,512]{1,0:T(8,128)(2,1)S(1)}, u32[]{:S(2)}, u32[]{:S(2)}) collective-permute-start(bf16[256,512]{1,0:T(8,128)(2,1)S(1)} %shard_map.124), channel_id=1, source_target_pairs={{0,2},{2,0},{1,3},{3,1},{4,6},{6,4},{5,7},{7,5},{8,10},{10,8},{9,1... | collective-permute-start | bytes 786440 | tf_op jit(solution)/shard_map/ppermute | solution.py:351
  45.9 12.1 %collective-permute-start.20 = (bf16[256,512]{1,0:T(8,128)(2,1)S(1)}, bf16[256,512]{1,0:T(8,128)(2,1)S(1)}, u32[]{:S(2)}, u32[]{:S(2)}) collective-permute-start(bf16[256,512]{1,0:T(8,128)(2,1)S(1)} %shard_map.125), channel_id=1, source_target_pairs={{0,2},{2,0},{1,3},{3,1},{4,6},{6,4},{5,7},{7,5},{8,10},{10,8},{9,1... | collective-permute-start | bytes 786440 | tf_op jit(solution)/shard_map/ppermute | solution.py:351
  46.2 11.9 %collective-permute-start.21 = (bf16[256,512]{1,0:T(8,128)(2,1)S(1)}, bf16[256,512]{1,0:T(8,128)(2,1)S(1)}, u32[]{:S(2)}, u32[]{:S(2)}) collective-permute-start(bf16[256,512]{1,0:T(8,128)(2,1)S(1)} %shard_map.126), channel_id=1, source_target_pairs={{2,4},{4,2},{3,5},{5,3},{10,12},{12,10},{11,13},{13,11},{18,20},{2... | collective-permute-start | bytes 786440 | tf_op jit(solution)/shard_map/ppermute | solution.py:351
  47.3 13.5 %collective-permute-start.16 = (bf16[256,512]{1,0:T(8,128)(2,1)S(1)}, bf16[256,512]{1,0:T(8,128)(2,1)S(1)}, u32[]{:S(2)}, u32[]{:S(2)}) collective-permute-start(bf16[256,512]{1,0:T(8,128)(2,1)S(1)} %shard_map.127), channel_id=1, source_target_pairs={{0,2},{2,0},{1,3},{3,1},{4,6},{6,4},{5,7},{7,5},{8,10},{10,8},{9,1... | collective-permute-start | bytes 786440 | tf_op jit(solution)/shard_map/ppermute | solution.py:351
  52.9 5.2 %copy-start.1 = (f32[1,512,512]{2,1,0:T(8,128)S(1)}, f32[1,512,512]{2,1,0:T(8,128)}, u32[]{:S(2)}) copy-start(f32[1,512,512]{2,1,0:T(8,128)} %param.12) | copy-start | bytes 3145732
  52.9 5.1 %copy-start.2 = (f32[1,512,512]{2,1,0:T(8,128)S(1)}, f32[1,512,512]{2,1,0:T(8,128)}, u32[]{:S(2)}) copy-start(f32[1,512,512]{2,1,0:T(8,128)} %param.13) | copy-start | bytes 3145732
  52.9 7.9 %collective-permute-start.18 = (bf16[256,512]{1,0:T(8,128)(2,1)S(1)}, bf16[256,512]{1,0:T(8,128)(2,1)S(1)}, u32[]{:S(2)}, u32[]{:S(2)}) collective-permute-start(bf16[256,512]{1,0:T(8,128)(2,1)S(1)} %shard_map.128), channel_id=1, source_target_pairs={{2,4},{4,2},{3,5},{5,3},{10,12},{12,10},{11,13},{13,11},{18,20},{2... | collective-permute-start | bytes 786440 | tf_op jit(solution)/shard_map/ppermute | solution.py:351
  58.5 2.9 %collective-permute-start.22 = (bf16[2,128,256]{2,1,0:T(8,128)(2,1)S(1)}, bf16[2,128,256]{2,1,0:T(8,128)(2,1)S(1)}, u32[]{:S(2)}, u32[]{:S(2)}) collective-permute-start(bf16[2,128,256]{2,1,0:T(8,128)(2,1)S(1)} %get-tuple-element.76), channel_id=1, source_target_pairs={{0,8},{8,0},{16,24},{24,16},{1,9},{9,1},{17,25},{25,17},{2,10},{10... | collective-permute-start | bytes 393224 | tf_op jit(solution)/shard_map/ppermute | solution.py:366
  61.3 1.6 %collective-permute-start.19 = (bf16[2,128,256]{2,1,0:T(8,128)(2,1)S(1)}, bf16[2,128,256]{2,1,0:T(8,128)(2,1)S(1)}, u32[]{:S(2)}, u32[]{:S(2)}) collective-permute-start(bf16[2,128,256]{2,1,0:T(8,128)(2,1)S(1)} %get-tuple-element.72), channel_id=1, source_target_pairs={{0,8},{8,0},{16,24},{24,16},{1,9},{9,1},{17,25},{25,17},{2,10},{10... | collective-permute-start | bytes 393224 | tf_op jit(solution)/shard_map/ppermute | solution.py:366
  61.4 6.4 %collective-permute-start.24 = (bf16[2,128,256]{2,1,0:T(8,128)(2,1)S(1)}, bf16[2,128,256]{2,1,0:T(8,128)(2,1)S(1)}, u32[]{:S(2)}, u32[]{:S(2)}) collective-permute-start(bf16[2,128,256]{2,1,0:T(8,128)(2,1)S(1)} %add_convert_fusion.both), channel_id=1, source_target_pairs={{0,16},{8,24},{16,0},{24,8},{1,17},{9,25},{17,1},{25,9},{2,18},{10... | collective-permute-start | bytes 393224 | tf_op jit(solution)/shard_map/ppermute | solution.py:376
  62.9 7.3 %collective-permute-start.23 = (bf16[2,128,256]{2,1,0:T(8,128)(2,1)S(1)}, bf16[2,128,256]{2,1,0:T(8,128)(2,1)S(1)}, u32[]{:S(2)}, u32[]{:S(2)}) collective-permute-start(bf16[2,128,256]{2,1,0:T(8,128)(2,1)S(1)} %add_convert_fusion.1.both), channel_id=1, source_target_pairs={{0,16},{8,24},{16,0},{24,8},{1,17},{9,25},{17,1},{25,9},{2,18},{10... | collective-permute-start | bytes 393224 | tf_op jit(solution)/shard_map/ppermute | solution.py:376
  68.5 2.4 %collective-permute-start.26 = (f32[2,128,256]{2,1,0:T(8,128)S(1)}, f32[2,128,256]{2,1,0:T(8,128)S(1)}, u32[]{:S(2)}, u32[]{:S(2)}) collective-permute-start(f32[2,128,256]{2,1,0:T(8,128)S(1)} %get-tuple-element.87.mine), channel_id=1, source_target_pairs={{0,8},{8,0},{16,24},{24,16},{1,9},{9,1},{17,25},{25,17},{2,10},{10... | collective-permute-start | bytes 786440 | tf_op jit(solution)/shard_map/ppermute | solution.py:390
  70.9 1.5 %collective-permute-start.25 = (f32[2,128,256]{2,1,0:T(8,128)S(1)}, f32[2,128,256]{2,1,0:T(8,128)S(1)}, u32[]{:S(2)}, u32[]{:S(2)}) collective-permute-start(f32[2,128,256]{2,1,0:T(8,128)S(1)} %get-tuple-element.86.mine), channel_id=1, source_target_pairs={{0,8},{8,0},{16,24},{24,16},{1,9},{9,1},{17,25},{25,17},{2,10},{10... | collective-permute-start | bytes 786440 | tf_op jit(solution)/shard_map/ppermute | solution.py:390
